TPU v7x, 32 devices: a whole 2x2x4 slice. The times are simulated.
32 devices in a mesh: basin: 16 (over z, y, core), unit: 2 (over x).
Axes of the slice: x: 2, y: 2, z: 4, core: 2. Of those that a mesh axis runs over, the one named last changes fastest.
Arguments:
- forcing: bfloat16 [12, 32, 32768], P(None, None, ('basin', 'unit')), may hold values from -6 to 6
- hidden_init: bfloat16 [128, 32768], P(None, ('basin', 'unit')), may hold values from -0.8984375 to 0.8984375
- cell_init: float32 [128, 32768], P(None, ('basin', 'unit')), may hold values from -6 to 6
- w_input: bfloat16 [512, 32], replicated, may hold values from -1 to 1
- w_recur: bfloat16 [512, 128], replicated, may hold values from -0.5 to 0.5
- gate_bias: float32 [512], replicated, may hold values from -4 to 4
- w_head: float32 [128], replicated, may hold values from -0.5 to 0.5
- remap_dest: int32 [256, 8], P(('basin', 'unit')), may hold values from 0 to 15, all different within a row; in each aligned block of 8 rows (0 to 7, 8 to 15, ...) at most 8 rows name the same one
- remap_block: int32 [256, 8], P(('basin', 'unit')), may hold values from 0 to 7
- remap_weight: bfloat16 [256, 8, 128, 128], P(('basin', 'unit')), may hold values from -0.5 to 0.5
- route_kernel: float32 [256, 128, 128], P(('basin', 'unit'))
- carry_gain: float32 [256, 128], P(('basin', 'unit')), may hold values from 0.85 to 1
- block_count: int32 [16], replicated, may hold values from 1 to 16, as said below
- parent_section: int32 [16], replicated, may hold values from 1 to 16, as said below
- reservoir: int32 [16], replicated, may hold values 0 or 1
- release: float32 [12, 16], replicated, may hold values from 0.5 to 3
Outputs:
- discharge: float32 [12, 32768], P(None, ('basin', 'unit'))
Inputs may be any that keep to these rules, and one draw needn't show every extreme that they name: `remap_dest`: in the rows of one device (aligned blocks of 8 rows) no value appears more than 8 times, and in some such block one value appears exactly 8 times; the 8 values of a row differ. `block_count`: the last section uses all 16 blocks. parent_section[s] > s for every section; the last section's value is 16 (the outlet), every other value is below 16. A section s below 8 flows into s + 8 or the section after it; every other section flows into one of the next two.
All inputs are finite; a program needn't handle non-finite values.
Results may differ from a plain program's by a relative error of at most 0.017.
Values may be sent and summed in bfloat16 or wider, within the bound.
No kernel may reach another device: no remote copies, remote signals or barrier semaphores. Data moves between devices by JAX's collectives and lax.ppermute only.
A program may use at most 64 MiB of HBM per device.

v0:
```python
import jax
import jax.numpy as jnp
from jax import lax
from jax.sharding import PartitionSpec as P

PRECISE = lax.Precision.HIGHEST


def prefix(x, axis, combine, identity):
    size, position = (lax.axis_size(axis), lax.axis_index(axis))
    everything = jax.tree.map(lambda part: lax.all_gather(part, axis), x)
    start = jax.tree.map(
        lambda part, zero: jnp.broadcast_to(jnp.asarray(zero, part.dtype), part.shape), x, identity
    )

    def hop(k, before):
        reached = k < position
        new = combine(before, jax.tree.map(lambda part: part[k], everything))
        return jax.tree.map(lambda a, b: jnp.where(reached, a, b), new, before)

    return lax.fori_loop(0, size, hop, start)


def compose(earlier, later):
    return (later[0] + later[1] * earlier[0], earlier[1] * later[1])


def lstm_steps(packed, first_step, step_count, forcing, w_input, w_recur, gate_bias, w_head):
    state_width = w_recur.shape[1]

    def lstm_step(step_idx, loop_state):
        hidden, cell_state, runoff_buf = loop_state
        frame_now = lax.dynamic_index_in_dim(forcing, step_idx, 0, keepdims=False)
        gate_sum = jnp.dot(w_input, frame_now, preferred_element_type=jnp.float32)
        gate_sum = (
            gate_sum
            + jnp.dot(w_recur, hidden, preferred_element_type=jnp.float32)
            + gate_bias[:, None]
        )
        in_gate = jax.nn.sigmoid(gate_sum[0:state_width])
        forget = jax.nn.sigmoid(gate_sum[state_width : 2 * state_width])
        cand_gate = jnp.tanh(gate_sum[2 * state_width : 3 * state_width])
        out_gate = jax.nn.sigmoid(gate_sum[3 * state_width :])
        cell_state = forget * cell_state + in_gate * cand_gate
        hidden = (out_gate * jnp.tanh(cell_state)).astype(jnp.bfloat16)
        runoff = jax.nn.softplus(
            jnp.sum(w_head[:, None] * hidden.astype(jnp.float32), axis=0)
        ).astype(jnp.bfloat16)
        runoff_buf = lax.dynamic_update_slice_in_dim(runoff_buf, runoff[None], step_idx, 0)
        return (hidden, cell_state, runoff_buf)

    return lax.fori_loop(first_step, first_step + step_count, lstm_step, packed)


def dispatch_plan(remap_dest, remap_block, peers, capacity):
    dest_flat = remap_dest.reshape(-1)
    block_flat = remap_block.reshape(-1)
    one_hot = (dest_flat[:, None] == jnp.arange(peers, dtype=jnp.int32)[None, :]).astype(jnp.int32)
    before_count = jnp.cumsum(one_hot, axis=0) - one_hot
    rank_in = jnp.sum(before_count * one_hot, axis=1)
    slot_of = dest_flat * capacity + rank_in
    match = jnp.arange(peers * capacity, dtype=jnp.int32)[:, None] == slot_of[None, :]
    placer = match.astype(jnp.bfloat16)
    slot_block = jnp.sum(jnp.where(match, block_flat[None, :] + 1, 0), axis=1) - 1
    return (placer, slot_block.reshape(peers, capacity))


def pack_items(runoff_part, remap_weight, placer, peers, capacity):
    part_steps = runoff_part.shape[0]
    unit_blocks = remap_weight.shape[0]
    fan_out = remap_weight.shape[1]
    block_size = remap_weight.shape[2]
    blocks = runoff_part.reshape(part_steps, unit_blocks, block_size)
    contrib = jnp.einsum("sub,ukbr->uksr", blocks, remap_weight, preferred_element_type=jnp.float32)
    item_rows = contrib.astype(jnp.bfloat16).reshape(unit_blocks * fan_out, part_steps * block_size)
    outgoing = jnp.dot(placer, item_rows, preferred_element_type=jnp.float32).astype(jnp.bfloat16)
    return outgoing.reshape(peers, capacity, part_steps * block_size)


def spread_items(received, got_block, reach_blocks):
    row_width = received.shape[2]
    picker = (
        jnp.arange(reach_blocks, dtype=jnp.int32)[:, None] == got_block.reshape(1, -1)
    ).astype(jnp.bfloat16)
    return jnp.dot(picker, received.reshape(-1, row_width), preferred_element_type=jnp.float32)


def shards(
    forcing,
    hidden_init,
    cell_init,
    w_input,
    w_recur,
    gate_bias,
    w_head,
    remap_dest,
    remap_block,
    remap_weight,
    route_kernel,
    carry_gain,
    block_count,
    parent_section,
    reservoir,
    release,
):
    total_steps = forcing.shape[0]
    unit_count = forcing.shape[2]
    unit_blocks = remap_weight.shape[0]
    fan_out = remap_weight.shape[1]
    block_size = remap_weight.shape[2]
    reach_blocks = route_kernel.shape[0]
    basin_size = lax.axis_size("basin")
    unit_size = lax.axis_size("unit")
    basin_here = lax.axis_index("basin")
    unit_here = lax.axis_index("unit")
    capacity = min(unit_blocks, max(2, 2 * unit_blocks * fan_out // basin_size))
    placer, slot_block = dispatch_plan(remap_dest, remap_block, basin_size, capacity)
    packed = (hidden_init, cell_init, jnp.zeros((total_steps, unit_count), jnp.bfloat16))
    packed = lstm_steps(packed, 0, total_steps, forcing, w_input, w_recur, gate_bias, w_head)
    outgoing = pack_items(packed[2], remap_weight, placer, basin_size, capacity)
    received, got_block = (
        lax.all_to_all(outgoing, "basin", split_axis=0, concat_axis=0, tiled=True),
        lax.all_to_all(slot_block, "basin", split_axis=0, concat_axis=0, tiled=True),
    )
    lateral = spread_items(received, got_block, reach_blocks).reshape(
        reach_blocks, total_steps, block_size
    )
    kernel_out = jnp.einsum("jsb,jib->jsi", lateral, route_kernel, precision=PRECISE)
    block_order = unit_here * reach_blocks + jnp.arange(reach_blocks, dtype=jnp.int32)
    live_blocks = block_order < block_count[basin_here]

    def chain_step(chain_state, inputs):
        carry_now, factor_now = chain_state
        kernel_blk, gain_row, live_one = inputs
        base_blk = kernel_blk + carry_now[:, None] * gain_row[None, :]
        resp_blk = factor_now * gain_row
        carry_next = jnp.where(live_one, base_blk[:, -1], carry_now)
        factor_next = jnp.where(live_one, factor_now * gain_row[-1], factor_now)
        base_blk = jnp.where(live_one, base_blk, 0.0)
        resp_blk = jnp.where(live_one, resp_blk, 0.0)
        return ((carry_next, factor_next), (base_blk, resp_blk))

    chain_init = (jnp.zeros((total_steps,), jnp.float32), jnp.ones((1,), jnp.float32))
    own_map, chain_out = lax.scan(chain_step, chain_init, (kernel_out, carry_gain, live_blocks))
    base_all, resp_all = chain_out
    identity = (jnp.zeros((total_steps,), jnp.float32), jnp.ones((1,), jnp.float32))
    before = prefix(own_map, "unit", compose, identity)
    section_total = compose(before, own_map)
    all_shift, all_factor = (
        lax.all_gather(section_total[0][None], ("basin", "unit"), axis=0, tiled=True),
        lax.all_gather(section_total[1][None], ("basin", "unit"), axis=0, tiled=True),
    )
    sec_shift = all_shift.reshape(basin_size, unit_size, total_steps)[:, unit_size - 1]
    sec_factor = all_factor.reshape(basin_size, unit_size)[:, unit_size - 1]

    def tree_step(section, inflow_acc):
        outflow = sec_shift[section] + sec_factor[section] * inflow_acc[section]
        release_col = lax.dynamic_index_in_dim(release, section, 1, keepdims=False)
        passed = jnp.where(reservoir[section] == 1, release_col, outflow)
        return inflow_acc.at[parent_section[section]].add(passed)

    inflow_acc = lax.fori_loop(
        0, basin_size, tree_step, jnp.zeros((basin_size + 1, total_steps), jnp.float32)
    )
    head_inflow = inflow_acc[basin_here]
    device_inflow = before[0] + before[1] * head_inflow
    discharge = base_all + resp_all[:, None, :] * device_inflow[None, :, None]
    return discharge.transpose(1, 0, 2).reshape(total_steps, reach_blocks * block_size)


def solution(mesh):
    placed = (
        P(None, None, ("basin", "unit")),
        P(None, ("basin", "unit")),
        P(None, ("basin", "unit")),
        P(),
        P(),
        P(),
        P(),
        P(("basin", "unit"), None),
        P(("basin", "unit"), None),
        P(("basin", "unit"), None, None, None),
        P(("basin", "unit"), None, None),
        P(("basin", "unit"), None),
        P(),
        P(),
        P(),
        P(),
    )
    return jax.shard_map(
        shards, mesh=mesh, in_specs=placed, out_specs=P(None, ("basin", "unit")), check_vma=False
    )
```

profile of v0, /device:TPU:0, one launch (start us, length us, event | category | flops | bytes accessed | tf_op | source)
XLA Modules:
  0.0 292.0 jit_solution(5777158603309257258)
XLA Ops:
  4.9 7.4 %all-to-all-start = ((s32[16,1,8]{2,1,0:T(1,128)}), s32[16,1,8]{2,1,0:T(1,128)S(1)}, u32[]{:S(2)}, u32[]{:S(2)}) async-start(s32[16,1,8]{2,1,0:T(1,128)} %bitcast.9), calls=%async_computation | async-start | bytes 16384 | tf_op jit(solution)/shard_map/all_to_all | solution.py:123
  12.3 41.4 %while.64 = (s32[]{:T(128)}, bf16[128,1024]{1,0:T(8,128)(2,1)S(1)}, f32[128,1024]{1,0:T(8,128)S(1)}, bf16[12,1024]{1,0:T(8,128)(2,1)S(1)}, bf16[12,32,1024]{2,1,...) while((s32[]{:T(128)}, bf16[128,1024]{1,0:T(8,128)(2,1)S(1)}, ...), condition=%wide.region_5.6_spmd, body=%wide.region_3.5_spmd.sunk | while | flops 171055104 | bytes 10349765 | solution.py:52
  55.2 6.0 %all-to-all-start.1 = ((bf16[16,8,1536]{2,1,0:T(8,128)(2,1)}), bf16[16,8,1536]{2,1,0:T(8,128)(2,1)S(1)}, u32[]{:S(2)}, u32[]{:S(2)}) async-start(bf16[16,8,1536]{2,1,0:T(8,128)(2,1)} %fusion.23), calls=%async_computation.1 | async-start | bytes 786432 | tf_op jit(solution)/shard_map/all_to_all | solution.py:122
  65.5 7.9 %all-to-all-done.1 = bf16[16,8,1536]{2,1,0:T(8,128)(2,1)S(1)} async-done(((bf16[16,8,1536]{2,1,0:T(8,128)(2,1)}), bf16[16,8,1536]{2,1,0:T(8,128)(2,1)S(1)}, u32[]{:S(2)}, u32[]{:S(2)}) %all-to-all-start.1) | async-done | bytes 393248 | tf_op jit(solution)/shard_map/all_to_all | solution.py:122
  74.5 57.5 %while.66 = (s32[]{:T(128)}, f32[12]{0:T(128)S(1)}, f32[1]{0:T(128)}, f32[8,12,128]{1,2,0:T(8,128)}, f32[8,128]{1,0:T(8,128)S(1)}, /*index=5*/pred[8]{0:T(512)(1...) while((s32[]{:T(128)}, f32[12]{0:T(128)S(1)}, f32[1]{0:T(128)}, ...), condition=%wide.region_7.8_spmd.clone, body=%wide.region_6.7_spmd.clone.sunk | while | flops 4917 | bytes 83824 | solution.py:144
  75.2 1.4 broadcast_select_fusion.14
  76.5 1.4 select_dynamic-update-slice_fusion.2
  82.3 1.4 broadcast_select_fusion.14
  83.7 1.4 select_dynamic-update-slice_fusion.2
  89.5 1.4 broadcast_select_fusion.14
  90.9 1.4 select_dynamic-update-slice_fusion.2
  96.7 1.4 broadcast_select_fusion.14
  98.1 1.4 select_dynamic-update-slice_fusion.2
  103.9 1.4 broadcast_select_fusion.14
  105.3 1.4 select_dynamic-update-slice_fusion.2
  111.1 1.4 broadcast_select_fusion.14
  112.5 1.4 select_dynamic-update-slice_fusion.2
  118.3 1.4 broadcast_select_fusion.14
  119.7 1.4 select_dynamic-update-slice_fusion.2
  125.5 1.4 broadcast_select_fusion.14
  126.8 1.4 select_dynamic-update-slice_fusion.2
  133.0 4.9 %all-reduce.5 = (f32[24]{0:T(128)S(1)}, f32[2]{0:T(128)S(1)}) all-reduce(f32[24]{0:T(128)S(1)} %dynamic-update-slice.7, f32[2]{0:T(128)S(1)} %dynamic-update-slice.8), channel_id=2, replica_groups=mesh['basin'=16,'unit'=2] {'unit'}, use_global_device_ids=true, to_apply=%add | all-reduce | flops 26 | bytes 208
  138.0 4.1 %while.67 = (s32[]{:T(128)}, f32[12]{0:T(128)S(1)}, f32[1]{0:T(128)}, s32[]{:T(128)}, f32[2,12]{1,0:T(2,128)S(1)}, /*index=5*/f32[2,1]{0,1:T(1,128)S(1)}, s32[]{:T(128)}, s32[]{:T(128)}) while((s32[]{:T(128)}, f32[12]{0:T(128)S(1)}, f32[1]{0:T(128)}, s32[]{:T(128)}, f32[2,12]{1,0:T(2,128)S(1)}, /*index=5*/f32[2,1]{0,1:T(1,128)S(1)}, ...), condition=%wide.region_9.10_spmd.clone, body=%wide.region_8.9_spmd.clone.sunk | while | flops 54 | bytes 294 | solution.py:21
  142.2 38.9 %all-reduce.4 = (f32[384]{0:T(512)S(1)}, f32[32]{0:T(128)S(1)}) all-reduce(f32[384]{0:T(512)S(1)} %add_dynamic-update-slice_fusion, f32[32]{0:T(128)S(1)} %multiply_dynamic-update-slice_fusion), channel_id=4, replica_groups=mesh['basin'=16,'unit'=2] {'basin','unit'}, use_global_device_ids=true, to_apply=%add.2 | all-reduce | flops 416 | bytes 3328
  181.6 108.3 %while.65 = (s32[]{:T(128)}, f32[17,12]{1,0:T(8,128)S(1)}, s32[16]{0:T(128)S(1)}, s32[16]{0:T(128)S(1)}, f32[12,16]{0,1:T(8,128)S(1)}, /*index=5*/f32[16,12]{1,0...) while((s32[]{:T(128)}, f32[17,12]{1,0:T(8,128)S(1)}, ...), condition=%wide.region_12.13_spmd, body=%wide.region_10.12_spmd.sunk | while | flops 75 | bytes 575 | solution.py:162
  193.7 1.4 broadcast_select_fusion.12
  207.3 1.4 broadcast_select_fusion.12
  214.0 1.4 broadcast_select_fusion.12
  227.6 1.4 broadcast_select_fusion.12
  247.9 1.4 broadcast_select_fusion.12
  261.4 1.4 broadcast_select_fusion.12
  268.2 1.4 broadcast_select_fusion.12
  (338 shorter events, 138.6 us)
Async XLA Ops:
  0.0 53.7 %copy-start = (bf16[8,8,128,128]{3,2,1,0:T(8,128)(2,1)S(1)}, bf16[8,8,128,128]{3,2,1,0:T(8,128)(2,1)}, u32[]{:S(2)}) copy-start(bf16[8,8,128,128]{3,2,1,0:T(8,128)(2,1)} %param.35) | copy-start | bytes 6291460
  4.9 50.4 %all-to-all-start = ((s32[16,1,8]{2,1,0:T(1,128)}), s32[16,1,8]{2,1,0:T(1,128)S(1)}, u32[]{:S(2)}, u32[]{:S(2)}) async-start(s32[16,1,8]{2,1,0:T(1,128)} %bitcast.9), calls=%async_computation | async-start | bytes 16384 | tf_op jit(solution)/shard_map/all_to_all | solution.py:123
  12.3 1.4 copy-start.1
  12.3 1.4 copy-start.3
  15.7 1.4 copy-start.1
  15.7 1.4 copy-start.3
  19.2 1.4 copy-start.1
  19.2 1.4 copy-start.3
  22.6 1.4 copy-start.1
  22.6 1.4 copy-start.3
  26.1 1.4 copy-start.1
  26.1 1.4 copy-start.3
  29.5 1.4 copy-start.1
  29.5 1.4 copy-start.3
  33.0 1.4 copy-start.1
  33.0 1.4 copy-start.3
  36.4 1.4 copy-start.1
  36.4 1.4 copy-start.3
  39.8 1.4 copy-start.1
  39.9 1.4 copy-start.3
  43.3 1.4 copy-start.1
  46.7 1.4 copy-start.1
  50.2 1.4 copy-start.1
  50.2 1.4 copy-start.3
  53.6 7.7 %copy-start.10 = (u32[32]{0:T(128)S(1)}, u32[32]{0:T(128)}, u32[]{:S(2)}) copy-start(u32[32]{0:T(128)} %constant.196) | copy-start | bytes 388
  53.6 8.4 %copy-start.6 = (f32[12,16]{1,0:T(8,128)S(1)}, f32[12,16]{1,0:T(8,128)}, u32[]{:S(2)}) copy-start(f32[12,16]{1,0:T(8,128)} %param.41) | copy-start | bytes 2308
  53.6 8.4 %copy-start.7 = (s32[16]{0:T(128)S(1)}, s32[16]{0:T(128)}, u32[]{:S(2)}) copy-start(s32[16]{0:T(128)} %param.38) | copy-start | bytes 196
  53.7 20.2 %copy-start.2 = (f32[8,128,128]{2,1,0:T(8,128)S(1)}, f32[8,128,128]{2,1,0:T(8,128)}, u32[]{:S(2)}) copy-start(f32[8,128,128]{2,1,0:T(8,128)} %param.36) | copy-start | bytes 1572868
  55.2 18.2 %all-to-all-start.1 = ((bf16[16,8,1536]{2,1,0:T(8,128)(2,1)}), bf16[16,8,1536]{2,1,0:T(8,128)(2,1)S(1)}, u32[]{:S(2)}, u32[]{:S(2)}) async-start(bf16[16,8,1536]{2,1,0:T(8,128)(2,1)} %fusion.23), calls=%async_computation.1 | async-start | bytes 786432 | tf_op jit(solution)/shard_map/all_to_all | solution.py:122
  61.3 120.3 %copy-start.5 = (s32[2]{0:T(128)S(1)}, s32[2]{0:T(128)}, u32[]{:S(2)}) copy-start(s32[2]{0:T(128)} %constant.174.clone.1) | copy-start | bytes 28
  61.3 120.3 %copy-start.8 = (s32[16]{0:T(128)S(1)}, s32[16]{0:T(128)}, u32[]{:S(2)}) copy-start(s32[16]{0:T(128)} %param.39) | copy-start | bytes 196
  61.3 120.3 %copy-start.9 = (s32[16]{0:T(128)S(1)}, s32[16]{0:T(128)}, u32[]{:S(2)}) copy-start(s32[16]{0:T(128)} %param.40) | copy-start | bytes 196
  (14 other events, 19.0 us)
where the time goes:
time: 295 us; the launch traced here: 292 us
  other arithmetic  79.4 us (27%)
  local copies, waits for them, and re-layouts  56.8 us (19%)
  loops' own time  55.4 us (19%)
  blocking collectives  43.9 us (15%)
  matrix products  34.3 us (12%)
  starting transfers between devices  13.4 us (5%)
  waiting for transfers between devices  7.92 us (3%)
    unnamed x2, blocking collectives  43.9 us
    another operation x1, loops' own time, shards(): lax.fori_loop(0, basin_size, tree_step, jnp.zeros((basin_size + 1, total_...  42.6 us
    another operation x32, other arithmetic  34.3 us
    dot_general x12, matrix products, lstm_step(): jnp.dot(w_recur, hidden, preferred_element_type=jnp.float32)  16 us
    dot_general x12, matrix products, lstm_step(): gate_sum = jnp.dot(w_input, frame_now, preferred_element_type=jnp.float32)  16 us
    dynamic_update_slice x8, other arithmetic, shards(): lax.scan(chain_step, chain_init, (kernel_out, carry_gain, live_blocks))  11.2 us
    select_n x8, other arithmetic, chain_step(): resp_blk = jnp.where(live_one, resp_blk, 0.0)  11.1 us
    dynamic_slice x16, local copies, waits for them, and re-layouts, tree_step(): outflow = sec_shift[section] + sec_factor[section] * inflow_acc[section]  10.7 us
  transfers between devices with their start and end apart: 2, of which 1 were waited for; matrix products, arithmetic and copies ran while one was open for 15% of the time, Pallas kernels for 0%

commit v1 on v0

v1 whole, which is shorter than its diff:
```python
import functools

import jax
import jax.numpy as jnp
from jax import lax
from jax.experimental import pallas as pl
from jax.experimental.pallas import tpu as pltpu
from jax.sharding import PartitionSpec as P

PRECISE = lax.Precision.HIGHEST
AXES = ("basin", "unit")
ROW_PAD = 16


def stage_bits(size):
    return [bit for bit in range(size.bit_length() - 1)]


def slot_of(relative, size):
    slot = relative * 0
    for bit in stage_bits(size):
        slot = slot * 2 + ((relative >> bit) & 1)
    return slot


def split3(x):
    high = x.astype(jnp.bfloat16)
    rest = x - high.astype(jnp.float32)
    middle = rest.astype(jnp.bfloat16)
    low = (rest - middle.astype(jnp.float32)).astype(jnp.bfloat16)
    return high, middle, low


def units_kernel(
    dest_ref,
    block_ref,
    forcing_ref,
    hidden_ref,
    cell_ref,
    w_input_ref,
    w_recur_ref,
    bias_ref,
    head_ref,
    weight_hbm,
    keep_ref,
    send_ref,
    table,
    hidden,
    cell,
    head_sum,
    weight,
    slots,
    packed,
    sem,
    *,
    size,
    reach_blocks,
    chunk,
):
    steps, features, units = forcing_ref.shape
    state = hidden_ref.shape[0]
    unit_blocks, fan_out, block, _ = weight_hbm.shape
    gates = 4 * state
    depth = state + features + ROW_PAD
    fetch = pltpu.make_async_copy(weight_hbm, weight, sem)
    fetch.start()

    for gate in range(4):
        rows = pl.ds(gate * state, state)
        scale = 0.5 if gate == 2 else 0.25
        table[rows, 0:state] = (w_recur_ref[rows, :].astype(jnp.float32) * scale).astype(jnp.bfloat16)
    row = lax.broadcasted_iota(jnp.int32, (state - features, gates), 0)
    parts = [part.astype(jnp.float32) for part in split3(bias_ref[...])]
    bias_rows = jnp.zeros((state - features, gates), jnp.float32)
    for at, part in enumerate(parts):
        bias_rows = jnp.where(row == at, jnp.broadcast_to(part, bias_rows.shape), bias_rows)
    tail = jnp.concatenate([w_input_ref[...].astype(jnp.float32), bias_rows], axis=0)
    lane = lax.broadcasted_iota(jnp.int32, tail.shape, 1)
    tail = jnp.where((lane >= 2 * state) & (lane < 3 * state), tail, tail * 0.5)
    for gate in range(4):
        piece = tail[:, gate * state : (gate + 1) * state]
        table[gate * state : (gate + 1) * state, state : 2 * state] = piece.T.astype(jnp.bfloat16)
    row = lax.broadcasted_iota(jnp.int32, (ROW_PAD, state), 0)
    head_rows = jnp.zeros((ROW_PAD, state), jnp.float32)
    for at, part in enumerate(split3(head_ref[...] * 0.5)):
        head_rows = jnp.where(
            row == at, jnp.broadcast_to(part.astype(jnp.float32), head_rows.shape), head_rows
        )
    table[gates : gates + ROW_PAD, 0:state] = head_rows.astype(jnp.bfloat16)
    table[gates : gates + ROW_PAD, state : 2 * state] = jnp.zeros((ROW_PAD, state), jnp.bfloat16)
    hidden[...] = hidden_ref[...] + hidden_ref[...]
    cell[...] = cell_ref[...]
    head_sum[...] = jnp.zeros_like(head_sum)
    slots[...] = jnp.zeros_like(slots)
    ones = jnp.ones((ROW_PAD, chunk), jnp.bfloat16)

    def step(now, carry):
        for first in range(0, units, chunk):
            cols = pl.ds(first, chunk)
            operand = jnp.concatenate([hidden[:, cols], forcing_ref[now, :, cols], ones], axis=0)
            total = jnp.dot(table[:, 0:depth], operand, preferred_element_type=jnp.float32)
            head_sum[pl.ds((now + ROW_PAD - 1) % ROW_PAD, 1), cols] = (
                total[gates : gates + 1] + total[gates + 1 : gates + 2] + total[gates + 2 : gates + 3]
            )
            in_gate = jnp.tanh(total[0:state]) + 1.0
            forget = jnp.tanh(total[state : 2 * state]) + 1.0
            candidate = jnp.tanh(total[2 * state : 3 * state])
            out_gate = jnp.tanh(total[3 * state : 4 * state]) + 1.0
            after = (forget * cell[:, cols] + in_gate * candidate) * 0.5
            cell[:, cols] = after
            hidden[:, cols] = (out_gate * jnp.tanh(after)).astype(jnp.bfloat16)
        return carry

    lax.fori_loop(0, steps, step, 0)
    last = jnp.dot(
        table[gates : gates + ROW_PAD, 0:state], hidden[...], preferred_element_type=jnp.float32
    )
    head_sum[steps - 1 : steps, :] = last[0:1] + last[1:2] + last[2:3]
    runoff = jax.nn.softplus(head_sum[...]).astype(jnp.bfloat16)

    me = lax.axis_index("basin")
    fetch.wait()
    for group in range(unit_blocks):
        left = runoff[:, group * block : (group + 1) * block]
        for k in range(fan_out):
            contrib = jnp.dot(left, weight[group, k], preferred_element_type=jnp.float32)
            slot = slot_of(dest_ref[group, k] ^ me, size) * reach_blocks + block_ref[group, k]
            slots[slot] = slots[slot] + contrib
    half = size // 2

    def pack(at):
        for blk in range(reach_blocks):
            packed[at, blk * steps : (blk + 1) * steps, :] = slots[at * reach_blocks + blk, 0:steps, :]

    if size <= 16:
        for at in range(size):
            pack(at)
    else:

        def pack_step(at, carry):
            pack(at)
            return carry

        lax.fori_loop(0, size, pack_step, 0)
    keep_ref[...] = packed[0:half].astype(jnp.bfloat16)
    send_ref[...] = packed[half:size].astype(jnp.bfloat16)


def units_call(forcing, hidden_init, cell_init, w_input, w_recur, gate_bias, w_head, dest, blk, weight, reach_blocks):
    size = lax.axis_size("basin")
    steps, features, units = forcing.shape
    state = hidden_init.shape[0]
    gates = 4 * state
    block = weight.shape[3]
    chunk = 256
    half = jax.ShapeDtypeStruct((size // 2, reach_blocks * steps, block), jnp.bfloat16)
    vmem = pl.BlockSpec(memory_space=pltpu.VMEM)
    smem = pl.BlockSpec(memory_space=pltpu.SMEM)
    return pl.pallas_call(
        functools.partial(units_kernel, size=size, reach_blocks=reach_blocks, chunk=chunk),
        out_shape=(half, half),
        in_specs=[smem, smem] + [vmem] * 7 + [pl.BlockSpec(memory_space=pl.ANY)],
        out_specs=(vmem, vmem),
        scratch_shapes=[
            pltpu.VMEM((gates + ROW_PAD, 2 * state), jnp.bfloat16),
            pltpu.VMEM((state, units), jnp.bfloat16),
            pltpu.VMEM((state, units), jnp.float32),
            pltpu.VMEM((ROW_PAD, units), jnp.float32),
            pltpu.VMEM(weight.shape, weight.dtype),
            pltpu.VMEM((size * reach_blocks, ROW_PAD, block), jnp.float32),
            pltpu.VMEM((size, reach_blocks * steps, block), jnp.float32),
            pltpu.SemaphoreType.DMA,
        ],
        compiler_params=pltpu.CompilerParams(vmem_limit_bytes=(16 << 20) + size * (192 << 10)),
        name="units",
    )(
        dest,
        blk,
        forcing,
        hidden_init,
        cell_init,
        w_input.T,
        w_recur,
        gate_bias.reshape(1, gates),
        w_head.reshape(1, state),
        weight,
    )


def route_kernel_body(
    count_ref, mine_ref, other_ref, kernel_ref, gain_ref, flow_ref, map_ref, *, steps, copies
):
    reach_blocks, block, _ = kernel_ref.shape
    lateral = mine_ref[...].astype(jnp.float32) + other_ref[...].astype(jnp.float32)
    first = lax.axis_index("unit") * reach_blocks
    count = count_ref[lax.axis_index("basin")]
    shift = jnp.zeros((steps, block), jnp.float32)
    factor = jnp.ones((1, block), jnp.float32)
    for blk in range(reach_blocks):
        rows = slice(blk * steps, (blk + 1) * steps)
        flow = lax.dot_general(
            lateral[rows], kernel_ref[blk], (((1,), (1,)), ((), ())), precision=PRECISE,
            preferred_element_type=jnp.float32,
        )
        flow_ref[rows, :] = flow
        gain = gain_ref[blk : blk + 1, :]
        live = first + blk < count
        shift = jnp.where(live, flow + shift * gain, shift)
        factor = jnp.where(live, factor * gain, factor)
    tile = jnp.concatenate(
        [
            jnp.broadcast_to(shift[:, block - 1 : block], (steps, block)),
            jnp.broadcast_to(factor[:, block - 1 : block], (ROW_PAD - steps, block)),
        ],
        axis=0,
    )
    for at in range(copies):
        map_ref[at] = tile


def finish_kernel(
    count_ref, parent_ref, reservoir_ref, release_ref, map_ref, flow_ref, gain_ref, out_ref, inflow, *, steps
):
    reach_blocks, block = gain_ref.shape
    size, unit_size = lax.axis_size("basin"), lax.axis_size("unit")
    basin, unit = lax.axis_index("basin"), lax.axis_index("unit")
    inflow[...] = jnp.zeros_like(inflow)

    def join(section, head):
        for at in range(unit_size):
            tile = map_ref[section * unit_size + at]
            head = tile + jnp.broadcast_to(tile[steps : steps + 1], tile.shape) * head
        return head

    def tree(section, carry):
        outflow = join(section, inflow[section])
        given = jnp.broadcast_to(release_ref[section], outflow.shape)
        passed = jnp.where(reservoir_ref[section] == 1, given, outflow)
        parent = parent_ref[section]
        inflow[parent] = inflow[parent] + passed
        return carry

    lax.fori_loop(0, size, tree, 0)
    head = inflow[basin]
    for at in range(unit_size - 1):
        tile = map_ref[basin * unit_size + at]
        through = tile + jnp.broadcast_to(tile[steps : steps + 1], tile.shape) * head
        head = jnp.where(at < unit, through, head)
    carry = head[0:steps]
    count = count_ref[basin]
    for blk in range(reach_blocks):
        live = unit * reach_blocks + blk < count
        flow = flow_ref[blk * steps : (blk + 1) * steps, :] + carry * gain_ref[blk : blk + 1, :]
        out_ref[:, blk * block : (blk + 1) * block] = jnp.where(live, flow, 0.0)
        carry = jnp.where(live, jnp.broadcast_to(flow[:, block - 1 : block], carry.shape), carry)


def shards(
    forcing,
    hidden_init,
    cell_init,
    w_input,
    w_recur,
    gate_bias,
    w_head,
    remap_dest,
    remap_block,
    remap_weight,
    route_kernel,
    carry_gain,
    block_count,
    parent_section,
    reservoir,
    release,
):
    steps = forcing.shape[0]
    reach_blocks, block, _ = route_kernel.shape
    size, unit_size = lax.axis_size("basin"), lax.axis_size("unit")
    keep, send = units_call(
        forcing, hidden_init, cell_init, w_input, w_recur, gate_bias, w_head,
        remap_dest, remap_block, remap_weight, reach_blocks,
    )
    for at, bit in enumerate(stage_bits(size)):
        if at > 0:
            total = (keep.astype(jnp.float32) + got.astype(jnp.float32)).astype(jnp.bfloat16)
            half = total.shape[0] // 2
            keep, send = total[:half], total[half:]
        got = lax.ppermute(send, "basin", [(i, i ^ (1 << bit)) for i in range(size)])
    vmem = pl.BlockSpec(memory_space=pltpu.VMEM)
    smem = pl.BlockSpec(memory_space=pltpu.SMEM)
    copies = size * unit_size
    flow, own = pl.pallas_call(
        functools.partial(route_kernel_body, steps=steps, copies=copies),
        out_shape=(
            jax.ShapeDtypeStruct((reach_blocks * steps, block), jnp.float32),
            jax.ShapeDtypeStruct((copies, ROW_PAD, block), jnp.float32),
        ),
        in_specs=[smem] + [vmem] * 4,
        out_specs=(vmem, vmem),
        name="route",
    )(block_count, keep[0], got[0], route_kernel, carry_gain)
    maps = lax.all_to_all(own, AXES, split_axis=0, concat_axis=0, tiled=True)
    given = jnp.pad(release.T, ((0, 0), (0, ROW_PAD - steps)))[:, :, None]
    return pl.pallas_call(
        functools.partial(finish_kernel, steps=steps),
        out_shape=jax.ShapeDtypeStruct((steps, reach_blocks * block), jnp.float32),
        in_specs=[smem, smem, smem] + [vmem] * 4,
        out_specs=vmem,
        scratch_shapes=[pltpu.VMEM((size + 1, ROW_PAD, block), jnp.float32)],
        name="finish",
    )(block_count, parent_section, reservoir, given, maps, flow, carry_gain)


def solution(mesh):
    placed = (
        P(None, None, AXES),
        P(None, AXES),
        P(None, AXES),
        P(),
        P(),
        P(),
        P(),
        P(AXES, None),
        P(AXES, None),
        P(AXES, None, None, None),
        P(AXES, None, None),
        P(AXES, None),
        P(),
        P(),
        P(),
        P(),
    )
    return jax.shard_map(
        shards, mesh=mesh, in_specs=placed, out_specs=P(None, AXES), check_vma=False
    )
```

time: 295 us -> 59.5 us (0.20)
  other arithmetic: 79.4 us -> 0.1 us
  loops' own time: 55.4 us -> 0 us
  local copies, waits for them, and re-layouts: 56.8 us -> 11.9 us
  blocking collectives: 43.9 us -> 0 us
  matrix products: 34.3 us -> 0 us
  Pallas kernels: 0 us -> 14.4 us
  waiting for transfers between devices: 7.92 us -> 18.1 us
    another operation x4 -> x0, loops' own time: 55.4 us -> none  [the longest x1 42.6 us: shards(): lax.fori_loop(0, basin_size, tree_step, jnp.zeros((basin_size + 1, total_...]
    unnamed x2 -> x0, blocking collectives: 43.9 us -> none
    dynamic_slice x59 -> x0, local copies, waits for them, and re-layouts: 38.1 us -> none  [the longest x16 10.7 us: tree_step(): outflow = sec_shift[section] + sec_factor[section] * inflow_acc[section]]
    another operation x33 -> x0, other arithmetic: 34.4 us -> none
    dot_general x28 -> x0, matrix products: 34.3 us -> none  [the longest x12 16 us: lstm_step(): jnp.dot(w_recur, hidden, preferred_element_type=jnp.float32)]
    select_n x18 -> x0, other arithmetic: 22.5 us -> none  [the longest x8 11.1 us: chain_step(): resp_blk = jnp.where(live_one, resp_blk, 0.0)]
    pallas_call x0 -> x3, Pallas kernels: none -> 14.4 us  [the longest x1 8.23 us: units_call(): pl.pallas_call(functools.partial(units_kernel, size=size, reach_blocks=re...]
    dynamic_update_slice x8 -> x0, other arithmetic: 11.2 us -> none  [shards(): lax.scan(chain_step, chain_init, (kernel_out, carry_gain, live_blocks))]
  transfers between devices with their start and end apart: 2 -> 5, of which waited for: 1 -> 5; matrix products, arithmetic and copies ran while one was open for 15% -> 2% of each run, Pallas kernels for 0% -> 0%
where the time goes in v1:
time: 59.5 us; the launch traced here: 59 us
  waiting for transfers between devices  18.1 us (30%)
  Pallas kernels  14.4 us (24%)
  starting transfers between devices  14.4 us (24%)
  local copies, waits for them, and re-layouts  11.9 us (20%)
    unnamed x27, local copies, waits for them, and re-layouts  10.5 us
    all_to_all x1, waiting for transfers between devices, shards(): maps = lax.all_to_all(own, AXES, split_axis=0, concat_axis=0, tiled=True)  9.77 us
    ppermute x4, waiting for transfers between devices, shards(): got = lax.ppermute(send, 'basin', [(i, i ^ 1 << bit) for i in range(size)])  8.37 us
    pallas_call x1, Pallas kernels, units_call(): pl.pallas_call(functools.partial(units_kernel, size=size, reach_blocks=re...  8.23 us
    ppermute x4, starting transfers between devices, shards(): got = lax.ppermute(send, 'basin', [(i, i ^ 1 << bit) for i in range(size)])  8.15 us
    all_to_all x1, starting transfers between devices, shards(): maps = lax.all_to_all(own, AXES, split_axis=0, concat_axis=0, tiled=True)  6.22 us
    pallas_call x1, Pallas kernels, shards(): pl.pallas_call(functools.partial(finish_kernel, steps=steps), out_shape=j...  3.32 us
    pallas_call x1, Pallas kernels, shards(): pl.pallas_call(functools.partial(route_kernel_body, steps=steps, copies=c...  2.8 us
  transfers between devices with their start and end apart: 5, of which 5 were waited for; matrix products, arithmetic and copies ran while one was open for 2% of the time, Pallas kernels for 0%

profile of v1, /device:TPU:0, one launch (start us, length us, event | category | flops | bytes accessed | tf_op | source)
XLA Modules:
  0.0 59.0 jit_solution(10789800474198417785)
XLA Ops:
  0.0 1.6 %copy-done = bf16[8,8,128,128]{3,2,1,0:T(8,128)(2,1)S(1)} copy-done((bf16[8,8,128,128]{3,2,1,0:T(8,128)(2,1)S(1)}, bf16[8,8,128,128]{3,2,1,0:T(8,128)(2,1)}, u32[]{:S(2)}) %copy-start) | copy-done | bytes 2097176
  1.6 0.0 copy-start.1
  1.6 1.1 %copy-done.1 = bf16[12,32,1024]{2,1,0:T(8,128)(2,1)S(1)} copy-done((bf16[12,32,1024]{2,1,0:T(8,128)(2,1)S(1)}, bf16[12,32,1024]{2,1,0:T(8,128)(2,1)}, u32[]{:S(2)}) %copy-start.1) | copy-done | bytes 786456
  2.7 1.0 %copy-done.2 = f32[128,1024]{1,0:T(8,128)S(1)} copy-done((f32[128,1024]{1,0:T(8,128)S(1)}, f32[128,1024]{1,0:T(8,128)}, u32[]{:S(2)}) %copy-start.2) | copy-done | bytes 524312
  3.8 0.9 %copy-done.3 = bf16[128,1024]{1,0:T(8,128)(2,1)S(1)} copy-done((bf16[128,1024]{1,0:T(8,128)(2,1)S(1)}, bf16[128,1024]{1,0:T(8,128)(2,1)}, u32[]{:S(2)}) %copy-start.3) | copy-done | bytes 262168
  4.7 0.9 %copy-done.4 = bf16[512,128]{1,0:T(8,128)(2,1)S(1)} copy-done((bf16[512,128]{1,0:T(8,128)(2,1)S(1)}, bf16[512,128]{1,0:T(8,128)(2,1)}, u32[]{:S(2)}) %copy-start.4) | copy-done | bytes 131096
  5.6 0.8 %copy-done.5 = bf16[512,32]{0,1:T(8,128)(2,1)S(1)} copy-done((bf16[512,32]{0,1:T(8,128)(2,1)S(1)}, bf16[512,32]{0,1:T(8,128)(2,1)}, u32[]{:S(2)}) %copy-start.5) | copy-done | bytes 32792
  6.4 0.7 %copy-done.6 = s32[8,8]{1,0:T(8,128)S(1)} copy-done((s32[8,8]{1,0:T(8,128)S(1)}, s32[8,8]{1,0:T(8,128)}, u32[]{:S(2)}) %copy-start.6) | copy-done | bytes 280
  7.1 0.7 %copy-done.7 = s32[8,8]{1,0:T(8,128)S(1)} copy-done((s32[8,8]{1,0:T(8,128)S(1)}, s32[8,8]{1,0:T(8,128)}, u32[]{:S(2)}) %copy-start.7) | copy-done | bytes 280
  7.8 0.7 %copy-done.8 = f32[512]{0:T(512)S(1)} copy-done((f32[512]{0:T(512)S(1)}, f32[512]{0:T(512)}, u32[]{:S(2)}) %copy-start.8) | copy-done | bytes 2072
  8.4 0.7 %copy-done.9 = f32[128]{0:T(128)S(1)} copy-done((f32[128]{0:T(128)S(1)}, f32[128]{0:T(128)}, u32[]{:S(2)}) %copy-start.9) | copy-done | bytes 536
  9.1 8.2 %units.1 = (bf16[8,96,128]{2,1,0:T(8,128)(2,1)S(1)}, bf16[8,96,128]{2,1,0:T(8,128)(2,1)S(1)}) custom-call(s32[8,8]{1,0:T(8,128)S(1)} %copy-done.6, s32[8,8]{1,0:T(8,128)S(1)} %copy-done.7, bf16[12,32,1024]{2,1,0:T(8,128)(2,1)S(1)} %copy-done.1, bf16[128,1024]{1,0:T(8,128)(2,1)S(1)} %copy-done.3, f32[128,1024]{1,0:T(8,128)S(1)} %copy-done.2, ...), custom_call_target="tpu_custom_call" | custom-call | tf_op jit(solution)/shard_map/units/pallas_call | solution.py:159
  17.3 0.0 copy-start.12
  17.3 0.5 collective-permute-start
  17.9 1.1 %collective-permute-done = bf16[8,96,128]{2,1,0:T(8,128)(2,1)S(1)} collective-permute-done((bf16[8,96,128]{2,1,0:T(8,128)(2,1)S(1)}, bf16[8,96,128]{2,1,0:T(8,128)(2,1)S(1)}, u32[]{:S(2)}, u32[]{:S(2)}) %collective-permute-start) | collective-permute-done | bytes 196640 | tf_op jit(solution)/shard_map/ppermute | solution.py:288
  18.9 0.1 add_convert_fusion
  19.0 2.9 %collective-permute-start.1 = (bf16[4,96,128]{2,1,0:T(8,128)(2,1)S(1)}, bf16[4,96,128]{2,1,0:T(8,128)(2,1)S(1)}, u32[]{:S(2)}, u32[]{:S(2)}) collective-permute-start(bf16[4,96,128]{2,1,0:T(8,128)(2,1)S(1)} %slice.25), channel_id=1, source_target_pairs={{0,4},{2,6},{4,0},{6,2},{8,12},{10,14},{12,8},{14,10},{16,20},{18,... | collective-permute-start | bytes 294920 | tf_op jit(solution)/shard_map/ppermute | solution.py:288
  22.0 3.1 %collective-permute-done.1 = bf16[4,96,128]{2,1,0:T(8,128)(2,1)S(1)} collective-permute-done((bf16[4,96,128]{2,1,0:T(8,128)(2,1)S(1)}, bf16[4,96,128]{2,1,0:T(8,128)(2,1)S(1)}, u32[]{:S(2)}, u32[]{:S(2)}) %collective-permute-start.1) | collective-permute-done | bytes 98336 | tf_op jit(solution)/shard_map/ppermute | solution.py:288
  25.1 1.9 %collective-permute-start.2 = (bf16[2,96,128]{2,1,0:T(8,128)(2,1)S(1)}, bf16[2,96,128]{2,1,0:T(8,128)(2,1)S(1)}, u32[]{:S(2)}, u32[]{:S(2)}) collective-permute-start(bf16[2,96,128]{2,1,0:T(8,128)(2,1)S(1)} %slice.27), channel_id=1, source_target_pairs={{0,8},{2,10},{4,12},{6,14},{8,0},{10,2},{12,4},{14,6},{16,24},{18,... | collective-permute-start | bytes 147464 | tf_op jit(solution)/shard_map/ppermute | solution.py:288
  27.0 2.3 %collective-permute-done.2 = bf16[2,96,128]{2,1,0:T(8,128)(2,1)S(1)} collective-permute-done((bf16[2,96,128]{2,1,0:T(8,128)(2,1)S(1)}, bf16[2,96,128]{2,1,0:T(8,128)(2,1)S(1)}, u32[]{:S(2)}, u32[]{:S(2)}) %collective-permute-start.2) | collective-permute-done | bytes 49184 | tf_op jit(solution)/shard_map/ppermute | solution.py:288
  29.3 0.6 %fusion = (bf16[1,96,128]{2,1,0:T(8,128)(2,1)S(1)}, bf16[96,128]{1,0:T(8,128)(2,1)}) fusion(bf16[2,96,128]{2,1,0:T(8,128)(2,1)S(1)} %add_convert_fusion.2), kind=kLoop, calls=%fused_computation.5 | loop fusion | bytes 98304 | tf_op jit(solution)/shard_map/slice | solution.py:287
  29.9 2.8 %collective-permute-start.3 = (bf16[1,96,128]{2,1,0:T(8,128)(2,1)S(1)}, bf16[1,96,128]{2,1,0:T(8,128)(2,1)S(1)}, u32[]{:S(2)}, u32[]{:S(2)}) collective-permute-start(bf16[1,96,128]{2,1,0:T(8,128)(2,1)S(1)} %get-tuple-element.13), channel_id=1, source_target_pairs={{0,16},{2,18},{4,20},{6,22},{8,24},{10,26},{12,28},{14,30},{16,0},... | collective-permute-start | bytes 73736 | tf_op jit(solution)/shard_map/ppermute | solution.py:288
  32.7 1.9 %collective-permute-done.3 = bf16[1,96,128]{2,1,0:T(8,128)(2,1)S(1)} collective-permute-done((bf16[1,96,128]{2,1,0:T(8,128)(2,1)S(1)}, bf16[1,96,128]{2,1,0:T(8,128)(2,1)S(1)}, u32[]{:S(2)}, u32[]{:S(2)}) %collective-permute-start.3) | collective-permute-done | bytes 24608 | tf_op jit(solution)/shard_map/ppermute | solution.py:288
  34.6 0.6 %copy-done.11 = bf16[1,96,128]{2,1,0:T(8,128)(2,1)} copy-done((bf16[1,96,128]{2,1,0:T(8,128)(2,1)}, bf16[1,96,128]{2,1,0:T(8,128)(2,1)S(1)}, u32[]{:S(2)}) %copy-start.11) | copy-done | bytes 24600
  35.2 2.8 %route.1 = (f32[96,128]{1,0:T(8,128)}, f32[32,16,128]{2,1,0:T(8,128)}) custom-call(s32[16]{0:T(128)} %count_ref.3, bf16[96,128]{1,0:T(8,128)(2,1)} %get-tuple-element.14.mine_ref, bf16[96,128]{1,0:T(8,128)(2,1)} %bitcast.13, f32[8,128,128]{2,1,0:T(8,128)} %kernel_ref.1, f32[8,128]{1,0:T(8,128)} %gain_ref.3), custom_call_target="tpu_custom_call" | custom-call | tf_op jit(solution)/shard_map/route/pallas_call | solution.py:292
  38.0 6.2 %all-to-all-start = ((f32[32,16,128]{2,1,0:T(8,128)}), f32[32,16,128]{2,1,0:T(8,128)S(1)}, u32[]{:S(2)}, u32[]{:S(2)}) async-start(f32[32,16,128]{2,1,0:T(8,128)} %get-tuple-element.11), calls=%async_computation | async-start | bytes 524288 | tf_op jit(solution)/shard_map/all_to_all | solution.py:302
  44.3 0.0 copy-done.12
  44.3 0.1 copy.18
  44.4 0.8 %copy.19.release_ref = f32[16,16,1]{2,1,0:T(8,128)} copy(f32[16,16,1]{1,0,2:T(8,128)S(1)} %pad_bitcast_fusion) | data formatting | bytes 2048 | tf_op jit(solution)/shard_map/broadcast_in_dim | solution.py:303
  45.2 9.8 %all-to-all-done.map_ref = f32[32,16,128]{2,1,0:T(8,128)S(1)} async-done(((f32[32,16,128]{2,1,0:T(8,128)}), f32[32,16,128]{2,1,0:T(8,128)S(1)}, u32[]{:S(2)}, u32[]{:S(2)}) %all-to-all-start) | async-done | bytes 262176 | tf_op jit(solution)/shard_map/all_to_all | solution.py:302
  55.0 0.7 %copy-done.10 = f32[32,16,128]{2,1,0:T(8,128)} copy-done((f32[32,16,128]{2,1,0:T(8,128)}, f32[32,16,128]{2,1,0:T(8,128)S(1)}, u32[]{:S(2)}) %copy-start.10) | copy-done | bytes 262168
  55.6 3.3 %finish.1 = f32[12,1024]{1,0:T(8,128)} custom-call(s32[16]{0:T(128)} %count_ref.3, s32[16]{0:T(128)} %parent_ref.1, s32[16]{0:T(128)} %reservoir_ref.1, f32[16,16,1]{2,1,0:T(8,128)} %copy.19.release_ref, f32[32,16,128]{2,1,0:T(8,128)} %copy-done.10, f32[96,128]{1,0:T(8,128)} %get-tuple-element.12.flow_ref, f32[8,128]{1,0:T(8,128)} %gain_ref.3), custom_call_target="tpu_custom_call" | custom-call | tf_op jit(solution)/shard_map/finish/pallas_call | solution.py:304
  (16 shorter events, 0.1 us)
Async XLA Ops:
  0.0 1.6 %copy-start = (bf16[8,8,128,128]{3,2,1,0:T(8,128)(2,1)S(1)}, bf16[8,8,128,128]{3,2,1,0:T(8,128)(2,1)}, u32[]{:S(2)}) copy-start(bf16[8,8,128,128]{3,2,1,0:T(8,128)(2,1)} %weight_hbm.1) | copy-start | bytes 6291460
  1.6 1.1 %copy-start.1 = (bf16[12,32,1024]{2,1,0:T(8,128)(2,1)S(1)}, bf16[12,32,1024]{2,1,0:T(8,128)(2,1)}, u32[]{:S(2)}) copy-start(bf16[12,32,1024]{2,1,0:T(8,128)(2,1)} %forcing_ref.1) | copy-start | bytes 2359300
  2.7 1.0 %copy-start.2 = (f32[128,1024]{1,0:T(8,128)S(1)}, f32[128,1024]{1,0:T(8,128)}, u32[]{:S(2)}) copy-start(f32[128,1024]{1,0:T(8,128)} %cell_ref.1) | copy-start | bytes 1572868
  3.8 0.9 %copy-start.3 = (bf16[128,1024]{1,0:T(8,128)(2,1)S(1)}, bf16[128,1024]{1,0:T(8,128)(2,1)}, u32[]{:S(2)}) copy-start(bf16[128,1024]{1,0:T(8,128)(2,1)} %hidden_ref.1) | copy-start | bytes 786436
  4.7 0.9 %copy-start.4 = (bf16[512,128]{1,0:T(8,128)(2,1)S(1)}, bf16[512,128]{1,0:T(8,128)(2,1)}, u32[]{:S(2)}) copy-start(bf16[512,128]{1,0:T(8,128)(2,1)} %w_recur_ref.1) | copy-start | bytes 393220
  5.6 0.8 %copy-start.5 = (bf16[512,32]{0,1:T(8,128)(2,1)S(1)}, bf16[512,32]{0,1:T(8,128)(2,1)}, u32[]{:S(2)}) copy-start(bf16[512,32]{0,1:T(8,128)(2,1)} %param.19) | copy-start | bytes 98308
  6.4 0.7 %copy-start.6 = (s32[8,8]{1,0:T(8,128)S(1)}, s32[8,8]{1,0:T(8,128)}, u32[]{:S(2)}) copy-start(s32[8,8]{1,0:T(8,128)} %dest_ref.1) | copy-start | bytes 772
  7.1 0.7 %copy-start.7 = (s32[8,8]{1,0:T(8,128)S(1)}, s32[8,8]{1,0:T(8,128)}, u32[]{:S(2)}) copy-start(s32[8,8]{1,0:T(8,128)} %block_ref.1) | copy-start | bytes 772
  7.8 0.7 %copy-start.8 = (f32[512]{0:T(512)S(1)}, f32[512]{0:T(512)}, u32[]{:S(2)}) copy-start(f32[512]{0:T(512)} %param.21) | copy-start | bytes 6148
  8.4 0.7 %copy-start.9 = (f32[128]{0:T(128)S(1)}, f32[128]{0:T(128)}, u32[]{:S(2)}) copy-start(f32[128]{0:T(128)} %param.22) | copy-start | bytes 1540
  17.3 26.9 %copy-start.12 = (f32[12,16]{1,0:T(8,128)S(1)}, f32[12,16]{1,0:T(8,128)}, u32[]{:S(2)}) copy-start(f32[12,16]{1,0:T(8,128)} %param.31) | copy-start | bytes 2308
  17.3 1.6 %collective-permute-start = (bf16[8,96,128]{2,1,0:T(8,128)(2,1)S(1)}, bf16[8,96,128]{2,1,0:T(8,128)(2,1)S(1)}, u32[]{:S(2)}, u32[]{:S(2)}) collective-permute-start(bf16[8,96,128]{2,1,0:T(8,128)(2,1)S(1)} %get-tuple-element.10), channel_id=1, source_target_pairs={{0,2},{2,0},{4,6},{6,4},{8,10},{10,8},{12,14},{14,12},{16,18},{18,... | collective-permute-start | bytes 589832 | tf_op jit(solution)/shard_map/ppermute | solution.py:288
  19.0 6.0 %collective-permute-start.1 = (bf16[4,96,128]{2,1,0:T(8,128)(2,1)S(1)}, bf16[4,96,128]{2,1,0:T(8,128)(2,1)S(1)}, u32[]{:S(2)}, u32[]{:S(2)}) collective-permute-start(bf16[4,96,128]{2,1,0:T(8,128)(2,1)S(1)} %slice.25), channel_id=1, source_target_pairs={{0,4},{2,6},{4,0},{6,2},{8,12},{10,14},{12,8},{14,10},{16,20},{18,... | collective-permute-start | bytes 294920 | tf_op jit(solution)/shard_map/ppermute | solution.py:288
  25.1 4.2 %collective-permute-start.2 = (bf16[2,96,128]{2,1,0:T(8,128)(2,1)S(1)}, bf16[2,96,128]{2,1,0:T(8,128)(2,1)S(1)}, u32[]{:S(2)}, u32[]{:S(2)}) collective-permute-start(bf16[2,96,128]{2,1,0:T(8,128)(2,1)S(1)} %slice.27), channel_id=1, source_target_pairs={{0,8},{2,10},{4,12},{6,14},{8,0},{10,2},{12,4},{14,6},{16,24},{18,... | collective-permute-start | bytes 147464 | tf_op jit(solution)/shard_map/ppermute | solution.py:288
  29.9 4.7 %collective-permute-start.3 = (bf16[1,96,128]{2,1,0:T(8,128)(2,1)S(1)}, bf16[1,96,128]{2,1,0:T(8,128)(2,1)S(1)}, u32[]{:S(2)}, u32[]{:S(2)}) collective-permute-start(bf16[1,96,128]{2,1,0:T(8,128)(2,1)S(1)} %get-tuple-element.13), channel_id=1, source_target_pairs={{0,16},{2,18},{4,20},{6,22},{8,24},{10,26},{12,28},{14,30},{16,0},... | collective-permute-start | bytes 73736 | tf_op jit(solution)/shard_map/ppermute | solution.py:288
  34.6 0.6 %copy-start.11 = (bf16[1,96,128]{2,1,0:T(8,128)(2,1)}, bf16[1,96,128]{2,1,0:T(8,128)(2,1)S(1)}, u32[]{:S(2)}) copy-start(bf16[1,96,128]{2,1,0:T(8,128)(2,1)S(1)} %collective-permute-done.3) | copy-start | bytes 73732
  38.0 16.9 %all-to-all-start = ((f32[32,16,128]{2,1,0:T(8,128)}), f32[32,16,128]{2,1,0:T(8,128)S(1)}, u32[]{:S(2)}, u32[]{:S(2)}) async-start(f32[32,16,128]{2,1,0:T(8,128)} %get-tuple-element.11), calls=%async_computation | async-start | bytes 524288 | tf_op jit(solution)/shard_map/all_to_all | solution.py:302
  54.9 0.7 %copy-start.10 = (f32[32,16,128]{2,1,0:T(8,128)}, f32[32,16,128]{2,1,0:T(8,128)S(1)}, u32[]{:S(2)}) copy-start(f32[32,16,128]{2,1,0:T(8,128)S(1)} %all-to-all-done.map_ref) | copy-start | bytes 786436

commit v2 on v1

v2 whole, which is shorter than its diff:
```python
import functools

import jax
import jax.numpy as jnp
from jax import lax
from jax.experimental import pallas as pl
from jax.experimental.pallas import tpu as pltpu
from jax.sharding import PartitionSpec as P

PRECISE = lax.Precision.HIGHEST
AXES = ("basin", "unit")
PAD = 16
VMEM = pl.BlockSpec(memory_space=pltpu.VMEM)
SMEM = pl.BlockSpec(memory_space=pltpu.SMEM)
HBM = pl.BlockSpec(memory_space=pltpu.HBM)


def in_hbm(*arrays):
    return [pltpu.with_memory_space_constraint(x, pltpu.HBM) for x in arrays]


def in_vmem(*arrays):
    return [pltpu.with_memory_space_constraint(x, pltpu.VMEM) for x in arrays]


def stage_bits(size):
    return range(size.bit_length() - 1)


def slot_of(relative, size):
    slot = relative * 0
    for bit in stage_bits(size):
        slot = slot * 2 + ((relative >> bit) & 1)
    return slot


def split3(x):
    high = x.astype(jnp.bfloat16)
    rest = x - high.astype(jnp.float32)
    middle = rest.astype(jnp.bfloat16)
    low = (rest - middle.astype(jnp.float32)).astype(jnp.bfloat16)
    return high, middle, low


def repeat(count, body):
    if count <= 16:
        for at in range(count):
            body(at)
    else:
        lax.fori_loop(0, count, lambda at, carry: (body(at), carry)[1], 0)


def prep_kernel(count_hbm, route_hbm, gain_hbm, share_ref, last_ref, gain_ref, count_ref, sems, *, size):
    reach_blocks, block = gain_hbm.shape
    copies = [
        pltpu.make_async_copy(route_hbm.at[:, block - 1, :], last_ref, sems.at[0]),
        pltpu.make_async_copy(gain_hbm, gain_ref, sems.at[1]),
        pltpu.make_async_copy(count_hbm, count_ref, sems.at[2]),
    ]
    for copy in copies:
        copy.start()
    for copy in copies:
        copy.wait()
    first = lax.axis_index("unit") * reach_blocks
    count = count_ref[lax.axis_index("basin")]
    factor = jnp.ones((1, block), jnp.float32)
    rows = [None] * reach_blocks
    for blk in reversed(range(reach_blocks)):
        live = first + blk < count
        rows[blk] = jnp.where(live, factor * last_ref[blk : blk + 1, :], 0.0)
        ratio = jnp.broadcast_to(gain_ref[blk : blk + 1, block - 1 : block], (1, block))
        factor = jnp.where(live, factor * ratio, factor)
    rows.append(factor * (1.0 / size))
    rows.append(jnp.zeros((PAD - len(rows), block), jnp.float32))
    tile = jnp.concatenate(rows, axis=0)

    def spread(at):
        share_ref[at] = tile

    repeat(size, spread)


def lstm_kernel(
    w_recur_hbm,
    w_input_hbm,
    bias_hbm,
    head_hbm,
    hidden_hbm,
    cell_hbm,
    release_hbm,
    forcing_hbm,
    weight_hbm,
    route_hbm,
    gain_hbm,
    runoff_ref,
    weight_ref,
    route_ref,
    gain_ref,
    given_ref,
    w_recur_ref,
    w_input_ref,
    bias_ref,
    head_ref,
    hidden,
    cell,
    release_ref,
    forcing_ref,
    table,
    head_sum,
    square,
    frame_sems,
    sems,
    *,
    chunk,
):
    steps, features, units = forcing_hbm.shape
    state = hidden_hbm.shape[0]
    gates = 4 * state
    depth = state + features + PAD
    pairs = [
        (w_recur_hbm, w_recur_ref),
        (w_input_hbm, w_input_ref),
        (bias_hbm, bias_ref),
        (head_hbm, head_ref),
        (hidden_hbm, hidden),
        (cell_hbm, cell),
        (release_hbm, release_ref),
        (gain_hbm, gain_ref),
        (weight_hbm, weight_ref),
        (route_hbm, route_ref),
    ]
    copies = [pltpu.make_async_copy(a, b, sems.at[at]) for at, (a, b) in enumerate(pairs)]

    def frame(now):
        return pltpu.make_async_copy(forcing_hbm.at[now], forcing_ref.at[now], frame_sems.at[now])

    for copy in copies[:7]:
        copy.start()
    for now in range(steps):
        frame(now).start()
    for copy in copies[7:]:
        copy.start()
    square[...] = jnp.zeros_like(square)
    table[gates : gates + PAD, state : 2 * state] = jnp.zeros((PAD, state), jnp.bfloat16)
    head_sum[...] = jnp.zeros_like(head_sum)
    copies[0].wait()
    for gate in range(4):
        at = pl.ds(gate * state, state)
        scale = 0.5 if gate == 2 else 0.25
        table[at, 0:state] = (w_recur_ref[at, :].astype(jnp.float32) * scale).astype(jnp.bfloat16)
    for copy in copies[1:4]:
        copy.wait()
    row = lax.broadcasted_iota(jnp.int32, (state - features, gates), 0)
    bias_rows = jnp.zeros((state - features, gates), jnp.float32)
    for at, part in enumerate(split3(bias_ref[...])):
        part = jnp.broadcast_to(part.astype(jnp.float32), bias_rows.shape)
        bias_rows = jnp.where(row == at, part, bias_rows)
    tail = jnp.concatenate([w_input_ref[...].astype(jnp.float32), bias_rows], axis=0)
    for gate in range(4):
        piece = tail[:, gate * state : (gate + 1) * state] * (1.0 if gate == 2 else 0.5)
        table[gate * state : (gate + 1) * state, state : 2 * state] = piece.T.astype(jnp.bfloat16)
    row = lax.broadcasted_iota(jnp.int32, (PAD, state), 0)
    head_rows = jnp.zeros((PAD, state), jnp.float32)
    for at, part in enumerate(split3(head_ref[...] * 0.5)):
        part = jnp.broadcast_to(part.astype(jnp.float32), head_rows.shape)
        head_rows = jnp.where(row == at, part, head_rows)
    table[gates : gates + PAD, 0:state] = head_rows.astype(jnp.bfloat16)
    copies[6].wait()
    square[0:steps, 0 : release_ref.shape[1]] = release_ref[...]
    given_ref[...] = square[...].T[0 : given_ref.shape[0]]
    for copy in copies[4:6]:
        copy.wait()
    hidden[...] = hidden[...] + hidden[...]
    ones = jnp.ones((PAD, chunk), jnp.bfloat16)

    def step(now, carry):
        frame(now).wait()
        for first in range(0, units, chunk):
            cols = pl.ds(first, chunk)
            operand = jnp.concatenate([hidden[:, cols], forcing_ref[now, :, cols], ones], axis=0)
            total = jnp.dot(table[:, 0:depth], operand, preferred_element_type=jnp.float32)
            head_sum[pl.ds((now + PAD - 1) % PAD, 1), cols] = (
                total[gates : gates + 1] + total[gates + 1 : gates + 2] + total[gates + 2 : gates + 3]
            )
            in_gate = jnp.tanh(total[0:state]) + 1.0
            forget = jnp.tanh(total[state : 2 * state]) + 1.0
            candidate = jnp.tanh(total[2 * state : 3 * state])
            out_gate = jnp.tanh(total[3 * state : 4 * state]) + 1.0
            after = (forget * cell[:, cols] + in_gate * candidate) * 0.5
            cell[:, cols] = after
            hidden[:, cols] = (out_gate * jnp.tanh(after)).astype(jnp.bfloat16)
        return carry

    lax.fori_loop(0, steps, step, 0)
    last = jnp.dot(table[gates : gates + PAD, 0:state], hidden[...], preferred_element_type=jnp.float32)
    head_sum[steps - 1 : steps, :] = last[0:1] + last[1:2] + last[2:3]
    runoff_ref[...] = jax.nn.softplus(head_sum[...]).astype(jnp.bfloat16)
    for copy in copies[7:]:
        copy.wait()


def remap_kernel(
    dest_ref,
    block_ref,
    runoff_ref,
    weight_ref,
    share_ref,
    keep_ref,
    send_ref,
    shift_ref,
    slots,
    square,
    *,
    size,
    reach_blocks,
    steps,
):
    unit_blocks, fan_out, block, _ = weight_ref.shape
    me = lax.axis_index("basin")
    slots[...] = jnp.zeros_like(slots)
    square[...] = jnp.zeros_like(square)
    for group in range(unit_blocks):
        left = runoff_ref[:, group * block : (group + 1) * block]
        for k in range(fan_out):
            contrib = jnp.dot(left, weight_ref[group, k], preferred_element_type=jnp.float32)
            slot = slot_of(dest_ref[group, k] ^ me, size) * reach_blocks + block_ref[group, k]
            slots[slot] = slots[slot] + contrib
    half = size // 2
    rows = reach_blocks * steps
    lane = lax.broadcasted_iota(jnp.int32, (PAD, block), 1)
    row = lax.broadcasted_iota(jnp.int32, (PAD, 1), 0)
    origin = lax.axis_index("unit") * PAD

    def gather(at, out_ref, base, columns):
        pieces = [slots[at * reach_blocks + blk] for blk in range(reach_blocks)]
        tile = jnp.concatenate([piece[0:steps] for piece in pieces], axis=0)
        out_ref[pl.ds((at - base) * rows, rows), :] = tile.astype(jnp.bfloat16)
        section = slot_of(at, size) ^ me
        share = share_ref[section]
        total = pieces[0] * share[0:1]
        for blk in range(1, reach_blocks):
            total = total + pieces[blk] * share[blk : blk + 1]
        column = jnp.sum(total, axis=1, keepdims=True)
        column = jnp.where(row == steps, share[reach_blocks : reach_blocks + 1, 0:1], column)
        column = jnp.where(row > steps, 0.0, column)
        return jnp.where(lane == section, column, columns)

    columns = jnp.zeros((PAD, block), jnp.float32)
    if size <= 16:
        for at in range(size):
            columns = gather(at, keep_ref if at < half else send_ref, 0 if at < half else half, columns)
    else:
        columns = lax.fori_loop(0, half, lambda at, c: gather(at, keep_ref, 0, c), columns)
        columns = lax.fori_loop(half, size, lambda at, c: gather(at, send_ref, half, c), columns)
    square[pl.ds(pl.multiple_of(origin, PAD), PAD), :] = columns
    shift = square[...].T[0:size]
    shift_ref[...] = shift
    high = shift.astype(jnp.bfloat16)
    send_ref[half * rows : half * rows + size, :] = high
    send_ref[half * rows + size : half * rows + 2 * size, :] = (shift - high.astype(jnp.float32)).astype(jnp.bfloat16)


def finish_kernel(
    count_ref,
    parent_ref,
    reservoir_ref,
    given_ref,
    shift_ref,
    mine_ref,
    got_ref,
    route_ref,
    gain_ref,
    out_ref,
    inflow,
    joined,
    *,
    steps,
    unit_size,
):
    reach_blocks, block = gain_ref.shape
    size = shift_ref.shape[0]
    basin, unit = lax.axis_index("basin"), lax.axis_index("unit")
    rows = reach_blocks * steps
    high = got_ref[rows : rows + size, :].astype(jnp.float32)
    total = shift_ref[...] + (high + got_ref[rows + size : rows + 2 * size, :].astype(jnp.float32))
    lateral = mine_ref[...].astype(jnp.float32) + got_ref[0:rows, :].astype(jnp.float32)
    flows = []
    for blk in range(reach_blocks):
        flows.append(
            lax.dot_general(
                lateral[blk * steps : (blk + 1) * steps], route_ref[blk], (((1,), (1,)), ((), ())),
                precision=PRECISE, preferred_element_type=jnp.float32,
            )
        )
    shift = jnp.zeros_like(total)
    factor = jnp.ones_like(total)
    for at in range(unit_size):
        own = jnp.broadcast_to(total[:, at * PAD + steps : at * PAD + steps + 1], total.shape)
        moved = total if at == 0 else pltpu.roll(total, block - at * PAD, 1)
        shift = moved + own * shift
        factor = factor * own
        joined[at, 0] = moved
        joined[at, 1] = own
    joined[unit_size, 0] = shift
    joined[unit_size, 1] = factor
    inflow[...] = jnp.zeros_like(inflow)

    def tree(section):
        at = pl.ds(section, 1)
        outflow = joined[unit_size, 0, at, :] + joined[unit_size, 1, at, :] * inflow[at, :]
        passed = jnp.where(reservoir_ref[section] == 1, given_ref[at, :], outflow)
        parent = pl.ds(parent_ref[section], 1)
        inflow[parent, :] = inflow[parent, :] + passed

    repeat(size, tree)
    here = pl.ds(basin, 1)
    head = inflow[here, :]
    for at in range(unit_size - 1):
        head = jnp.where(at < unit, joined[at, 0, here, :] + joined[at, 1, here, :] * head, head)
    lane = lax.broadcasted_iota(jnp.int32, (PAD, block), 1)
    row = lax.broadcasted_iota(jnp.int32, (PAD, block), 0)
    column = jnp.sum(jnp.where(lane == row, jnp.broadcast_to(head, lane.shape), 0.0), axis=1, keepdims=True)
    carry = jnp.broadcast_to(column[0:steps], (steps, block))
    count = count_ref[basin]
    for blk in range(reach_blocks):
        live = unit * reach_blocks + blk < count
        flow = flows[blk] + carry * gain_ref[blk : blk + 1, :]
        out_ref[:, blk * block : (blk + 1) * block] = jnp.where(live, flow, 0.0)
        carry = jnp.where(live, jnp.broadcast_to(flow[:, block - 1 : block], carry.shape), carry)


def halves(shift):
    high = lax.reduce_precision(shift, 8, 7)
    return [high.astype(jnp.bfloat16), lax.reduce_precision(shift - high, 8, 7).astype(jnp.bfloat16)]


def shards(
    forcing,
    hidden_init,
    cell_init,
    w_input,
    w_recur,
    gate_bias,
    w_head,
    remap_dest,
    remap_block,
    remap_weight,
    route_kernel,
    carry_gain,
    block_count,
    parent_section,
    reservoir,
    release,
):
    steps, features, units = forcing.shape
    state = hidden_init.shape[0]
    gates = 4 * state
    reach_blocks, block, _ = route_kernel.shape
    size, unit_size = lax.axis_size("basin"), lax.axis_size("unit")
    rows = reach_blocks * steps
    like = lambda x: pltpu.VMEM(x.shape, x.dtype)
    params = pltpu.CompilerParams(vmem_limit_bytes=(8 << 20) + (size << 18))

    share = pl.pallas_call(
        functools.partial(prep_kernel, size=size),
        out_shape=jax.ShapeDtypeStruct((size, PAD, block), jnp.float32),
        in_specs=[HBM] * 3,
        out_specs=VMEM,
        scratch_shapes=[
            pltpu.VMEM((reach_blocks, block), jnp.float32),
            pltpu.VMEM((reach_blocks, block), jnp.float32),
            pltpu.SMEM(block_count.shape, jnp.int32),
            pltpu.SemaphoreType.DMA((3,)),
        ],
        compiler_params=params,
        name="prep",
    )(*in_hbm(block_count, route_kernel, carry_gain))
    shares = lax.all_to_all(share, "basin", split_axis=0, concat_axis=0, tiled=True)
    runoff, weight_v, route_v, gain_v, given = pl.pallas_call(
        functools.partial(lstm_kernel, chunk=256),
        out_shape=(
            pltpu.VMEM((PAD, units), jnp.bfloat16),
            like(remap_weight),
            like(route_kernel),
            like(carry_gain),
            pltpu.VMEM((size, block), jnp.float32),
        ),
        in_specs=[HBM] * 11,
        out_specs=(VMEM,) * 5,
        scratch_shapes=[
            pltpu.VMEM((gates, state), jnp.bfloat16),
            pltpu.VMEM((features, gates), jnp.bfloat16),
            pltpu.VMEM((1, gates), jnp.float32),
            pltpu.VMEM((1, state), jnp.float32),
            pltpu.VMEM((state, units), jnp.bfloat16),
            pltpu.VMEM((state, units), jnp.float32),
            pltpu.VMEM(release.shape, jnp.float32),
            pltpu.VMEM((steps, features, units), jnp.bfloat16),
            pltpu.VMEM((gates + PAD, 2 * state), jnp.bfloat16),
            pltpu.VMEM((PAD, units), jnp.float32),
            pltpu.VMEM((block, block), jnp.float32),
            pltpu.SemaphoreType.DMA((steps,)),
            pltpu.SemaphoreType.DMA((10,)),
        ],
        compiler_params=params,
        cost_estimate=pl.CostEstimate(
            flops=2 * steps * gates * (state + features) * units,
            bytes_accessed=4 << 20,
            transcendentals=5 * steps * state * units,
        ),
        name="lstm",
    )(
        *in_hbm(
            w_recur,
            w_input.T,
            gate_bias.reshape(1, gates),
            w_head.reshape(1, state),
            hidden_init,
            cell_init,
            release,
            forcing,
            remap_weight,
            route_kernel,
            carry_gain,
        )
    )
    keep, send, shift = pl.pallas_call(
        functools.partial(remap_kernel, size=size, reach_blocks=reach_blocks, steps=steps),
        out_shape=(
            pltpu.VMEM((size // 2 * rows, block), jnp.bfloat16),
            pltpu.VMEM((size // 2 * rows + 2 * size, block), jnp.bfloat16),
            pltpu.VMEM((size, block), jnp.float32),
        ),
        in_specs=[SMEM, SMEM] + [VMEM] * 3,
        out_specs=(VMEM,) * 3,
        scratch_shapes=[
            pltpu.VMEM((size * reach_blocks, PAD, block), jnp.float32),
            pltpu.VMEM((block, block), jnp.float32),
        ],
        compiler_params=params,
        name="remap",
    )(remap_dest, remap_block, *in_vmem(runoff, weight_v), shares)

    wide = jnp.float32
    exchange = [(at, bit) for at, bit in enumerate(stage_bits(size))]
    across_at = min(1, len(exchange) - 1)
    for at, bit in exchange:
        if at > 0:
            kept = keep.shape[0]
            total = (keep.astype(wide) + got[:kept].astype(wide)).astype(jnp.bfloat16)
            shift = shift + (got[kept : kept + size].astype(wide) + got[kept + size :].astype(wide))
            for part in others:
                shift = shift + part
            keep, send = total[: kept // 2], jnp.concatenate([total[kept // 2 :]] + halves(shift), axis=0)
        swap = 1 << bit
        got = lax.ppermute(send, "basin", [(i, i ^ swap) for i in range(size)])
        others = []
        if at == across_at:
            for turn in range(1, unit_size):
                for hop in (0, swap):
                    route = [
                        (b * unit_size + u, (b ^ hop) * unit_size + (u ^ turn))
                        for b in range(size)
                        for u in range(unit_size)
                    ]
                    others.append(lax.ppermute(shift, AXES, route))
    for part in others:
        shift = shift + part
    return pl.pallas_call(
        functools.partial(finish_kernel, steps=steps, unit_size=unit_size),
        out_shape=jax.ShapeDtypeStruct((steps, reach_blocks * block), jnp.float32),
        in_specs=[SMEM, SMEM, SMEM] + [VMEM] * 6,
        out_specs=VMEM,
        scratch_shapes=[
            pltpu.VMEM((size + 8, block), jnp.float32),
            pltpu.VMEM((unit_size + 1, 2, size, block), jnp.float32),
        ],
        compiler_params=params,
        name="finish",
    )(block_count, parent_section, reservoir, *in_vmem(given), shift, keep, got, *in_vmem(route_v, gain_v))


def solution(mesh):
    placed = (
        P(None, None, AXES),
        P(None, AXES),
        P(None, AXES),
        P(),
        P(),
        P(),
        P(),
        P(AXES, None),
        P(AXES, None),
        P(AXES, None, None, None),
        P(AXES, None, None),
        P(AXES, None),
        P(),
        P(),
        P(),
        P(),
    )
    return jax.shard_map(
        shards, mesh=mesh, in_specs=placed, out_specs=P(None, AXES), check_vma=False
    )
```

time: 59.5 us -> 40.4 us (0.68)
  local copies, waits for them, and re-layouts: 11.9 us -> 0.05 us
  waiting for transfers between devices: 18.1 us -> 10.7 us
  starting transfers between devices: 14.4 us -> 15.4 us
  Pallas kernels: 14.4 us -> 13.7 us
    unnamed x27 -> x10, local copies, waits for them, and re-layouts: 10.5 us -> 0.03 us
    all_to_all x1, waiting for transfers between devices: 9.77 us -> 0.01 us  [shards(): lax.all_to_all(share, 'basin', split_axis=0, concat_axis=0, tiled=True)]
    ppermute x4 -> x6, waiting for transfers between devices: 8.37 us -> 10.6 us  [the longest x4 6.23 us: shards(): got = lax.ppermute(send, 'basin', [(i, i ^ swap) for i in range(size)])]
    all_to_all x1, starting transfers between devices: 6.22 us -> 7.4 us  [shards(): lax.all_to_all(share, 'basin', split_axis=0, concat_axis=0, tiled=True)]
    broadcast_in_dim x2 -> x0, local copies, waits for them, and re-layouts: 0.83 us -> none  [shards(): given = jnp.pad(release.T, ((0, 0), (0, ROW_PAD - steps)))[:, :, None]]
    pallas_call x3 -> x4, Pallas kernels: 14.4 us -> 13.7 us  [the longest x1 8.22 us: shards(): pl.pallas_call(functools.partial(lstm_kernel, chunk=256), out_shape=(pltp...]
    slice x3, local copies, waits for them, and re-layouts: 0.63 us -> 0.02 us  [shards(): total[kept // 2:]]
    ppermute x4 -> x6, starting transfers between devices: 8.15 us -> 8 us  [the longest x4 6.38 us: shards(): got = lax.ppermute(send, 'basin', [(i, i ^ swap) for i in range(size)])]
  transfers between devices with their start and end apart: 5 -> 7, of which waited for: 5 -> 5; matrix products, arithmetic and copies ran while one was open for 2% -> 0% of each run, Pallas kernels for 0% -> 20%
where the time goes in v2:
time: 40.4 us; the launch traced here: 40.1 us
  starting transfers between devices  15.4 us (38%)
  Pallas kernels  13.7 us (34%)
  waiting for transfers between devices  10.7 us (26%)
    pallas_call x1, Pallas kernels, shards(): pl.pallas_call(functools.partial(lstm_kernel, chunk=256), out_shape=(pltp...  8.22 us
    all_to_all x1, starting transfers between devices, shards(): lax.all_to_all(share, 'basin', split_axis=0, concat_axis=0, tiled=True)  7.4 us
    ppermute x4, starting transfers between devices, shards(): got = lax.ppermute(send, 'basin', [(i, i ^ swap) for i in range(size)])  6.38 us
    ppermute x4, waiting for transfers between devices, shards(): got = lax.ppermute(send, 'basin', [(i, i ^ swap) for i in range(size)])  6.23 us
    ppermute x2, waiting for transfers between devices, shards(): others.append(lax.ppermute(shift, AXES, route))  4.42 us
    pallas_call x1, Pallas kernels, shards(): pl.pallas_call(functools.partial(finish_kernel, steps=steps, unit_size=un...  2.19 us
    pallas_call x1, Pallas kernels, shards(): pl.pallas_call(functools.partial(remap_kernel, size=size, reach_blocks=re...  1.7 us
    ppermute x2, starting transfers between devices, shards(): others.append(lax.ppermute(shift, AXES, route))  1.62 us
  transfers between devices with their start and end apart: 7, of which 5 were waited for; matrix products, arithmetic and copies ran while one was open for 0% of the time, Pallas kernels for 20%

profile of v2, /device:TPU:0, one launch (start us, length us, event | category | flops | bytes accessed | tf_op | source)
XLA Modules:
  0.0 40.1 jit_solution(14693684207479486977)
XLA Ops:
  0.0 1.6 %prep.1 = f32[16,16,128]{2,1,0:T(8,128)} custom-call(s32[16]{0:T(128)} %count_ref.1, f32[8,128,128]{2,1,0:T(8,128)} %route_hbm.3, f32[8,128]{1,0:T(8,128)} %gain_hbm.3), custom_call_target="tpu_custom_call" | custom-call | tf_op jit(solution)/shard_map/prep/pallas_call | solution.py:364
  1.6 7.4 %all-to-all-start = ((f32[16,16,128]{2,1,0:T(8,128)}), f32[16,16,128]{2,1,0:T(8,128)S(1)}, u32[]{:S(2)}, u32[]{:S(2)}) async-start(f32[16,16,128]{2,1,0:T(8,128)} %prep.1), calls=%async_computation | async-start | bytes 262144 | tf_op jit(solution)/shard_map/all_to_all | solution.py:378
  9.0 0.0 copy-start
  9.0 0.0 copy-start.1
  9.0 8.2 %lstm.1 = (bf16[16,1024]{1,0:T(8,128)(2,1)S(1)}, bf16[8,8,128,128]{3,2,1,0:T(8,128)(2,1)S(1)}, f32[8,128,128]{2,1,0:T(8,128)S(1)}, f32[8,128]{1,0:T(8,128)S(1)}, f32[16,128]{1,0:T(8,128)S(1)}) custom-call(bf16[512,128]{1,0:T(8,128)(2,1)} %w_recur_hbm.1, bf16[32,512]{1,0:T(8,128)(2,1)} %bitcast.3, f32[1,512]{1,0:T(1,128)} %bitcast.4, f32[1,128]{1,0:T(1,128)} %bitcast.5, ...), custom_call_target="tpu_custom_call" | custom-call | flops 2013265920 | bytes 4194304 | tf_op jit(solution)/shard_map/lstm/pallas_call | solution.py:379
  17.2 0.0 all-to-all-done.share_ref
  17.3 0.0 copy-done
  17.3 0.0 copy-done.1
  17.3 0.0 copy-start.2
  17.3 0.0 copy-start.3
  17.3 0.0 copy-start.4
  17.3 1.7 %remap.1 = (bf16[768,128]{1,0:T(8,128)(2,1)S(1)}, bf16[800,128]{1,0:T(8,128)(2,1)S(1)}, f32[16,128]{1,0:T(8,128)S(1)}) custom-call(s32[8,8]{1,0:T(8,128)S(1)} %copy-done, s32[8,8]{1,0:T(8,128)S(1)} %copy-done.1, bf16[16,1024]{1,0:T(8,128)(2,1)S(1)} %get-tuple-element.14.runoff_ref, bf16[8,8,128,128]{3,2,1,0:T(8,128)(2,1)S(1)} %get-tuple-element.15.weight_ref, ...), custom_call_target="tpu_custom_call" | custom-call | tf_op jit(solution)/shard_map/remap/pallas_call | solution.py:427
  19.0 0.5 %collective-permute-start = (bf16[800,128]{1,0:T(8,128)(2,1)S(1)}, bf16[800,128]{1,0:T(8,128)(2,1)S(1)}, u32[]{:S(2)}, u32[]{:S(2)}) collective-permute-start(bf16[800,128]{1,0:T(8,128)(2,1)S(1)} %get-tuple-element.17), channel_id=1, source_target_pairs={{0,2},{2,0},{4,6},{6,4},{8,10},{10,8},{12,14},{14,12},{16,18},{18,... | collective-permute-start | bytes 614408 | tf_op jit(solution)/shard_map/ppermute | solution.py:456
  19.5 1.1 %collective-permute-done = bf16[800,128]{1,0:T(8,128)(2,1)S(1)} collective-permute-done((bf16[800,128]{1,0:T(8,128)(2,1)S(1)}, bf16[800,128]{1,0:T(8,128)(2,1)S(1)}, u32[]{:S(2)}, u32[]{:S(2)}) %collective-permute-start) | collective-permute-done | bytes 204832 | tf_op jit(solution)/shard_map/ppermute | solution.py:456
  20.6 0.1 add_convert_fusion
  20.7 1.9 %collective-permute-start.1 = (bf16[416,128]{1,0:T(8,128)(2,1)S(1)}, bf16[416,128]{1,0:T(8,128)(2,1)S(1)}, u32[]{:S(2)}, u32[]{:S(2)}) collective-permute-start(bf16[416,128]{1,0:T(8,128)(2,1)S(1)} %pad_maximum_fusion), channel_id=1, source_target_pairs={{0,4},{2,6},{4,0},{6,2},{8,12},{10,14},{12,8},{14,10},{16,20},{18,... | collective-permute-start | bytes 319496 | tf_op jit(solution)/shard_map/ppermute | solution.py:456
  22.6 1.5 %collective-permute-start.2 = (f32[16,128]{1,0:T(8,128)S(1)}, f32[16,128]{1,0:T(8,128)S(1)}, u32[]{:S(2)}, u32[]{:S(2)}) collective-permute-start(f32[16,128]{1,0:T(8,128)S(1)} %get-tuple-element.26), channel_id=1, source_target_pairs={{0,1},{1,0},{2,3},{3,2},{4,5},{5,4},{6,7},{7,6},{8,9},{9,8},{10,11... | collective-permute-start | bytes 24584 | tf_op jit(solution)/shard_map/ppermute | solution.py:466
  24.1 0.1 collective-permute-start.3
  24.2 2.0 %collective-permute-done.2 = f32[16,128]{1,0:T(8,128)S(1)} collective-permute-done((f32[16,128]{1,0:T(8,128)S(1)}, f32[16,128]{1,0:T(8,128)S(1)}, u32[]{:S(2)}, u32[]{:S(2)}) %collective-permute-start.2) | collective-permute-done | bytes 8224 | tf_op jit(solution)/shard_map/ppermute | solution.py:466
  26.3 2.4 %collective-permute-done.3 = f32[16,128]{1,0:T(8,128)S(1)} collective-permute-done((f32[16,128]{1,0:T(8,128)S(1)}, f32[16,128]{1,0:T(8,128)S(1)}, u32[]{:S(2)}, u32[]{:S(2)}) %collective-permute-start.3) | collective-permute-done | bytes 8224 | tf_op jit(solution)/shard_map/ppermute | solution.py:466
  28.7 0.0 collective-permute-done.1
  28.7 1.5 %collective-permute-start.4 = (bf16[224,128]{1,0:T(8,128)(2,1)S(1)}, bf16[224,128]{1,0:T(8,128)(2,1)S(1)}, u32[]{:S(2)}, u32[]{:S(2)}) collective-permute-start(bf16[224,128]{1,0:T(8,128)(2,1)S(1)} %pad_maximum_fusion.1), channel_id=1, source_target_pairs={{0,8},{2,10},{4,12},{6,14},{8,0},{10,2},{12,4},{14,6},{16,24},{18,... | collective-permute-start | bytes 172040 | tf_op jit(solution)/shard_map/ppermute | solution.py:456
  30.3 2.7 %collective-permute-done.4 = bf16[224,128]{1,0:T(8,128)(2,1)S(1)} collective-permute-done((bf16[224,128]{1,0:T(8,128)(2,1)S(1)}, bf16[224,128]{1,0:T(8,128)(2,1)S(1)}, u32[]{:S(2)}, u32[]{:S(2)}) %collective-permute-start.4) | collective-permute-done | bytes 57376 | tf_op jit(solution)/shard_map/ppermute | solution.py:456
  33.1 2.4 %collective-permute-start.5 = (bf16[128,128]{1,0:T(8,128)(2,1)S(1)}, bf16[128,128]{1,0:T(8,128)(2,1)S(1)}, u32[]{:S(2)}, u32[]{:S(2)}) collective-permute-start(bf16[128,128]{1,0:T(8,128)(2,1)S(1)} %pad_maximum_fusion.2), channel_id=1, source_target_pairs={{0,16},{2,18},{4,20},{6,22},{8,24},{10,26},{12,28},{14,30},{16,0},... | collective-permute-start | bytes 98312 | tf_op jit(solution)/shard_map/ppermute | solution.py:456
  35.5 2.4 %collective-permute-done.5.got_ref = bf16[128,128]{1,0:T(8,128)(2,1)S(1)} collective-permute-done((bf16[128,128]{1,0:T(8,128)(2,1)S(1)}, bf16[128,128]{1,0:T(8,128)(2,1)S(1)}, u32[]{:S(2)}, u32[]{:S(2)}) %collective-permute-start.5) | collective-permute-done | bytes 32800 | tf_op jit(solution)/shard_map/ppermute | solution.py:456
  37.9 0.0 copy-done.2
  37.9 0.0 copy-done.3
  37.9 0.0 copy-done.4
  37.9 2.2 %finish.1 = f32[12,1024]{1,0:T(8,128)} custom-call(s32[16]{0:T(128)S(1)} %copy-done.2, s32[16]{0:T(128)S(1)} %copy-done.3, s32[16]{0:T(128)S(1)} %copy-done.4, f32[16,128]{1,0:T(8,128)S(1)} %get-tuple-element.13.given_ref, f32[16,128]{1,0:T(8,128)S(1)} %get-tuple-element.22.shift_ref, bf16[96,128]{1,0:T(8,128)(2,1)S(1)} %get-tuple-element.28.mine_ref, ...), custom_call_target="tpu_custom_call" | custom-call | tf_op jit(solution)/shard_map/finish/pallas_call | solution.py:469
  (14 shorter events, 0.1 us)
Async XLA Ops:
  1.6 15.7 %all-to-all-start = ((f32[16,16,128]{2,1,0:T(8,128)}), f32[16,16,128]{2,1,0:T(8,128)S(1)}, u32[]{:S(2)}, u32[]{:S(2)}) async-start(f32[16,16,128]{2,1,0:T(8,128)} %prep.1), calls=%async_computation | async-start | bytes 262144 | tf_op jit(solution)/shard_map/all_to_all | solution.py:378
  9.0 8.3 %copy-start = (s32[8,8]{1,0:T(8,128)S(1)}, s32[8,8]{1,0:T(8,128)}, u32[]{:S(2)}) copy-start(s32[8,8]{1,0:T(8,128)} %dest_ref.1) | copy-start | bytes 772
  9.0 8.3 %copy-start.1 = (s32[8,8]{1,0:T(8,128)S(1)}, s32[8,8]{1,0:T(8,128)}, u32[]{:S(2)}) copy-start(s32[8,8]{1,0:T(8,128)} %block_ref.1) | copy-start | bytes 772
  17.3 20.7 %copy-start.2 = (s32[16]{0:T(128)S(1)}, s32[16]{0:T(128)}, u32[]{:S(2)}) copy-start(s32[16]{0:T(128)} %count_ref.1) | copy-start | bytes 196
  17.3 20.7 %copy-start.3 = (s32[16]{0:T(128)S(1)}, s32[16]{0:T(128)}, u32[]{:S(2)}) copy-start(s32[16]{0:T(128)} %parent_ref.1) | copy-start | bytes 196
  17.3 20.6 %copy-start.4 = (s32[16]{0:T(128)S(1)}, s32[16]{0:T(128)}, u32[]{:S(2)}) copy-start(s32[16]{0:T(128)} %reservoir_ref.1) | copy-start | bytes 196
  19.0 1.5 %collective-permute-start = (bf16[800,128]{1,0:T(8,128)(2,1)S(1)}, bf16[800,128]{1,0:T(8,128)(2,1)S(1)}, u32[]{:S(2)}, u32[]{:S(2)}) collective-permute-start(bf16[800,128]{1,0:T(8,128)(2,1)S(1)} %get-tuple-element.17), channel_id=1, source_target_pairs={{0,2},{2,0},{4,6},{6,4},{8,10},{10,8},{12,14},{14,12},{16,18},{18,... | collective-permute-start | bytes 614408 | tf_op jit(solution)/shard_map/ppermute | solution.py:456
  20.7 8.0 %collective-permute-start.1 = (bf16[416,128]{1,0:T(8,128)(2,1)S(1)}, bf16[416,128]{1,0:T(8,128)(2,1)S(1)}, u32[]{:S(2)}, u32[]{:S(2)}) collective-permute-start(bf16[416,128]{1,0:T(8,128)(2,1)S(1)} %pad_maximum_fusion), channel_id=1, source_target_pairs={{0,4},{2,6},{4,0},{6,2},{8,12},{10,14},{12,8},{14,10},{16,20},{18,... | collective-permute-start | bytes 319496 | tf_op jit(solution)/shard_map/ppermute | solution.py:456
  22.6 3.7 %collective-permute-start.2 = (f32[16,128]{1,0:T(8,128)S(1)}, f32[16,128]{1,0:T(8,128)S(1)}, u32[]{:S(2)}, u32[]{:S(2)}) collective-permute-start(f32[16,128]{1,0:T(8,128)S(1)} %get-tuple-element.26), channel_id=1, source_target_pairs={{0,1},{1,0},{2,3},{3,2},{4,5},{5,4},{6,7},{7,6},{8,9},{9,8},{10,11... | collective-permute-start | bytes 24584 | tf_op jit(solution)/shard_map/ppermute | solution.py:466
  24.1 4.5 %collective-permute-start.3 = (f32[16,128]{1,0:T(8,128)S(1)}, f32[16,128]{1,0:T(8,128)S(1)}, u32[]{:S(2)}, u32[]{:S(2)}) collective-permute-start(f32[16,128]{1,0:T(8,128)S(1)} %get-tuple-element.26), channel_id=1, source_target_pairs={{0,5},{1,4},{2,7},{3,6},{4,1},{5,0},{6,3},{7,2},{8,13},{9,12},{10,... | collective-permute-start | bytes 24584 | tf_op jit(solution)/shard_map/ppermute | solution.py:466
  28.7 4.2 %collective-permute-start.4 = (bf16[224,128]{1,0:T(8,128)(2,1)S(1)}, bf16[224,128]{1,0:T(8,128)(2,1)S(1)}, u32[]{:S(2)}, u32[]{:S(2)}) collective-permute-start(bf16[224,128]{1,0:T(8,128)(2,1)S(1)} %pad_maximum_fusion.1), channel_id=1, source_target_pairs={{0,8},{2,10},{4,12},{6,14},{8,0},{10,2},{12,4},{14,6},{16,24},{18,... | collective-permute-start | bytes 172040 | tf_op jit(solution)/shard_map/ppermute | solution.py:456
  33.1 4.9 %collective-permute-start.5 = (bf16[128,128]{1,0:T(8,128)(2,1)S(1)}, bf16[128,128]{1,0:T(8,128)(2,1)S(1)}, u32[]{:S(2)}, u32[]{:S(2)}) collective-permute-start(bf16[128,128]{1,0:T(8,128)(2,1)S(1)} %pad_maximum_fusion.2), channel_id=1, source_target_pairs={{0,16},{2,18},{4,20},{6,22},{8,24},{10,26},{12,28},{14,30},{16,0},... | collective-permute-start | bytes 98312 | tf_op jit(solution)/shard_map/ppermute | solution.py:456

commit v3 on v2

--- a/solution.py
+++ b/solution.py
@@ -72,84 +72,39 @@
         factor = jnp.where(live, factor * ratio, factor)
     rows.append(factor * (1.0 / size))
     rows.append(jnp.zeros((PAD - len(rows), block), jnp.float32))
-    tile = jnp.concatenate(rows, axis=0)
-
-    def spread(at):
-        share_ref[at] = tile
-
-    repeat(size, spread)
-
-
-def lstm_kernel(
-    w_recur_hbm,
-    w_input_hbm,
-    bias_hbm,
-    head_hbm,
-    hidden_hbm,
-    cell_hbm,
-    release_hbm,
-    forcing_hbm,
-    weight_hbm,
-    route_hbm,
-    gain_hbm,
-    runoff_ref,
-    weight_ref,
-    route_ref,
-    gain_ref,
-    given_ref,
-    w_recur_ref,
-    w_input_ref,
-    bias_ref,
-    head_ref,
-    hidden,
-    cell,
-    release_ref,
-    forcing_ref,
-    table,
-    head_sum,
-    square,
-    frame_sems,
-    sems,
-    *,
-    chunk,
-):
-    steps, features, units = forcing_hbm.shape
-    state = hidden_hbm.shape[0]
-    gates = 4 * state
-    depth = state + features + PAD
-    pairs = [
-        (w_recur_hbm, w_recur_ref),
-        (w_input_hbm, w_input_ref),
-        (bias_hbm, bias_ref),
-        (head_hbm, head_ref),
-        (hidden_hbm, hidden),
-        (cell_hbm, cell),
-        (release_hbm, release_ref),
-        (gain_hbm, gain_ref),
-        (weight_hbm, weight_ref),
-        (route_hbm, route_ref),
-    ]
-    copies = [pltpu.make_async_copy(a, b, sems.at[at]) for at, (a, b) in enumerate(pairs)]
-
-    def frame(now):
-        return pltpu.make_async_copy(forcing_hbm.at[now], forcing_ref.at[now], frame_sems.at[now])
-
-    for copy in copies[:7]:
-        copy.start()
-    for now in range(steps):
-        frame(now).start()
-    for copy in copies[7:]:
-        copy.start()
-    square[...] = jnp.zeros_like(square)
+    share_ref[...] = jnp.concatenate(rows, axis=0)
+
+
+def advance(table, frame, hidden, cell, hidden_out, cell_out, head_row, *, chunk):
+    state, units = hidden.shape
+    depth = state + frame.shape[0] + PAD
+    ones = jnp.ones((PAD, chunk), jnp.bfloat16)
+    for first in range(0, units, chunk):
+        cols = pl.ds(first, chunk)
+        operand = jnp.concatenate([hidden[:, cols], frame[:, cols], ones], axis=0)
+
+        def gate(at, rows=state):
+            piece = table[at * state : at * state + rows, 0:depth]
+            return jnp.dot(piece, operand, preferred_element_type=jnp.float32)
+
+        if head_row is not None:
+            head = gate(4, PAD)
+            head_row[:, cols] = head[0:1] + head[1:2] + head[2:3]
+        kept = (jnp.tanh(gate(1)) + 1.0) * cell[:, cols]
+        taken = (jnp.tanh(gate(0)) + 1.0) * jnp.tanh(gate(2))
+        after = (kept + taken) * 0.5
+        cell_out[:, cols] = after
+        hidden_out[:, cols] = ((jnp.tanh(gate(3)) + 1.0) * jnp.tanh(after)).astype(jnp.bfloat16)
+
+
+def build_table(table, w_recur_ref, w_input_ref, bias_ref, head_ref):
+    gates, state = w_recur_ref.shape
+    features = w_input_ref.shape[0]
     table[gates : gates + PAD, state : 2 * state] = jnp.zeros((PAD, state), jnp.bfloat16)
-    head_sum[...] = jnp.zeros_like(head_sum)
-    copies[0].wait()
     for gate in range(4):
         at = pl.ds(gate * state, state)
         scale = 0.5 if gate == 2 else 0.25
         table[at, 0:state] = (w_recur_ref[at, :].astype(jnp.float32) * scale).astype(jnp.bfloat16)
-    for copy in copies[1:4]:
-        copy.wait()
     row = lax.broadcasted_iota(jnp.int32, (state - features, gates), 0)
     bias_rows = jnp.zeros((state - features, gates), jnp.float32)
     for at, part in enumerate(split3(bias_ref[...])):
@@ -165,37 +120,99 @@
         part = jnp.broadcast_to(part.astype(jnp.float32), head_rows.shape)
         head_rows = jnp.where(row == at, part, head_rows)
     table[gates : gates + PAD, 0:state] = head_rows.astype(jnp.bfloat16)
-    copies[6].wait()
+
+
+def first_kernel(
+    w_recur_hbm,
+    w_input_hbm,
+    bias_hbm,
+    head_hbm,
+    hidden_hbm,
+    cell_hbm,
+    release_hbm,
+    forcing_hbm,
+    forcing_ref,
+    table,
+    hidden,
+    cell,
+    head_sum,
+    given_ref,
+    w_recur_ref,
+    w_input_ref,
+    bias_ref,
+    head_ref,
+    release_ref,
+    square,
+    frame_sems,
+    sems,
+    *,
+    count,
+    chunk,
+):
+    steps = forcing_hbm.shape[0]
+    pairs = [
+        (w_recur_hbm, w_recur_ref),
+        (w_input_hbm, w_input_ref),
+        (bias_hbm, bias_ref),
+        (head_hbm, head_ref),
+        (release_hbm, release_ref),
+        (hidden_hbm, hidden),
+        (cell_hbm, cell),
+    ]
+    copies = [pltpu.make_async_copy(a, b, sems.at[at]) for at, (a, b) in enumerate(pairs)]
+    frames = [
+        pltpu.make_async_copy(forcing_hbm.at[now], forcing_ref.at[now], frame_sems.at[now])
+        for now in range(steps)
+    ]
+    for copy in copies + frames:
+        copy.start()
+    square[...] = jnp.zeros_like(square)
+    head_sum[...] = jnp.zeros_like(head_sum)
+    for copy in copies[:5]:
+        copy.wait()
+    build_table(table, w_recur_ref, w_input_ref, bias_ref, head_ref)
     square[0:steps, 0 : release_ref.shape[1]] = release_ref[...]
     given_ref[...] = square[...].T[0 : given_ref.shape[0]]
-    for copy in copies[4:6]:
+    for copy in copies[5:]:
         copy.wait()
     hidden[...] = hidden[...] + hidden[...]
-    ones = jnp.ones((PAD, chunk), jnp.bfloat16)
-
-    def step(now, carry):
-        frame(now).wait()
-        for first in range(0, units, chunk):
-            cols = pl.ds(first, chunk)
-            operand = jnp.concatenate([hidden[:, cols], forcing_ref[now, :, cols], ones], axis=0)
-            total = jnp.dot(table[:, 0:depth], operand, preferred_element_type=jnp.float32)
-            head_sum[pl.ds((now + PAD - 1) % PAD, 1), cols] = (
-                total[gates : gates + 1] + total[gates + 1 : gates + 2] + total[gates + 2 : gates + 3]
-            )
-            in_gate = jnp.tanh(total[0:state]) + 1.0
-            forget = jnp.tanh(total[state : 2 * state]) + 1.0
-            candidate = jnp.tanh(total[2 * state : 3 * state])
-            out_gate = jnp.tanh(total[3 * state : 4 * state]) + 1.0
-            after = (forget * cell[:, cols] + in_gate * candidate) * 0.5
-            cell[:, cols] = after
-            hidden[:, cols] = (out_gate * jnp.tanh(after)).astype(jnp.bfloat16)
-        return carry
-
-    lax.fori_loop(0, steps, step, 0)
-    last = jnp.dot(table[gates : gates + PAD, 0:state], hidden[...], preferred_element_type=jnp.float32)
-    head_sum[steps - 1 : steps, :] = last[0:1] + last[1:2] + last[2:3]
-    runoff_ref[...] = jax.nn.softplus(head_sum[...]).astype(jnp.bfloat16)
-    for copy in copies[7:]:
+    for now in range(count):
+        frames[now].wait()
+        row = head_sum.at[now - 1 : now] if now > 0 else None
+        advance(table, forcing_ref.at[now], hidden, cell, hidden, cell, row, chunk=chunk)
+    for now in range(count, steps):
+        frames[now].wait()
+
+
+def later_kernel(*refs, first, count, last, fetched, chunk):
+    forcing_ref, table, hidden_in, cell_in, head_in = refs[:5]
+    sources, refs = refs[6 : 6 + fetched], refs[6 + fetched :]
+    if last:
+        runoff_ref, refs = refs[0], refs[1:]
+    else:
+        (hidden, cell, head_sum), refs = refs[:3], refs[3:]
+    targets, refs = refs[:fetched], refs[fetched:]
+    if last:
+        hidden, cell, head_sum, sems = refs
+    else:
+        (sems,) = refs
+    copies = [pltpu.make_async_copy(a, b, sems.at[at]) for at, (a, b) in enumerate(zip(sources, targets))]
+    for copy in copies:
+        copy.start()
+    state = hidden_in.shape[0]
+    gates = 4 * state
+    head_sum[...] = head_in[...]
+    for now in range(first, first + count):
+        begin = now == first
+        row = head_sum.at[now - 1 : now]
+        old = (hidden_in, cell_in) if begin else (hidden, cell)
+        advance(table, forcing_ref.at[now], *old, hidden, cell, row, chunk=chunk)
+    if last:
+        end = jnp.dot(table[gates : gates + PAD, 0:state], hidden[...], preferred_element_type=jnp.float32)
+        now = first + count
+        head_sum[now - 1 : now, :] = end[0:1] + end[1:2] + end[2:3]
+        runoff_ref[...] = jax.nn.softplus(head_sum[...]).astype(jnp.bfloat16)
+    for copy in copies:
         copy.wait()
 
 
@@ -235,8 +252,9 @@
         pieces = [slots[at * reach_blocks + blk] for blk in range(reach_blocks)]
         tile = jnp.concatenate([piece[0:steps] for piece in pieces], axis=0)
         out_ref[pl.ds((at - base) * rows, rows), :] = tile.astype(jnp.bfloat16)
-        section = slot_of(at, size) ^ me
-        share = share_ref[section]
+        relative = slot_of(at, size)
+        section = relative ^ me
+        share = share_ref[relative]
         total = pieces[0] * share[0:1]
         for blk in range(1, reach_blocks):
             total = total + pieces[blk] * share[blk : blk + 1]
@@ -363,7 +381,7 @@
 
     share = pl.pallas_call(
         functools.partial(prep_kernel, size=size),
-        out_shape=jax.ShapeDtypeStruct((size, PAD, block), jnp.float32),
+        out_shape=pltpu.VMEM((PAD, block), jnp.float32),
         in_specs=[HBM] * 3,
         out_specs=VMEM,
         scratch_shapes=[
@@ -375,40 +393,52 @@
         compiler_params=params,
         name="prep",
     )(*in_hbm(block_count, route_kernel, carry_gain))
-    shares = lax.all_to_all(share, "basin", split_axis=0, concat_axis=0, tiled=True)
-    runoff, weight_v, route_v, gain_v, given = pl.pallas_call(
-        functools.partial(lstm_kernel, chunk=256),
+    shares = share[None]
+    order = []
+    for bit in stage_bits(size):
+        other = lax.ppermute(shares, "basin", [(i, i ^ (1 << bit)) for i in range(size)])
+        order.append(other)
+        shares = jnp.concatenate([shares, other], axis=0)
+
+    chunk = 256
+    parts = 4
+    bounds = [0] + [1 + (steps - 1) * part // (parts - 1) for part in range(parts)]
+    carried = (
+        pltpu.VMEM((state, units), jnp.bfloat16),
+        pltpu.VMEM((state, units), jnp.float32),
+        pltpu.VMEM((PAD, units), jnp.float32),
+    )
+
+    def cost(count):
+        return pl.CostEstimate(
+            flops=2 * count * gates * (state + features) * units,
+            bytes_accessed=4 << 20,
+            transcendentals=5 * count * state * units,
+        )
+
+    forcing_v, table, hidden, cell, head_sum, given = pl.pallas_call(
+        functools.partial(first_kernel, count=bounds[1], chunk=chunk),
         out_shape=(
-            pltpu.VMEM((PAD, units), jnp.bfloat16),
-            like(remap_weight),
-            like(route_kernel),
-            like(carry_gain),
+            like(forcing),
+            pltpu.VMEM((gates + PAD, 2 * state), jnp.bfloat16),
+            *carried,
             pltpu.VMEM((size, block), jnp.float32),
         ),
-        in_specs=[HBM] * 11,
-        out_specs=(VMEM,) * 5,
+        in_specs=[HBM] * 8,
+        out_specs=(VMEM,) * 6,
         scratch_shapes=[
             pltpu.VMEM((gates, state), jnp.bfloat16),
             pltpu.VMEM((features, gates), jnp.bfloat16),
             pltpu.VMEM((1, gates), jnp.float32),
             pltpu.VMEM((1, state), jnp.float32),
-            pltpu.VMEM((state, units), jnp.bfloat16),
-            pltpu.VMEM((state, units), jnp.float32),
             pltpu.VMEM(release.shape, jnp.float32),
-            pltpu.VMEM((steps, features, units), jnp.bfloat16),
-            pltpu.VMEM((gates + PAD, 2 * state), jnp.bfloat16),
-            pltpu.VMEM((PAD, units), jnp.float32),
             pltpu.VMEM((block, block), jnp.float32),
             pltpu.SemaphoreType.DMA((steps,)),
-            pltpu.SemaphoreType.DMA((10,)),
+            pltpu.SemaphoreType.DMA((7,)),
         ],
         compiler_params=params,
-        cost_estimate=pl.CostEstimate(
-            flops=2 * steps * gates * (state + features) * units,
-            bytes_accessed=4 << 20,
-            transcendentals=5 * steps * state * units,
-        ),
-        name="lstm",
+        cost_estimate=cost(bounds[1]),
+        name="lstm0",
     )(
         *in_hbm(
             w_recur,
@@ -419,11 +449,39 @@
             cell_init,
             release,
             forcing,
-            remap_weight,
-            route_kernel,
-            carry_gain,
         )
     )
+    for part in range(1, parts):
+        last = part == parts - 1
+        fetch = {1: (route_kernel, carry_gain), parts - 1: (remap_weight,)}.get(part, ())
+        results = (pltpu.VMEM((PAD, units), jnp.bfloat16),) if last else carried
+        outs = pl.pallas_call(
+            functools.partial(
+                later_kernel,
+                first=bounds[part],
+                count=bounds[part + 1] - bounds[part],
+                last=last,
+                fetched=len(fetch),
+                chunk=chunk,
+            ),
+            out_shape=results + tuple(like(x) for x in fetch),
+            in_specs=[VMEM] * 5 + [pl.BlockSpec(memory_space=pl.ANY)] + [HBM] * len(fetch),
+            out_specs=(VMEM,) * (len(results) + len(fetch)),
+            scratch_shapes=(list(carried) if last else []) + [pltpu.SemaphoreType.DMA((max(1, len(fetch)),))],
+            compiler_params=params,
+            cost_estimate=cost(bounds[part + 1] - bounds[part]),
+            name=f"lstm{part}",
+        )(
+            *in_vmem(forcing_v, table, hidden, cell, head_sum),
+            order[min(part, len(order)) - 1],
+            *in_hbm(*fetch),
+        )
+        if part == 1:
+            route_v, gain_v = outs[len(results) :]
+        if last:
+            runoff, weight_v = outs
+        else:
+            hidden, cell, head_sum = outs[:3]
     keep, send, shift = pl.pallas_call(
         functools.partial(remap_kernel, size=size, reach_blocks=reach_blocks, steps=steps),
         out_shape=(

time: 40.4 us -> 39.4 us (0.975)
  Pallas kernels: 13.7 us -> 12.2 us
  starting transfers between devices: 15.4 us -> 16.3 us
    ppermute x0 -> x4, starting transfers between devices: none -> 8.26 us  [shards(): lax.ppermute(shares, 'basin', [(i, i ^ 1 << bit) for i in range(size)])]
    all_to_all x1 -> x0, starting transfers between devices: 7.4 us -> none  [shards(): lax.all_to_all(share, 'basin', split_axis=0, concat_axis=0, tiled=True)]
    pallas_call x2 -> x5, Pallas kernels: 9.8 us -> 8.26 us  [the longest x3 5.09 us: shards(): pl.pallas_call(functools.partial(later_kernel, first=bounds[part], count=...]
    ppermute x2, waiting for transfers between devices: 4.42 us -> 3.42 us  [shards(): others.append(lax.ppermute(shift, AXES, route))]
    ppermute x0 -> x4, waiting for transfers between devices: none -> 0.72 us  [shards(): lax.ppermute(shares, 'basin', [(i, i ^ 1 << bit) for i in range(size)])]
  transfers between devices with their start and end apart: 7 -> 10, of which waited for: 5 -> 8; matrix products, arithmetic and copies ran while one was open for 0% -> 0% of each run, Pallas kernels for 20% -> 19%
where the time goes in v3:
time: 39.4 us; the launch traced here: 39.2 us
  starting transfers between devices  16.3 us (41%)
  Pallas kernels  12.2 us (31%)
  waiting for transfers between devices  10.3 us (26%)
    ppermute x4, starting transfers between devices, shards(): lax.ppermute(shares, 'basin', [(i, i ^ 1 << bit) for i in range(size)])  8.26 us
    ppermute x4, starting transfers between devices, shards(): got = lax.ppermute(send, 'basin', [(i, i ^ swap) for i in range(size)])  6.39 us
    ppermute x4, waiting for transfers between devices, shards(): got = lax.ppermute(send, 'basin', [(i, i ^ swap) for i in range(size)])  6.12 us
    pallas_call x3, Pallas kernels, shards(): pl.pallas_call(functools.partial(later_kernel, first=bounds[part], count=...  5.09 us
    ppermute x2, waiting for transfers between devices, shards(): others.append(lax.ppermute(shift, AXES, route))  3.42 us
    pallas_call x1, Pallas kernels, shards(): pl.pallas_call(functools.partial(first_kernel, count=bounds[1], chunk=chu...  2.26 us
    pallas_call x1, Pallas kernels, shards(): pl.pallas_call(functools.partial(finish_kernel, steps=steps, unit_size=un...  2.19 us
    pallas_call x1, Pallas kernels, shards(): pl.pallas_call(functools.partial(remap_kernel, size=size, reach_blocks=re...  1.71 us
  transfers between devices with their start and end apart: 10, of which 8 were waited for; matrix products, arithmetic and copies ran while one was open for 0% of the time, Pallas kernels for 19%

profile of v3, /device:TPU:0, one launch (start us, length us, event | category | flops | bytes accessed | tf_op | source)
XLA Modules:
  0.0 39.2 jit_solution(174897137426679605)
XLA Ops:
  0.0 0.9 %prep.1 = f32[16,128]{1,0:T(8,128)S(1)} custom-call(s32[16]{0:T(128)} %count_ref.1, f32[8,128,128]{2,1,0:T(8,128)} %refs_6_.2, f32[8,128]{1,0:T(8,128)} %refs_7_.1), custom_call_target="tpu_custom_call" | custom-call | tf_op jit(solution)/shard_map/prep/pallas_call | solution.py:382
  0.9 0.5 %collective-permute-start = (f32[1,16,128]{2,1,0:T(8,128)S(1)}, f32[1,16,128]{2,1,0:T(8,128)S(1)}, u32[]{:S(2)}, u32[]{:S(2)}) collective-permute-start(f32[1,16,128]{2,1,0:T(8,128)S(1)} %bitcast.5), channel_id=1, source_target_pairs={{0,2},{2,0},{4,6},{6,4},{8,10},{10,8},{12,14},{14,12},{16,18},{18,... | collective-permute-start | bytes 24584 | tf_op jit(solution)/shard_map/ppermute | solution.py:399
  1.4 2.3 %lstm0.1 = (bf16[12,32,1024]{2,1,0:T(8,128)(2,1)S(1)}, bf16[528,256]{1,0:T(8,128)(2,1)S(1)}, bf16[128,1024]{1,0:T(8,128)(2,1)S(1)}, f32[128,1024]{1,0:T(8,128)S(...) custom-call(bf16[512,128]{1,0:T(8,128)(2,1)} %w_recur_hbm.1, bf16[32,512]{1,0:T(8,128)(2,1)} %bitcast.9, ...), custom_call_target="tpu_custom_call" | custom-call | flops 167772160 | bytes 4194304 | tf_op jit(solution)/shard_map/lstm0/pallas_call | solution.py:419
  3.7 0.0 collective-permute-done.refs_5_
  3.7 2.6 %collective-permute-start.1 = (f32[2,16,128]{2,1,0:T(8,128)S(1)}, f32[2,16,128]{2,1,0:T(8,128)S(1)}, u32[]{:S(2)}, u32[]{:S(2)}) collective-permute-start(f32[2,16,128]{2,1,0:T(8,128)S(1)} %pad_maximum_fusion.5), channel_id=1, source_target_pairs={{0,4},{2,6},{4,0},{6,2},{8,12},{10,14},{12,8},{14,10},{16,20},{18,... | collective-permute-start | bytes 49160 | tf_op jit(solution)/shard_map/ppermute | solution.py:399
  6.3 1.4 %lstm1.1 = (bf16[128,1024]{1,0:T(8,128)(2,1)S(1)}, f32[128,1024]{1,0:T(8,128)S(1)}, f32[16,1024]{1,0:T(8,128)S(1)}, f32[8,128,128]{2,1,0:T(8,128)S(1)}, f32[8,128]{1,0:T(8,128)S(1)}) custom-call(bf16[12,32,1024]{2,1,0:T(8,128)(2,1)S(1)} %get-tuple-element.25.refs_0_, bf16[528,256]{1,0:T(8,128)(2,1)S(1)} %get-tuple-element.26.refs_1_, ...), custom_call_target="tpu_custom_call" | custom-call | flops 503316480 | bytes 4194304 | tf_op jit(solution)/shard_map/lstm1/pallas_call | solution.py:458
  7.7 0.3 collective-permute-done.1.refs_5_
  8.1 2.1 %collective-permute-start.2 = (f32[4,16,128]{2,1,0:T(8,128)S(1)}, f32[4,16,128]{2,1,0:T(8,128)S(1)}, u32[]{:S(2)}, u32[]{:S(2)}) collective-permute-start(f32[4,16,128]{2,1,0:T(8,128)S(1)} %pad_maximum_fusion.3), channel_id=1, source_target_pairs={{0,8},{2,10},{4,12},{6,14},{8,0},{10,2},{12,4},{14,6},{16,24},{18,... | collective-permute-start | bytes 98312 | tf_op jit(solution)/shard_map/ppermute | solution.py:399
  10.2 1.8 %lstm2.1 = (bf16[128,1024]{1,0:T(8,128)(2,1)S(1)}, f32[128,1024]{1,0:T(8,128)S(1)}, f32[16,1024]{1,0:T(8,128)S(1)}) custom-call(bf16[12,32,1024]{2,1,0:T(8,128)(2,1)S(1)} %get-tuple-element.25.refs_0_, bf16[528,256]{1,0:T(8,128)(2,1)S(1)} %get-tuple-element.26.refs_1_, bf16[128,1024]{1,0:T(8,128)(2,1)S(1)} %get-tuple-element.30.refs_2_, ...), custom_call_target="tpu_custom_call" | custom-call | flops 671088640 | bytes 4194304 | tf_op jit(solution)/shard_map/lstm2/pallas_call | solution.py:458
  12.0 0.1 collective-permute-done.2.refs_5_
  12.1 3.0 %collective-permute-start.3 = (f32[8,16,128]{2,1,0:T(8,128)S(1)}, f32[8,16,128]{2,1,0:T(8,128)S(1)}, u32[]{:S(2)}, u32[]{:S(2)}) collective-permute-start(f32[8,16,128]{2,1,0:T(8,128)S(1)} %pad_maximum_fusion.1), channel_id=1, source_target_pairs={{0,16},{2,18},{4,20},{6,22},{8,24},{10,26},{12,28},{14,30},{16,0},... | collective-permute-start | bytes 196616 | tf_op jit(solution)/shard_map/ppermute | solution.py:399
  15.1 1.9 %lstm3.1 = (bf16[16,1024]{1,0:T(8,128)(2,1)S(1)}, bf16[8,8,128,128]{3,2,1,0:T(8,128)(2,1)S(1)}) custom-call(bf16[12,32,1024]{2,1,0:T(8,128)(2,1)S(1)} %get-tuple-element.25.refs_0_, bf16[528,256]{1,0:T(8,128)(2,1)S(1)} %get-tuple-element.26.refs_1_, bf16[128,1024]{1,0:T(8,128)(2,1)S(1)} %get-tuple-element.33.refs_2_, ...), custom_call_target="tpu_custom_call" | custom-call | flops 671088640 | bytes 4194304 | tf_op jit(solution)/shard_map/lstm3/pallas_call | solution.py:458
  17.0 0.3 collective-permute-done.3
  17.3 0.0 copy-done
  17.4 0.0 copy-start.2
  17.4 0.0 copy-start.3
  17.4 0.0 copy-start.4
  17.4 1.7 %remap.1 = (bf16[768,128]{1,0:T(8,128)(2,1)S(1)}, bf16[800,128]{1,0:T(8,128)(2,1)S(1)}, f32[16,128]{1,0:T(8,128)S(1)}) custom-call(s32[8,8]{1,0:T(8,128)S(1)} %copy-done, s32[8,8]{1,0:T(8,128)S(1)} %copy-done.1, bf16[16,1024]{1,0:T(8,128)(2,1)S(1)} %get-tuple-element.36.runoff_ref, bf16[8,8,128,128]{3,2,1,0:T(8,128)(2,1)S(1)} %get-tuple-element.37.weight_ref, ...), custom_call_target="tpu_custom_call" | custom-call | tf_op jit(solution)/shard_map/remap/pallas_call | solution.py:485
  19.1 0.1 collective-permute-start.4
  19.2 1.4 %collective-permute-done.4 = bf16[800,128]{1,0:T(8,128)(2,1)S(1)} collective-permute-done((bf16[800,128]{1,0:T(8,128)(2,1)S(1)}, bf16[800,128]{1,0:T(8,128)(2,1)S(1)}, u32[]{:S(2)}, u32[]{:S(2)}) %collective-permute-start.4) | collective-permute-done | bytes 204832 | tf_op jit(solution)/shard_map/ppermute | solution.py:514
  20.6 0.1 add_convert_fusion
  20.7 1.9 %collective-permute-start.5 = (bf16[416,128]{1,0:T(8,128)(2,1)S(1)}, bf16[416,128]{1,0:T(8,128)(2,1)S(1)}, u32[]{:S(2)}, u32[]{:S(2)}) collective-permute-start(bf16[416,128]{1,0:T(8,128)(2,1)S(1)} %pad_maximum_fusion), channel_id=1, source_target_pairs={{0,4},{2,6},{4,0},{6,2},{8,12},{10,14},{12,8},{14,10},{16,20},{18,... | collective-permute-start | bytes 319496 | tf_op jit(solution)/shard_map/ppermute | solution.py:514
  22.6 1.4 %collective-permute-start.7 = (f32[16,128]{1,0:T(8,128)S(1)}, f32[16,128]{1,0:T(8,128)S(1)}, u32[]{:S(2)}, u32[]{:S(2)}) collective-permute-start(f32[16,128]{1,0:T(8,128)S(1)} %get-tuple-element.48), channel_id=1, source_target_pairs={{0,5},{1,4},{2,7},{3,6},{4,1},{5,0},{6,3},{7,2},{8,13},{9,12},{10,... | collective-permute-start | bytes 24584 | tf_op jit(solution)/shard_map/ppermute | solution.py:524
  24.0 0.2 collective-permute-start.6
  24.3 2.9 %collective-permute-done.7 = f32[16,128]{1,0:T(8,128)S(1)} collective-permute-done((f32[16,128]{1,0:T(8,128)S(1)}, f32[16,128]{1,0:T(8,128)S(1)}, u32[]{:S(2)}, u32[]{:S(2)}) %collective-permute-start.7) | collective-permute-done | bytes 8224 | tf_op jit(solution)/shard_map/ppermute | solution.py:524
  27.2 0.5 %collective-permute-done.6 = f32[16,128]{1,0:T(8,128)S(1)} collective-permute-done((f32[16,128]{1,0:T(8,128)S(1)}, f32[16,128]{1,0:T(8,128)S(1)}, u32[]{:S(2)}, u32[]{:S(2)}) %collective-permute-start.6) | collective-permute-done | bytes 8224 | tf_op jit(solution)/shard_map/ppermute | solution.py:524
  27.7 0.0 collective-permute-done.5
  27.8 1.6 %collective-permute-start.8 = (bf16[224,128]{1,0:T(8,128)(2,1)S(1)}, bf16[224,128]{1,0:T(8,128)(2,1)S(1)}, u32[]{:S(2)}, u32[]{:S(2)}) collective-permute-start(bf16[224,128]{1,0:T(8,128)(2,1)S(1)} %pad_maximum_fusion.2), channel_id=1, source_target_pairs={{0,8},{2,10},{4,12},{6,14},{8,0},{10,2},{12,4},{14,6},{16,24},{18,... | collective-permute-start | bytes 172040 | tf_op jit(solution)/shard_map/ppermute | solution.py:514
  29.4 2.6 %collective-permute-done.8 = bf16[224,128]{1,0:T(8,128)(2,1)S(1)} collective-permute-done((bf16[224,128]{1,0:T(8,128)(2,1)S(1)}, bf16[224,128]{1,0:T(8,128)(2,1)S(1)}, u32[]{:S(2)}, u32[]{:S(2)}) %collective-permute-start.8) | collective-permute-done | bytes 57376 | tf_op jit(solution)/shard_map/ppermute | solution.py:514
  32.1 2.8 %collective-permute-start.9 = (bf16[128,128]{1,0:T(8,128)(2,1)S(1)}, bf16[128,128]{1,0:T(8,128)(2,1)S(1)}, u32[]{:S(2)}, u32[]{:S(2)}) collective-permute-start(bf16[128,128]{1,0:T(8,128)(2,1)S(1)} %pad_maximum_fusion.4), channel_id=1, source_target_pairs={{0,16},{2,18},{4,20},{6,22},{8,24},{10,26},{12,28},{14,30},{16,0},... | collective-permute-start | bytes 98312 | tf_op jit(solution)/shard_map/ppermute | solution.py:514
  34.9 2.1 %collective-permute-done.9.got_ref = bf16[128,128]{1,0:T(8,128)(2,1)S(1)} collective-permute-done((bf16[128,128]{1,0:T(8,128)(2,1)S(1)}, bf16[128,128]{1,0:T(8,128)(2,1)S(1)}, u32[]{:S(2)}, u32[]{:S(2)}) %collective-permute-start.9) | collective-permute-done | bytes 32800 | tf_op jit(solution)/shard_map/ppermute | solution.py:514
  37.0 2.2 %finish.1 = f32[12,1024]{1,0:T(8,128)} custom-call(s32[16]{0:T(128)S(1)} %copy-done.2, s32[16]{0:T(128)S(1)} %copy-done.3, s32[16]{0:T(128)S(1)} %copy-done.4, f32[16,128]{1,0:T(8,128)S(1)} %get-tuple-element.24.given_ref, f32[16,128]{1,0:T(8,128)S(1)} %get-tuple-element.44.shift_ref, bf16[96,128]{1,0:T(8,128)(2,1)S(1)} %get-tuple-element.50.mine_ref, ...), custom_call_target="tpu_custom_call" | custom-call | tf_op jit(solution)/shard_map/finish/pallas_call | solution.py:527
  (28 shorter events, 0.2 us)
Async XLA Ops:
  0.9 2.8 %collective-permute-start = (f32[1,16,128]{2,1,0:T(8,128)S(1)}, f32[1,16,128]{2,1,0:T(8,128)S(1)}, u32[]{:S(2)}, u32[]{:S(2)}) collective-permute-start(f32[1,16,128]{2,1,0:T(8,128)S(1)} %bitcast.5), channel_id=1, source_target_pairs={{0,2},{2,0},{4,6},{6,4},{8,10},{10,8},{12,14},{14,12},{16,18},{18,... | collective-permute-start | bytes 24584 | tf_op jit(solution)/shard_map/ppermute | solution.py:399
  3.7 4.3 %collective-permute-start.1 = (f32[2,16,128]{2,1,0:T(8,128)S(1)}, f32[2,16,128]{2,1,0:T(8,128)S(1)}, u32[]{:S(2)}, u32[]{:S(2)}) collective-permute-start(f32[2,16,128]{2,1,0:T(8,128)S(1)} %pad_maximum_fusion.5), channel_id=1, source_target_pairs={{0,4},{2,6},{4,0},{6,2},{8,12},{10,14},{12,8},{14,10},{16,20},{18,... | collective-permute-start | bytes 49160 | tf_op jit(solution)/shard_map/ppermute | solution.py:399
  8.1 4.0 %collective-permute-start.2 = (f32[4,16,128]{2,1,0:T(8,128)S(1)}, f32[4,16,128]{2,1,0:T(8,128)S(1)}, u32[]{:S(2)}, u32[]{:S(2)}) collective-permute-start(f32[4,16,128]{2,1,0:T(8,128)S(1)} %pad_maximum_fusion.3), channel_id=1, source_target_pairs={{0,8},{2,10},{4,12},{6,14},{8,0},{10,2},{12,4},{14,6},{16,24},{18,... | collective-permute-start | bytes 98312 | tf_op jit(solution)/shard_map/ppermute | solution.py:399
  12.1 5.3 %collective-permute-start.3 = (f32[8,16,128]{2,1,0:T(8,128)S(1)}, f32[8,16,128]{2,1,0:T(8,128)S(1)}, u32[]{:S(2)}, u32[]{:S(2)}) collective-permute-start(f32[8,16,128]{2,1,0:T(8,128)S(1)} %pad_maximum_fusion.1), channel_id=1, source_target_pairs={{0,16},{2,18},{4,20},{6,22},{8,24},{10,26},{12,28},{14,30},{16,0},... | collective-permute-start | bytes 196616 | tf_op jit(solution)/shard_map/ppermute | solution.py:399
  15.1 2.2 %copy-start = (s32[8,8]{1,0:T(8,128)S(1)}, s32[8,8]{1,0:T(8,128)}, u32[]{:S(2)}) copy-start(s32[8,8]{1,0:T(8,128)} %dest_ref.1) | copy-start | bytes 772
  15.1 2.2 %copy-start.1 = (s32[8,8]{1,0:T(8,128)S(1)}, s32[8,8]{1,0:T(8,128)}, u32[]{:S(2)}) copy-start(s32[8,8]{1,0:T(8,128)} %block_ref.1) | copy-start | bytes 772
  17.4 19.6 %copy-start.2 = (s32[16]{0:T(128)S(1)}, s32[16]{0:T(128)}, u32[]{:S(2)}) copy-start(s32[16]{0:T(128)} %count_ref.1) | copy-start | bytes 196
  17.4 19.6 %copy-start.3 = (s32[16]{0:T(128)S(1)}, s32[16]{0:T(128)}, u32[]{:S(2)}) copy-start(s32[16]{0:T(128)} %parent_ref.1) | copy-start | bytes 196
  17.4 19.6 %copy-start.4 = (s32[16]{0:T(128)S(1)}, s32[16]{0:T(128)}, u32[]{:S(2)}) copy-start(s32[16]{0:T(128)} %reservoir_ref.1) | copy-start | bytes 196
  19.1 1.5 %collective-permute-start.4 = (bf16[800,128]{1,0:T(8,128)(2,1)S(1)}, bf16[800,128]{1,0:T(8,128)(2,1)S(1)}, u32[]{:S(2)}, u32[]{:S(2)}) collective-permute-start(bf16[800,128]{1,0:T(8,128)(2,1)S(1)} %get-tuple-element.39), channel_id=1, source_target_pairs={{0,2},{2,0},{4,6},{6,4},{8,10},{10,8},{12,14},{14,12},{16,18},{18,... | collective-permute-start | bytes 614408 | tf_op jit(solution)/shard_map/ppermute | solution.py:514
  20.7 7.0 %collective-permute-start.5 = (bf16[416,128]{1,0:T(8,128)(2,1)S(1)}, bf16[416,128]{1,0:T(8,128)(2,1)S(1)}, u32[]{:S(2)}, u32[]{:S(2)}) collective-permute-start(bf16[416,128]{1,0:T(8,128)(2,1)S(1)} %pad_maximum_fusion), channel_id=1, source_target_pairs={{0,4},{2,6},{4,0},{6,2},{8,12},{10,14},{12,8},{14,10},{16,20},{18,... | collective-permute-start | bytes 319496 | tf_op jit(solution)/shard_map/ppermute | solution.py:514
  22.6 4.5 %collective-permute-start.7 = (f32[16,128]{1,0:T(8,128)S(1)}, f32[16,128]{1,0:T(8,128)S(1)}, u32[]{:S(2)}, u32[]{:S(2)}) collective-permute-start(f32[16,128]{1,0:T(8,128)S(1)} %get-tuple-element.48), channel_id=1, source_target_pairs={{0,5},{1,4},{2,7},{3,6},{4,1},{5,0},{6,3},{7,2},{8,13},{9,12},{10,... | collective-permute-start | bytes 24584 | tf_op jit(solution)/shard_map/ppermute | solution.py:524
  24.0 3.7 %collective-permute-start.6 = (f32[16,128]{1,0:T(8,128)S(1)}, f32[16,128]{1,0:T(8,128)S(1)}, u32[]{:S(2)}, u32[]{:S(2)}) collective-permute-start(f32[16,128]{1,0:T(8,128)S(1)} %get-tuple-element.48), channel_id=1, source_target_pairs={{0,1},{1,0},{2,3},{3,2},{4,5},{5,4},{6,7},{7,6},{8,9},{9,8},{10,11... | collective-permute-start | bytes 24584 | tf_op jit(solution)/shard_map/ppermute | solution.py:524
  27.8 4.2 %collective-permute-start.8 = (bf16[224,128]{1,0:T(8,128)(2,1)S(1)}, bf16[224,128]{1,0:T(8,128)(2,1)S(1)}, u32[]{:S(2)}, u32[]{:S(2)}) collective-permute-start(bf16[224,128]{1,0:T(8,128)(2,1)S(1)} %pad_maximum_fusion.2), channel_id=1, source_target_pairs={{0,8},{2,10},{4,12},{6,14},{8,0},{10,2},{12,4},{14,6},{16,24},{18,... | collective-permute-start | bytes 172040 | tf_op jit(solution)/shard_map/ppermute | solution.py:514
  32.1 4.9 %collective-permute-start.9 = (bf16[128,128]{1,0:T(8,128)(2,1)S(1)}, bf16[128,128]{1,0:T(8,128)(2,1)S(1)}, u32[]{:S(2)}, u32[]{:S(2)}) collective-permute-start(bf16[128,128]{1,0:T(8,128)(2,1)S(1)} %pad_maximum_fusion.4), channel_id=1, source_target_pairs={{0,16},{2,18},{4,20},{6,22},{8,24},{10,26},{12,28},{14,30},{16,0},... | collective-permute-start | bytes 98312 | tf_op jit(solution)/shard_map/ppermute | solution.py:514

commit v4 on v3

--- a/solution.py
+++ b/solution.py
@@ -27,11 +27,25 @@
     return range(size.bit_length() - 1)
 
 
+def gather_bits(size):
+    bits = list(range(size.bit_length() - 1))
+    return bits[1:] + bits[:1]
+
+
+def place_of(relative, size):
+    return sum(((relative >> bit) & 1) << at for at, bit in enumerate(gather_bits(size)))
+
+
 def slot_of(relative, size):
     slot = relative * 0
     for bit in stage_bits(size):
         slot = slot * 2 + ((relative >> bit) & 1)
     return slot
+
+
+def relative_of(slot, size):
+    bits = list(stage_bits(size))
+    return sum(((slot >> (len(bits) - 1 - at)) & 1) << bit for at, bit in enumerate(bits))
 
 
 def split3(x):
@@ -252,9 +266,9 @@
         pieces = [slots[at * reach_blocks + blk] for blk in range(reach_blocks)]
         tile = jnp.concatenate([piece[0:steps] for piece in pieces], axis=0)
         out_ref[pl.ds((at - base) * rows, rows), :] = tile.astype(jnp.bfloat16)
-        relative = slot_of(at, size)
+        relative = relative_of(at, size)
         section = relative ^ me
-        share = share_ref[relative]
+        share = share_ref[place_of(relative, size)]
         total = pieces[0] * share[0:1]
         for blk in range(1, reach_blocks):
             total = total + pieces[blk] * share[blk : blk + 1]
@@ -395,14 +409,14 @@
     )(*in_hbm(block_count, route_kernel, carry_gain))
     shares = share[None]
     order = []
-    for bit in stage_bits(size):
+    for bit in gather_bits(size):
         other = lax.ppermute(shares, "basin", [(i, i ^ (1 << bit)) for i in range(size)])
         order.append(other)
         shares = jnp.concatenate([shares, other], axis=0)
 
     chunk = 256
     parts = 4
-    bounds = [0] + [1 + (steps - 1) * part // (parts - 1) for part in range(parts)]
+    bounds = [0, 1, 6, 11, 12]
     carried = (
         pltpu.VMEM((state, units), jnp.bfloat16),
         pltpu.VMEM((state, units), jnp.float32),

time: 39.4 us -> 38.8 us (0.985)
  waiting for transfers between devices: 10.3 us -> 9.26 us
  Pallas kernels: 12.2 us -> 13.2 us
  starting transfers between devices: 16.3 us -> 15.6 us
    pallas_call x3, Pallas kernels: 5.09 us -> 6.14 us  [shards(): pl.pallas_call(functools.partial(later_kernel, first=bounds[part], count=...]
    ppermute x4, starting transfers between devices: 8.26 us -> 7.4 us  [shards(): lax.ppermute(shares, 'basin', [(i, i ^ 1 << bit) for i in range(size)])]
    ppermute x4, waiting for transfers between devices: 0.72 us -> 0.01 us  [shards(): lax.ppermute(shares, 'basin', [(i, i ^ 1 << bit) for i in range(size)])]
    ppermute x2, starting transfers between devices: 1.66 us -> 2.19 us  [shards(): others.append(lax.ppermute(shift, AXES, route))]
    ppermute x4, starting transfers between devices: 6.39 us -> 5.99 us  [shards(): got = lax.ppermute(send, 'basin', [(i, i ^ swap) for i in range(size)])]
  transfers between devices with their start and end apart: 10 -> 10, of which waited for: 8 -> 5; matrix products, arithmetic and copies ran while one was open for 0% -> 0% of each run, Pallas kernels for 19% -> 22%
where the time goes in v4:
time: 38.8 us; the launch traced here: 38.6 us
  starting transfers between devices  15.6 us (40%)
  Pallas kernels  13.2 us (34%)
  waiting for transfers between devices  9.26 us (24%)
    ppermute x4, starting transfers between devices, shards(): lax.ppermute(shares, 'basin', [(i, i ^ 1 << bit) for i in range(size)])  7.4 us
    pallas_call x3, Pallas kernels, shards(): pl.pallas_call(functools.partial(later_kernel, first=bounds[part], count=...  6.14 us
    ppermute x4, waiting for transfers between devices, shards(): got = lax.ppermute(send, 'basin', [(i, i ^ swap) for i in range(size)])  6.13 us
    ppermute x4, starting transfers between devices, shards(): got = lax.ppermute(send, 'basin', [(i, i ^ swap) for i in range(size)])  5.99 us
    ppermute x2, waiting for transfers between devices, shards(): others.append(lax.ppermute(shift, AXES, route))  3.12 us
    pallas_call x1, Pallas kernels, shards(): pl.pallas_call(functools.partial(first_kernel, count=bounds[1], chunk=chu...  2.26 us
    pallas_call x1, Pallas kernels, shards(): pl.pallas_call(functools.partial(finish_kernel, steps=steps, unit_size=un...  2.19 us
    ppermute x2, starting transfers between devices, shards(): others.append(lax.ppermute(shift, AXES, route))  2.19 us
  transfers between devices with their start and end apart: 10, of which 5 were waited for; matrix products, arithmetic and copies ran while one was open for 0% of the time, Pallas kernels for 22%

profile of v4, /device:TPU:0, one launch (start us, length us, event | category | flops | bytes accessed | tf_op | source)
XLA Modules:
  0.0 38.6 jit_solution(6126131220563549468)
XLA Ops:
  0.0 0.9 %prep.1 = f32[16,128]{1,0:T(8,128)S(1)} custom-call(s32[16]{0:T(128)} %count_ref.1, f32[8,128,128]{2,1,0:T(8,128)} %refs_6_.2, f32[8,128]{1,0:T(8,128)} %refs_7_.1), custom_call_target="tpu_custom_call" | custom-call | tf_op jit(solution)/shard_map/prep/pallas_call | solution.py:396
  0.9 3.0 %collective-permute-start = (f32[1,16,128]{2,1,0:T(8,128)S(1)}, f32[1,16,128]{2,1,0:T(8,128)S(1)}, u32[]{:S(2)}, u32[]{:S(2)}) collective-permute-start(f32[1,16,128]{2,1,0:T(8,128)S(1)} %bitcast.5), channel_id=1, source_target_pairs={{0,4},{2,6},{4,0},{6,2},{8,12},{10,14},{12,8},{14,10},{16,20},{18,... | collective-permute-start | bytes 24584 | tf_op jit(solution)/shard_map/ppermute | solution.py:413
  3.9 2.3 %lstm0.1 = (bf16[12,32,1024]{2,1,0:T(8,128)(2,1)S(1)}, bf16[528,256]{1,0:T(8,128)(2,1)S(1)}, bf16[128,1024]{1,0:T(8,128)(2,1)S(1)}, f32[128,1024]{1,0:T(8,128)S(...) custom-call(bf16[512,128]{1,0:T(8,128)(2,1)} %w_recur_hbm.1, bf16[32,512]{1,0:T(8,128)(2,1)} %bitcast.9, ...), custom_call_target="tpu_custom_call" | custom-call | flops 167772160 | bytes 4194304 | tf_op jit(solution)/shard_map/lstm0/pallas_call | solution.py:433
  6.2 0.0 collective-permute-done.refs_5_
  6.2 1.6 %collective-permute-start.1 = (f32[2,16,128]{2,1,0:T(8,128)S(1)}, f32[2,16,128]{2,1,0:T(8,128)S(1)}, u32[]{:S(2)}, u32[]{:S(2)}) collective-permute-start(f32[2,16,128]{2,1,0:T(8,128)S(1)} %pad_maximum_fusion.5), channel_id=1, source_target_pairs={{0,8},{2,10},{4,12},{6,14},{8,0},{10,2},{12,4},{14,6},{16,24},{18,... | collective-permute-start | bytes 49160 | tf_op jit(solution)/shard_map/ppermute | solution.py:413
  7.9 2.3 %lstm1.1 = (bf16[128,1024]{1,0:T(8,128)(2,1)S(1)}, f32[128,1024]{1,0:T(8,128)S(1)}, f32[16,1024]{1,0:T(8,128)S(1)}, f32[8,128,128]{2,1,0:T(8,128)S(1)}, f32[8,128]{1,0:T(8,128)S(1)}) custom-call(bf16[12,32,1024]{2,1,0:T(8,128)(2,1)S(1)} %get-tuple-element.25.refs_0_, bf16[528,256]{1,0:T(8,128)(2,1)S(1)} %get-tuple-element.26.refs_1_, ...), custom_call_target="tpu_custom_call" | custom-call | flops 838860800 | bytes 4194304 | tf_op jit(solution)/shard_map/lstm1/pallas_call | solution.py:472
  10.2 2.7 %collective-permute-start.2 = (f32[4,16,128]{2,1,0:T(8,128)S(1)}, f32[4,16,128]{2,1,0:T(8,128)S(1)}, u32[]{:S(2)}, u32[]{:S(2)}) collective-permute-start(f32[4,16,128]{2,1,0:T(8,128)S(1)} %pad_maximum_fusion.3), channel_id=1, source_target_pairs={{0,16},{2,18},{4,20},{6,22},{8,24},{10,26},{12,28},{14,30},{16,0},... | collective-permute-start | bytes 98312 | tf_op jit(solution)/shard_map/ppermute | solution.py:413
  12.8 2.3 %lstm2.1 = (bf16[128,1024]{1,0:T(8,128)(2,1)S(1)}, f32[128,1024]{1,0:T(8,128)S(1)}, f32[16,1024]{1,0:T(8,128)S(1)}) custom-call(bf16[12,32,1024]{2,1,0:T(8,128)(2,1)S(1)} %get-tuple-element.25.refs_0_, bf16[528,256]{1,0:T(8,128)(2,1)S(1)} %get-tuple-element.26.refs_1_, bf16[128,1024]{1,0:T(8,128)(2,1)S(1)} %get-tuple-element.30.refs_2_, ...), custom_call_target="tpu_custom_call" | custom-call | flops 838860800 | bytes 4194304 | tf_op jit(solution)/shard_map/lstm2/pallas_call | solution.py:472
  15.1 0.0 collective-permute-done.2.refs_5_
  15.1 0.1 collective-permute-start.3
  15.2 0.0 copy-start
  15.2 0.0 copy-start.1
  15.2 1.6 %lstm3.1 = (bf16[16,1024]{1,0:T(8,128)(2,1)S(1)}, bf16[8,8,128,128]{3,2,1,0:T(8,128)(2,1)S(1)}) custom-call(bf16[12,32,1024]{2,1,0:T(8,128)(2,1)S(1)} %get-tuple-element.25.refs_0_, bf16[528,256]{1,0:T(8,128)(2,1)S(1)} %get-tuple-element.26.refs_1_, bf16[128,1024]{1,0:T(8,128)(2,1)S(1)} %get-tuple-element.33.refs_2_, ...), custom_call_target="tpu_custom_call" | custom-call | flops 167772160 | bytes 4194304 | tf_op jit(solution)/shard_map/lstm3/pallas_call | solution.py:472
  16.9 0.0 collective-permute-done.3
  16.9 0.0 copy-start.2
  16.9 0.0 copy-start.3
  16.9 0.0 copy-start.4
  16.9 1.7 %remap.1 = (bf16[768,128]{1,0:T(8,128)(2,1)S(1)}, bf16[800,128]{1,0:T(8,128)(2,1)S(1)}, f32[16,128]{1,0:T(8,128)S(1)}) custom-call(s32[8,8]{1,0:T(8,128)S(1)} %copy-done, s32[8,8]{1,0:T(8,128)S(1)} %copy-done.1, bf16[16,1024]{1,0:T(8,128)(2,1)S(1)} %get-tuple-element.36.runoff_ref, bf16[8,8,128,128]{3,2,1,0:T(8,128)(2,1)S(1)} %get-tuple-element.37.weight_ref, ...), custom_call_target="tpu_custom_call" | custom-call | tf_op jit(solution)/shard_map/remap/pallas_call | solution.py:499
  18.7 0.5 %collective-permute-start.4 = (bf16[800,128]{1,0:T(8,128)(2,1)S(1)}, bf16[800,128]{1,0:T(8,128)(2,1)S(1)}, u32[]{:S(2)}, u32[]{:S(2)}) collective-permute-start(bf16[800,128]{1,0:T(8,128)(2,1)S(1)} %get-tuple-element.39), channel_id=1, source_target_pairs={{0,2},{2,0},{4,6},{6,4},{8,10},{10,8},{12,14},{14,12},{16,18},{18,... | collective-permute-start | bytes 614408 | tf_op jit(solution)/shard_map/ppermute | solution.py:528
  19.2 1.1 %collective-permute-done.4 = bf16[800,128]{1,0:T(8,128)(2,1)S(1)} collective-permute-done((bf16[800,128]{1,0:T(8,128)(2,1)S(1)}, bf16[800,128]{1,0:T(8,128)(2,1)S(1)}, u32[]{:S(2)}, u32[]{:S(2)}) %collective-permute-start.4) | collective-permute-done | bytes 204832 | tf_op jit(solution)/shard_map/ppermute | solution.py:528
  20.3 0.1 add_convert_fusion
  20.4 1.4 %collective-permute-start.5 = (bf16[416,128]{1,0:T(8,128)(2,1)S(1)}, bf16[416,128]{1,0:T(8,128)(2,1)S(1)}, u32[]{:S(2)}, u32[]{:S(2)}) collective-permute-start(bf16[416,128]{1,0:T(8,128)(2,1)S(1)} %pad_maximum_fusion), channel_id=1, source_target_pairs={{0,4},{2,6},{4,0},{6,2},{8,12},{10,14},{12,8},{14,10},{16,20},{18,... | collective-permute-start | bytes 319496 | tf_op jit(solution)/shard_map/ppermute | solution.py:528
  21.8 1.7 %collective-permute-start.7 = (f32[16,128]{1,0:T(8,128)S(1)}, f32[16,128]{1,0:T(8,128)S(1)}, u32[]{:S(2)}, u32[]{:S(2)}) collective-permute-start(f32[16,128]{1,0:T(8,128)S(1)} %get-tuple-element.48), channel_id=1, source_target_pairs={{0,5},{1,4},{2,7},{3,6},{4,1},{5,0},{6,3},{7,2},{8,13},{9,12},{10,... | collective-permute-start | bytes 24584 | tf_op jit(solution)/shard_map/ppermute | solution.py:538
  23.4 0.5 %collective-permute-start.6 = (f32[16,128]{1,0:T(8,128)S(1)}, f32[16,128]{1,0:T(8,128)S(1)}, u32[]{:S(2)}, u32[]{:S(2)}) collective-permute-start(f32[16,128]{1,0:T(8,128)S(1)} %get-tuple-element.48), channel_id=1, source_target_pairs={{0,1},{1,0},{2,3},{3,2},{4,5},{5,4},{6,7},{7,6},{8,9},{9,8},{10,11... | collective-permute-start | bytes 24584 | tf_op jit(solution)/shard_map/ppermute | solution.py:538
  24.0 2.4 %collective-permute-done.7 = f32[16,128]{1,0:T(8,128)S(1)} collective-permute-done((f32[16,128]{1,0:T(8,128)S(1)}, f32[16,128]{1,0:T(8,128)S(1)}, u32[]{:S(2)}, u32[]{:S(2)}) %collective-permute-start.7) | collective-permute-done | bytes 8224 | tf_op jit(solution)/shard_map/ppermute | solution.py:538
  26.3 0.8 %collective-permute-done.6 = f32[16,128]{1,0:T(8,128)S(1)} collective-permute-done((f32[16,128]{1,0:T(8,128)S(1)}, f32[16,128]{1,0:T(8,128)S(1)}, u32[]{:S(2)}, u32[]{:S(2)}) %collective-permute-start.6) | collective-permute-done | bytes 8224 | tf_op jit(solution)/shard_map/ppermute | solution.py:538
  27.1 0.0 collective-permute-done.5
  27.2 1.4 %collective-permute-start.8 = (bf16[224,128]{1,0:T(8,128)(2,1)S(1)}, bf16[224,128]{1,0:T(8,128)(2,1)S(1)}, u32[]{:S(2)}, u32[]{:S(2)}) collective-permute-start(bf16[224,128]{1,0:T(8,128)(2,1)S(1)} %pad_maximum_fusion.2), channel_id=1, source_target_pairs={{0,8},{2,10},{4,12},{6,14},{8,0},{10,2},{12,4},{14,6},{16,24},{18,... | collective-permute-start | bytes 172040 | tf_op jit(solution)/shard_map/ppermute | solution.py:528
  28.6 2.8 %collective-permute-done.8 = bf16[224,128]{1,0:T(8,128)(2,1)S(1)} collective-permute-done((bf16[224,128]{1,0:T(8,128)(2,1)S(1)}, bf16[224,128]{1,0:T(8,128)(2,1)S(1)}, u32[]{:S(2)}, u32[]{:S(2)}) %collective-permute-start.8) | collective-permute-done | bytes 57376 | tf_op jit(solution)/shard_map/ppermute | solution.py:528
  31.5 2.6 %collective-permute-start.9 = (bf16[128,128]{1,0:T(8,128)(2,1)S(1)}, bf16[128,128]{1,0:T(8,128)(2,1)S(1)}, u32[]{:S(2)}, u32[]{:S(2)}) collective-permute-start(bf16[128,128]{1,0:T(8,128)(2,1)S(1)} %pad_maximum_fusion.4), channel_id=1, source_target_pairs={{0,16},{2,18},{4,20},{6,22},{8,24},{10,26},{12,28},{14,30},{16,0},... | collective-permute-start | bytes 98312 | tf_op jit(solution)/shard_map/ppermute | solution.py:528
  34.1 2.2 %collective-permute-done.9.got_ref = bf16[128,128]{1,0:T(8,128)(2,1)S(1)} collective-permute-done((bf16[128,128]{1,0:T(8,128)(2,1)S(1)}, bf16[128,128]{1,0:T(8,128)(2,1)S(1)}, u32[]{:S(2)}, u32[]{:S(2)}) %collective-permute-start.9) | collective-permute-done | bytes 32800 | tf_op jit(solution)/shard_map/ppermute | solution.py:528
  36.4 2.2 %finish.1 = f32[12,1024]{1,0:T(8,128)} custom-call(s32[16]{0:T(128)S(1)} %copy-done.2, s32[16]{0:T(128)S(1)} %copy-done.3, s32[16]{0:T(128)S(1)} %copy-done.4, f32[16,128]{1,0:T(8,128)S(1)} %get-tuple-element.24.given_ref, f32[16,128]{1,0:T(8,128)S(1)} %get-tuple-element.44.shift_ref, bf16[96,128]{1,0:T(8,128)(2,1)S(1)} %get-tuple-element.50.mine_ref, ...), custom_call_target="tpu_custom_call" | custom-call | tf_op jit(solution)/shard_map/finish/pallas_call | solution.py:541
  (28 shorter events, 0.2 us)
Async XLA Ops:
  0.9 5.3 %collective-permute-start = (f32[1,16,128]{2,1,0:T(8,128)S(1)}, f32[1,16,128]{2,1,0:T(8,128)S(1)}, u32[]{:S(2)}, u32[]{:S(2)}) collective-permute-start(f32[1,16,128]{2,1,0:T(8,128)S(1)} %bitcast.5), channel_id=1, source_target_pairs={{0,4},{2,6},{4,0},{6,2},{8,12},{10,14},{12,8},{14,10},{16,20},{18,... | collective-permute-start | bytes 24584 | tf_op jit(solution)/shard_map/ppermute | solution.py:413
  6.2 3.9 %collective-permute-start.1 = (f32[2,16,128]{2,1,0:T(8,128)S(1)}, f32[2,16,128]{2,1,0:T(8,128)S(1)}, u32[]{:S(2)}, u32[]{:S(2)}) collective-permute-start(f32[2,16,128]{2,1,0:T(8,128)S(1)} %pad_maximum_fusion.5), channel_id=1, source_target_pairs={{0,8},{2,10},{4,12},{6,14},{8,0},{10,2},{12,4},{14,6},{16,24},{18,... | collective-permute-start | bytes 49160 | tf_op jit(solution)/shard_map/ppermute | solution.py:413
  10.2 4.9 %collective-permute-start.2 = (f32[4,16,128]{2,1,0:T(8,128)S(1)}, f32[4,16,128]{2,1,0:T(8,128)S(1)}, u32[]{:S(2)}, u32[]{:S(2)}) collective-permute-start(f32[4,16,128]{2,1,0:T(8,128)S(1)} %pad_maximum_fusion.3), channel_id=1, source_target_pairs={{0,16},{2,18},{4,20},{6,22},{8,24},{10,26},{12,28},{14,30},{16,0},... | collective-permute-start | bytes 98312 | tf_op jit(solution)/shard_map/ppermute | solution.py:413
  15.1 1.7 %collective-permute-start.3 = (f32[8,16,128]{2,1,0:T(8,128)S(1)}, f32[8,16,128]{2,1,0:T(8,128)S(1)}, u32[]{:S(2)}, u32[]{:S(2)}) collective-permute-start(f32[8,16,128]{2,1,0:T(8,128)S(1)} %pad_maximum_fusion.1), channel_id=1, source_target_pairs={{0,2},{2,0},{4,6},{6,4},{8,10},{10,8},{12,14},{14,12},{16,18},{18,... | collective-permute-start | bytes 196616 | tf_op jit(solution)/shard_map/ppermute | solution.py:413
  15.2 1.7 %copy-start = (s32[8,8]{1,0:T(8,128)S(1)}, s32[8,8]{1,0:T(8,128)}, u32[]{:S(2)}) copy-start(s32[8,8]{1,0:T(8,128)} %dest_ref.1) | copy-start | bytes 772
  15.2 1.7 %copy-start.1 = (s32[8,8]{1,0:T(8,128)S(1)}, s32[8,8]{1,0:T(8,128)}, u32[]{:S(2)}) copy-start(s32[8,8]{1,0:T(8,128)} %block_ref.1) | copy-start | bytes 772
  16.9 19.5 %copy-start.2 = (s32[16]{0:T(128)S(1)}, s32[16]{0:T(128)}, u32[]{:S(2)}) copy-start(s32[16]{0:T(128)} %count_ref.1) | copy-start | bytes 196
  16.9 19.4 %copy-start.3 = (s32[16]{0:T(128)S(1)}, s32[16]{0:T(128)}, u32[]{:S(2)}) copy-start(s32[16]{0:T(128)} %parent_ref.1) | copy-start | bytes 196
  16.9 19.4 %copy-start.4 = (s32[16]{0:T(128)S(1)}, s32[16]{0:T(128)}, u32[]{:S(2)}) copy-start(s32[16]{0:T(128)} %reservoir_ref.1) | copy-start | bytes 196
  18.7 1.6 %collective-permute-start.4 = (bf16[800,128]{1,0:T(8,128)(2,1)S(1)}, bf16[800,128]{1,0:T(8,128)(2,1)S(1)}, u32[]{:S(2)}, u32[]{:S(2)}) collective-permute-start(bf16[800,128]{1,0:T(8,128)(2,1)S(1)} %get-tuple-element.39), channel_id=1, source_target_pairs={{0,2},{2,0},{4,6},{6,4},{8,10},{10,8},{12,14},{14,12},{16,18},{18,... | collective-permute-start | bytes 614408 | tf_op jit(solution)/shard_map/ppermute | solution.py:528
  20.4 6.7 %collective-permute-start.5 = (bf16[416,128]{1,0:T(8,128)(2,1)S(1)}, bf16[416,128]{1,0:T(8,128)(2,1)S(1)}, u32[]{:S(2)}, u32[]{:S(2)}) collective-permute-start(bf16[416,128]{1,0:T(8,128)(2,1)S(1)} %pad_maximum_fusion), channel_id=1, source_target_pairs={{0,4},{2,6},{4,0},{6,2},{8,12},{10,14},{12,8},{14,10},{16,20},{18,... | collective-permute-start | bytes 319496 | tf_op jit(solution)/shard_map/ppermute | solution.py:528
  21.8 4.5 %collective-permute-start.7 = (f32[16,128]{1,0:T(8,128)S(1)}, f32[16,128]{1,0:T(8,128)S(1)}, u32[]{:S(2)}, u32[]{:S(2)}) collective-permute-start(f32[16,128]{1,0:T(8,128)S(1)} %get-tuple-element.48), channel_id=1, source_target_pairs={{0,5},{1,4},{2,7},{3,6},{4,1},{5,0},{6,3},{7,2},{8,13},{9,12},{10,... | collective-permute-start | bytes 24584 | tf_op jit(solution)/shard_map/ppermute | solution.py:538
  23.4 3.7 %collective-permute-start.6 = (f32[16,128]{1,0:T(8,128)S(1)}, f32[16,128]{1,0:T(8,128)S(1)}, u32[]{:S(2)}, u32[]{:S(2)}) collective-permute-start(f32[16,128]{1,0:T(8,128)S(1)} %get-tuple-element.48), channel_id=1, source_target_pairs={{0,1},{1,0},{2,3},{3,2},{4,5},{5,4},{6,7},{7,6},{8,9},{9,8},{10,11... | collective-permute-start | bytes 24584 | tf_op jit(solution)/shard_map/ppermute | solution.py:538
  27.2 4.2 %collective-permute-start.8 = (bf16[224,128]{1,0:T(8,128)(2,1)S(1)}, bf16[224,128]{1,0:T(8,128)(2,1)S(1)}, u32[]{:S(2)}, u32[]{:S(2)}) collective-permute-start(bf16[224,128]{1,0:T(8,128)(2,1)S(1)} %pad_maximum_fusion.2), channel_id=1, source_target_pairs={{0,8},{2,10},{4,12},{6,14},{8,0},{10,2},{12,4},{14,6},{16,24},{18,... | collective-permute-start | bytes 172040 | tf_op jit(solution)/shard_map/ppermute | solution.py:528
  31.5 4.9 %collective-permute-start.9 = (bf16[128,128]{1,0:T(8,128)(2,1)S(1)}, bf16[128,128]{1,0:T(8,128)(2,1)S(1)}, u32[]{:S(2)}, u32[]{:S(2)}) collective-permute-start(bf16[128,128]{1,0:T(8,128)(2,1)S(1)} %pad_maximum_fusion.4), channel_id=1, source_target_pairs={{0,16},{2,18},{4,20},{6,22},{8,24},{10,26},{12,28},{14,30},{16,0},... | collective-permute-start | bytes 98312 | tf_op jit(solution)/shard_map/ppermute | solution.py:528

commit v5 on v4

--- a/solution.py
+++ b/solution.py
@@ -252,10 +252,12 @@
     square[...] = jnp.zeros_like(square)
     for group in range(unit_blocks):
         left = runoff_ref[:, group * block : (group + 1) * block]
-        for k in range(fan_out):
-            contrib = jnp.dot(left, weight_ref[group, k], preferred_element_type=jnp.float32)
-            slot = slot_of(dest_ref[group, k] ^ me, size) * reach_blocks + block_ref[group, k]
-            slots[slot] = slots[slot] + contrib
+        for k in range(0, fan_out, 2):
+            right = jnp.concatenate([weight_ref[group, k], weight_ref[group, k + 1]], axis=1)
+            both = jnp.dot(left, right, preferred_element_type=jnp.float32)
+            for side in range(2):
+                slot = slot_of(dest_ref[group, k + side] ^ me, size) * reach_blocks + block_ref[group, k + side]
+                slots[slot] = slots[slot] + both[:, side * block : (side + 1) * block]
     half = size // 2
     rows = reach_blocks * steps
     lane = lax.broadcasted_iota(jnp.int32, (PAD, block), 1)
@@ -415,8 +417,8 @@
         shares = jnp.concatenate([shares, other], axis=0)
 
     chunk = 256
-    parts = 4
-    bounds = [0, 1, 6, 11, 12]
+    parts = 3
+    bounds = [0, 1, steps // 2, steps]
     carried = (
         pltpu.VMEM((state, units), jnp.bfloat16),
         pltpu.VMEM((state, units), jnp.float32),

time: 38.8 us -> 38.3 us (0.987)
  waiting for transfers between devices: 9.26 us -> 11.1 us
  Pallas kernels: 13.2 us -> 11.7 us
  starting transfers between devices: 15.6 us -> 14.8 us
    pallas_call x3 -> x2, Pallas kernels: 6.14 us -> 4.88 us  [shards(): pl.pallas_call(functools.partial(later_kernel, first=bounds[part], count=...]
    ppermute x4, waiting for transfers between devices: 0.01 us -> 1.24 us  [shards(): lax.ppermute(shares, 'basin', [(i, i ^ 1 << bit) for i in range(size)])]
    ppermute x4, starting transfers between devices: 5.99 us -> 5.17 us  [shards(): got = lax.ppermute(send, 'basin', [(i, i ^ swap) for i in range(size)])]
    ppermute x4, waiting for transfers between devices: 6.13 us -> 6.79 us  [shards(): got = lax.ppermute(send, 'basin', [(i, i ^ swap) for i in range(size)])]
  transfers between devices with their start and end apart: 10 -> 10, of which waited for: 5 -> 6; matrix products, arithmetic and copies ran while one was open for 0% -> 0% of each run, Pallas kernels for 22% -> 19%
where the time goes in v5:
time: 38.3 us; the launch traced here: 38.1 us
  starting transfers between devices  14.8 us (39%)
  Pallas kernels  11.7 us (31%)
  waiting for transfers between devices  11.1 us (29%)
    ppermute x4, starting transfers between devices, shards(): lax.ppermute(shares, 'basin', [(i, i ^ 1 << bit) for i in range(size)])  7.43 us
    ppermute x4, waiting for transfers between devices, shards(): got = lax.ppermute(send, 'basin', [(i, i ^ swap) for i in range(size)])  6.79 us
    ppermute x4, starting transfers between devices, shards(): got = lax.ppermute(send, 'basin', [(i, i ^ swap) for i in range(size)])  5.17 us
    pallas_call x2, Pallas kernels, shards(): pl.pallas_call(functools.partial(later_kernel, first=bounds[part], count=...  4.88 us
    ppermute x2, waiting for transfers between devices, shards(): others.append(lax.ppermute(shift, AXES, route))  3.11 us
    pallas_call x1, Pallas kernels, shards(): pl.pallas_call(functools.partial(first_kernel, count=bounds[1], chunk=chu...  2.27 us
    ppermute x2, starting transfers between devices, shards(): others.append(lax.ppermute(shift, AXES, route))  2.23 us
    pallas_call x1, Pallas kernels, shards(): pl.pallas_call(functools.partial(finish_kernel, steps=steps, unit_size=un...  2.19 us
  transfers between devices with their start and end apart: 10, of which 6 were waited for; matrix products, arithmetic and copies ran while one was open for 0% of the time, Pallas kernels for 19%

profile of v5, /device:TPU:0, one launch (start us, length us, event | category | flops | bytes accessed | tf_op | source)
XLA Modules:
  0.0 38.1 jit_solution(13769005158443910296)
XLA Ops:
  0.0 0.9 %prep.1 = f32[16,128]{1,0:T(8,128)S(1)} custom-call(s32[16]{0:T(128)} %count_ref.1, f32[8,128,128]{2,1,0:T(8,128)} %refs_6_.2, f32[8,128]{1,0:T(8,128)} %refs_7_.1), custom_call_target="tpu_custom_call" | custom-call | tf_op jit(solution)/shard_map/prep/pallas_call | solution.py:398
  0.9 3.0 %collective-permute-start = (f32[1,16,128]{2,1,0:T(8,128)S(1)}, f32[1,16,128]{2,1,0:T(8,128)S(1)}, u32[]{:S(2)}, u32[]{:S(2)}) collective-permute-start(f32[1,16,128]{2,1,0:T(8,128)S(1)} %bitcast.5), channel_id=1, source_target_pairs={{0,4},{2,6},{4,0},{6,2},{8,12},{10,14},{12,8},{14,10},{16,20},{18,... | collective-permute-start | bytes 24584 | tf_op jit(solution)/shard_map/ppermute | solution.py:415
  3.9 2.3 %lstm0.1 = (bf16[12,32,1024]{2,1,0:T(8,128)(2,1)S(1)}, bf16[528,256]{1,0:T(8,128)(2,1)S(1)}, bf16[128,1024]{1,0:T(8,128)(2,1)S(1)}, f32[128,1024]{1,0:T(8,128)S(...) custom-call(bf16[512,128]{1,0:T(8,128)(2,1)} %w_recur_hbm.1, bf16[32,512]{1,0:T(8,128)(2,1)} %bitcast.9, ...), custom_call_target="tpu_custom_call" | custom-call | flops 167772160 | bytes 4194304 | tf_op jit(solution)/shard_map/lstm0/pallas_call | solution.py:435
  6.2 0.0 collective-permute-done.refs_5_
  6.2 1.7 %collective-permute-start.1 = (f32[2,16,128]{2,1,0:T(8,128)S(1)}, f32[2,16,128]{2,1,0:T(8,128)S(1)}, u32[]{:S(2)}, u32[]{:S(2)}) collective-permute-start(f32[2,16,128]{2,1,0:T(8,128)S(1)} %pad_maximum_fusion.5), channel_id=1, source_target_pairs={{0,8},{2,10},{4,12},{6,14},{8,0},{10,2},{12,4},{14,6},{16,24},{18,... | collective-permute-start | bytes 49160 | tf_op jit(solution)/shard_map/ppermute | solution.py:415
  7.9 2.2 %lstm1.1 = (bf16[128,1024]{1,0:T(8,128)(2,1)S(1)}, f32[128,1024]{1,0:T(8,128)S(1)}, f32[16,1024]{1,0:T(8,128)S(1)}, f32[8,128,128]{2,1,0:T(8,128)S(1)}, f32[8,128]{1,0:T(8,128)S(1)}) custom-call(bf16[12,32,1024]{2,1,0:T(8,128)(2,1)S(1)} %get-tuple-element.22.refs_0_, bf16[528,256]{1,0:T(8,128)(2,1)S(1)} %get-tuple-element.23.refs_1_, ...), custom_call_target="tpu_custom_call" | custom-call | flops 838860800 | bytes 4194304 | tf_op jit(solution)/shard_map/lstm1/pallas_call | solution.py:474
  10.1 0.0 collective-permute-done.1.refs_5_
  10.1 2.7 %collective-permute-start.2 = (f32[4,16,128]{2,1,0:T(8,128)S(1)}, f32[4,16,128]{2,1,0:T(8,128)S(1)}, u32[]{:S(2)}, u32[]{:S(2)}) collective-permute-start(f32[4,16,128]{2,1,0:T(8,128)S(1)} %pad_maximum_fusion.3), channel_id=1, source_target_pairs={{0,16},{2,18},{4,20},{6,22},{8,24},{10,26},{12,28},{14,30},{16,0},... | collective-permute-start | bytes 98312 | tf_op jit(solution)/shard_map/ppermute | solution.py:415
  12.8 2.7 %lstm2.1 = (bf16[16,1024]{1,0:T(8,128)(2,1)S(1)}, bf16[8,8,128,128]{3,2,1,0:T(8,128)(2,1)S(1)}) custom-call(bf16[12,32,1024]{2,1,0:T(8,128)(2,1)S(1)} %get-tuple-element.22.refs_0_, bf16[528,256]{1,0:T(8,128)(2,1)S(1)} %get-tuple-element.23.refs_1_, bf16[128,1024]{1,0:T(8,128)(2,1)S(1)} %get-tuple-element.27.refs_2_, ...), custom_call_target="tpu_custom_call" | custom-call | flops 1006632960 | bytes 4194304 | tf_op jit(solution)/shard_map/lstm2/pallas_call | solution.py:474
  15.5 0.0 collective-permute-done.2
  15.5 0.1 collective-permute-start.3
  15.6 1.2 %collective-permute-done.3 = f32[8,16,128]{2,1,0:T(8,128)S(1)} collective-permute-done((f32[8,16,128]{2,1,0:T(8,128)S(1)}, f32[8,16,128]{2,1,0:T(8,128)S(1)}, u32[]{:S(2)}, u32[]{:S(2)}) %collective-permute-start.3) | collective-permute-done | bytes 65568 | tf_op jit(solution)/shard_map/ppermute | solution.py:415
  16.9 0.0 copy-done
  16.9 0.0 copy-done.1
  16.9 0.0 copy-start.2
  16.9 0.0 copy-start.3
  16.9 0.0 copy-start.4
  16.9 1.5 %remap.1 = (bf16[768,128]{1,0:T(8,128)(2,1)S(1)}, bf16[800,128]{1,0:T(8,128)(2,1)S(1)}, f32[16,128]{1,0:T(8,128)S(1)}) custom-call(s32[8,8]{1,0:T(8,128)S(1)} %copy-done, s32[8,8]{1,0:T(8,128)S(1)} %copy-done.1, bf16[16,1024]{1,0:T(8,128)(2,1)S(1)} %get-tuple-element.30.runoff_ref, bf16[8,8,128,128]{3,2,1,0:T(8,128)(2,1)S(1)} %get-tuple-element.31.weight_ref, ...), custom_call_target="tpu_custom_call" | custom-call | tf_op jit(solution)/shard_map/remap/pallas_call | solution.py:501
  18.4 0.2 collective-permute-start.4
  18.6 1.3 %collective-permute-done.4 = bf16[800,128]{1,0:T(8,128)(2,1)S(1)} collective-permute-done((bf16[800,128]{1,0:T(8,128)(2,1)S(1)}, bf16[800,128]{1,0:T(8,128)(2,1)S(1)}, u32[]{:S(2)}, u32[]{:S(2)}) %collective-permute-start.4) | collective-permute-done | bytes 204832 | tf_op jit(solution)/shard_map/ppermute | solution.py:530
  19.9 0.1 add_convert_fusion
  20.0 1.3 %collective-permute-start.5 = (bf16[416,128]{1,0:T(8,128)(2,1)S(1)}, bf16[416,128]{1,0:T(8,128)(2,1)S(1)}, u32[]{:S(2)}, u32[]{:S(2)}) collective-permute-start(bf16[416,128]{1,0:T(8,128)(2,1)S(1)} %pad_maximum_fusion), channel_id=1, source_target_pairs={{0,4},{2,6},{4,0},{6,2},{8,12},{10,14},{12,8},{14,10},{16,20},{18,... | collective-permute-start | bytes 319496 | tf_op jit(solution)/shard_map/ppermute | solution.py:530
  21.3 1.7 %collective-permute-start.7 = (f32[16,128]{1,0:T(8,128)S(1)}, f32[16,128]{1,0:T(8,128)S(1)}, u32[]{:S(2)}, u32[]{:S(2)}) collective-permute-start(f32[16,128]{1,0:T(8,128)S(1)} %get-tuple-element.42), channel_id=1, source_target_pairs={{0,5},{1,4},{2,7},{3,6},{4,1},{5,0},{6,3},{7,2},{8,13},{9,12},{10,... | collective-permute-start | bytes 24584 | tf_op jit(solution)/shard_map/ppermute | solution.py:540
  23.0 0.5 %collective-permute-start.6 = (f32[16,128]{1,0:T(8,128)S(1)}, f32[16,128]{1,0:T(8,128)S(1)}, u32[]{:S(2)}, u32[]{:S(2)}) collective-permute-start(f32[16,128]{1,0:T(8,128)S(1)} %get-tuple-element.42), channel_id=1, source_target_pairs={{0,1},{1,0},{2,3},{3,2},{4,5},{5,4},{6,7},{7,6},{8,9},{9,8},{10,11... | collective-permute-start | bytes 24584 | tf_op jit(solution)/shard_map/ppermute | solution.py:540
  23.5 2.3 %collective-permute-done.7 = f32[16,128]{1,0:T(8,128)S(1)} collective-permute-done((f32[16,128]{1,0:T(8,128)S(1)}, f32[16,128]{1,0:T(8,128)S(1)}, u32[]{:S(2)}, u32[]{:S(2)}) %collective-permute-start.7) | collective-permute-done | bytes 8224 | tf_op jit(solution)/shard_map/ppermute | solution.py:540
  25.9 0.8 %collective-permute-done.6 = f32[16,128]{1,0:T(8,128)S(1)} collective-permute-done((f32[16,128]{1,0:T(8,128)S(1)}, f32[16,128]{1,0:T(8,128)S(1)}, u32[]{:S(2)}, u32[]{:S(2)}) %collective-permute-start.6) | collective-permute-done | bytes 8224 | tf_op jit(solution)/shard_map/ppermute | solution.py:540
  26.6 0.0 collective-permute-done.5
  26.7 1.5 %collective-permute-start.8 = (bf16[224,128]{1,0:T(8,128)(2,1)S(1)}, bf16[224,128]{1,0:T(8,128)(2,1)S(1)}, u32[]{:S(2)}, u32[]{:S(2)}) collective-permute-start(bf16[224,128]{1,0:T(8,128)(2,1)S(1)} %pad_maximum_fusion.2), channel_id=1, source_target_pairs={{0,8},{2,10},{4,12},{6,14},{8,0},{10,2},{12,4},{14,6},{16,24},{18,... | collective-permute-start | bytes 172040 | tf_op jit(solution)/shard_map/ppermute | solution.py:530
  28.3 2.7 %collective-permute-done.8 = bf16[224,128]{1,0:T(8,128)(2,1)S(1)} collective-permute-done((bf16[224,128]{1,0:T(8,128)(2,1)S(1)}, bf16[224,128]{1,0:T(8,128)(2,1)S(1)}, u32[]{:S(2)}, u32[]{:S(2)}) %collective-permute-start.8) | collective-permute-done | bytes 57376 | tf_op jit(solution)/shard_map/ppermute | solution.py:530
  31.1 2.1 %collective-permute-start.9 = (bf16[128,128]{1,0:T(8,128)(2,1)S(1)}, bf16[128,128]{1,0:T(8,128)(2,1)S(1)}, u32[]{:S(2)}, u32[]{:S(2)}) collective-permute-start(bf16[128,128]{1,0:T(8,128)(2,1)S(1)} %pad_maximum_fusion.4), channel_id=1, source_target_pairs={{0,16},{2,18},{4,20},{6,22},{8,24},{10,26},{12,28},{14,30},{16,0},... | collective-permute-start | bytes 98312 | tf_op jit(solution)/shard_map/ppermute | solution.py:530
  33.2 2.8 %collective-permute-done.9.got_ref = bf16[128,128]{1,0:T(8,128)(2,1)S(1)} collective-permute-done((bf16[128,128]{1,0:T(8,128)(2,1)S(1)}, bf16[128,128]{1,0:T(8,128)(2,1)S(1)}, u32[]{:S(2)}, u32[]{:S(2)}) %collective-permute-start.9) | collective-permute-done | bytes 32800 | tf_op jit(solution)/shard_map/ppermute | solution.py:530
  35.9 2.2 %finish.1 = f32[12,1024]{1,0:T(8,128)} custom-call(s32[16]{0:T(128)S(1)} %copy-done.2, s32[16]{0:T(128)S(1)} %copy-done.3, s32[16]{0:T(128)S(1)} %copy-done.4, f32[16,128]{1,0:T(8,128)S(1)} %get-tuple-element.21.given_ref, f32[16,128]{1,0:T(8,128)S(1)} %get-tuple-element.38.shift_ref, bf16[96,128]{1,0:T(8,128)(2,1)S(1)} %get-tuple-element.44.mine_ref, ...), custom_call_target="tpu_custom_call" | custom-call | tf_op jit(solution)/shard_map/finish/pallas_call | solution.py:543
  (27 shorter events, 0.2 us)
Async XLA Ops:
  0.9 5.3 %collective-permute-start = (f32[1,16,128]{2,1,0:T(8,128)S(1)}, f32[1,16,128]{2,1,0:T(8,128)S(1)}, u32[]{:S(2)}, u32[]{:S(2)}) collective-permute-start(f32[1,16,128]{2,1,0:T(8,128)S(1)} %bitcast.5), channel_id=1, source_target_pairs={{0,4},{2,6},{4,0},{6,2},{8,12},{10,14},{12,8},{14,10},{16,20},{18,... | collective-permute-start | bytes 24584 | tf_op jit(solution)/shard_map/ppermute | solution.py:415
  6.2 3.9 %collective-permute-start.1 = (f32[2,16,128]{2,1,0:T(8,128)S(1)}, f32[2,16,128]{2,1,0:T(8,128)S(1)}, u32[]{:S(2)}, u32[]{:S(2)}) collective-permute-start(f32[2,16,128]{2,1,0:T(8,128)S(1)} %pad_maximum_fusion.5), channel_id=1, source_target_pairs={{0,8},{2,10},{4,12},{6,14},{8,0},{10,2},{12,4},{14,6},{16,24},{18,... | collective-permute-start | bytes 49160 | tf_op jit(solution)/shard_map/ppermute | solution.py:415
  10.1 5.4 %collective-permute-start.2 = (f32[4,16,128]{2,1,0:T(8,128)S(1)}, f32[4,16,128]{2,1,0:T(8,128)S(1)}, u32[]{:S(2)}, u32[]{:S(2)}) collective-permute-start(f32[4,16,128]{2,1,0:T(8,128)S(1)} %pad_maximum_fusion.3), channel_id=1, source_target_pairs={{0,16},{2,18},{4,20},{6,22},{8,24},{10,26},{12,28},{14,30},{16,0},... | collective-permute-start | bytes 98312 | tf_op jit(solution)/shard_map/ppermute | solution.py:415
  12.8 4.1 %copy-start = (s32[8,8]{1,0:T(8,128)S(1)}, s32[8,8]{1,0:T(8,128)}, u32[]{:S(2)}) copy-start(s32[8,8]{1,0:T(8,128)} %dest_ref.1) | copy-start | bytes 772
  12.8 4.1 %copy-start.1 = (s32[8,8]{1,0:T(8,128)S(1)}, s32[8,8]{1,0:T(8,128)}, u32[]{:S(2)}) copy-start(s32[8,8]{1,0:T(8,128)} %block_ref.1) | copy-start | bytes 772
  15.5 1.3 %collective-permute-start.3 = (f32[8,16,128]{2,1,0:T(8,128)S(1)}, f32[8,16,128]{2,1,0:T(8,128)S(1)}, u32[]{:S(2)}, u32[]{:S(2)}) collective-permute-start(f32[8,16,128]{2,1,0:T(8,128)S(1)} %pad_maximum_fusion.1), channel_id=1, source_target_pairs={{0,2},{2,0},{4,6},{6,4},{8,10},{10,8},{12,14},{14,12},{16,18},{18,... | collective-permute-start | bytes 196616 | tf_op jit(solution)/shard_map/ppermute | solution.py:415
  16.9 19.1 %copy-start.2 = (s32[16]{0:T(128)S(1)}, s32[16]{0:T(128)}, u32[]{:S(2)}) copy-start(s32[16]{0:T(128)} %count_ref.1) | copy-start | bytes 196
  16.9 19.1 %copy-start.3 = (s32[16]{0:T(128)S(1)}, s32[16]{0:T(128)}, u32[]{:S(2)}) copy-start(s32[16]{0:T(128)} %parent_ref.1) | copy-start | bytes 196
  16.9 19.0 %copy-start.4 = (s32[16]{0:T(128)S(1)}, s32[16]{0:T(128)}, u32[]{:S(2)}) copy-start(s32[16]{0:T(128)} %reservoir_ref.1) | copy-start | bytes 196
  18.4 1.5 %collective-permute-start.4 = (bf16[800,128]{1,0:T(8,128)(2,1)S(1)}, bf16[800,128]{1,0:T(8,128)(2,1)S(1)}, u32[]{:S(2)}, u32[]{:S(2)}) collective-permute-start(bf16[800,128]{1,0:T(8,128)(2,1)S(1)} %get-tuple-element.33), channel_id=1, source_target_pairs={{0,2},{2,0},{4,6},{6,4},{8,10},{10,8},{12,14},{14,12},{16,18},{18,... | collective-permute-start | bytes 614408 | tf_op jit(solution)/shard_map/ppermute | solution.py:530
  20.0 6.7 %collective-permute-start.5 = (bf16[416,128]{1,0:T(8,128)(2,1)S(1)}, bf16[416,128]{1,0:T(8,128)(2,1)S(1)}, u32[]{:S(2)}, u32[]{:S(2)}) collective-permute-start(bf16[416,128]{1,0:T(8,128)(2,1)S(1)} %pad_maximum_fusion), channel_id=1, source_target_pairs={{0,4},{2,6},{4,0},{6,2},{8,12},{10,14},{12,8},{14,10},{16,20},{18,... | collective-permute-start | bytes 319496 | tf_op jit(solution)/shard_map/ppermute | solution.py:530
  21.3 4.5 %collective-permute-start.7 = (f32[16,128]{1,0:T(8,128)S(1)}, f32[16,128]{1,0:T(8,128)S(1)}, u32[]{:S(2)}, u32[]{:S(2)}) collective-permute-start(f32[16,128]{1,0:T(8,128)S(1)} %get-tuple-element.42), channel_id=1, source_target_pairs={{0,5},{1,4},{2,7},{3,6},{4,1},{5,0},{6,3},{7,2},{8,13},{9,12},{10,... | collective-permute-start | bytes 24584 | tf_op jit(solution)/shard_map/ppermute | solution.py:540
  23.0 3.7 %collective-permute-start.6 = (f32[16,128]{1,0:T(8,128)S(1)}, f32[16,128]{1,0:T(8,128)S(1)}, u32[]{:S(2)}, u32[]{:S(2)}) collective-permute-start(f32[16,128]{1,0:T(8,128)S(1)} %get-tuple-element.42), channel_id=1, source_target_pairs={{0,1},{1,0},{2,3},{3,2},{4,5},{5,4},{6,7},{7,6},{8,9},{9,8},{10,11... | collective-permute-start | bytes 24584 | tf_op jit(solution)/shard_map/ppermute | solution.py:540
  26.7 4.2 %collective-permute-start.8 = (bf16[224,128]{1,0:T(8,128)(2,1)S(1)}, bf16[224,128]{1,0:T(8,128)(2,1)S(1)}, u32[]{:S(2)}, u32[]{:S(2)}) collective-permute-start(bf16[224,128]{1,0:T(8,128)(2,1)S(1)} %pad_maximum_fusion.2), channel_id=1, source_target_pairs={{0,8},{2,10},{4,12},{6,14},{8,0},{10,2},{12,4},{14,6},{16,24},{18,... | collective-permute-start | bytes 172040 | tf_op jit(solution)/shard_map/ppermute | solution.py:530
  31.1 4.9 %collective-permute-start.9 = (bf16[128,128]{1,0:T(8,128)(2,1)S(1)}, bf16[128,128]{1,0:T(8,128)(2,1)S(1)}, u32[]{:S(2)}, u32[]{:S(2)}) collective-permute-start(bf16[128,128]{1,0:T(8,128)(2,1)S(1)} %pad_maximum_fusion.4), channel_id=1, source_target_pairs={{0,16},{2,18},{4,20},{6,22},{8,24},{10,26},{12,28},{14,30},{16,0},... | collective-permute-start | bytes 98312 | tf_op jit(solution)/shard_map/ppermute | solution.py:530

commit v6 on v5

--- a/solution.py
+++ b/solution.py
@@ -418,7 +418,7 @@
 
     chunk = 256
     parts = 3
-    bounds = [0, 1, steps // 2, steps]
+    bounds = [0, 1, steps * 5 // 12, steps]
     carried = (
         pltpu.VMEM((state, units), jnp.bfloat16),
         pltpu.VMEM((state, units), jnp.float32),

time: 38.3 us -> 38.6 us (level)
  waiting for transfers between devices: 11.1 us -> 11.7 us
  transfers between devices with their start and end apart: 10 -> 10, of which waited for: 6 -> 7; matrix products, arithmetic and copies ran while one was open for 0% -> 0% of each run, Pallas kernels for 19% -> 19%
where the time goes in v6:
time: 38.6 us; the launch traced here: 38.4 us
  starting transfers between devices  14.5 us (38%)
  Pallas kernels  11.7 us (30%)
  waiting for transfers between devices  11.7 us (30%)
    ppermute x4, starting transfers between devices, shards(): lax.ppermute(shares, 'basin', [(i, i ^ 1 << bit) for i in range(size)])  7.38 us
    ppermute x4, waiting for transfers between devices, shards(): got = lax.ppermute(send, 'basin', [(i, i ^ swap) for i in range(size)])  7.06 us
    ppermute x4, starting transfers between devices, shards(): got = lax.ppermute(send, 'basin', [(i, i ^ swap) for i in range(size)])  4.9 us
    pallas_call x2, Pallas kernels, shards(): pl.pallas_call(functools.partial(later_kernel, first=bounds[part], count=...  4.89 us
    ppermute x2, waiting for transfers between devices, shards(): others.append(lax.ppermute(shift, AXES, route))  3.09 us
    pallas_call x1, Pallas kernels, shards(): pl.pallas_call(functools.partial(first_kernel, count=bounds[1], chunk=chu...  2.27 us
    ppermute x2, starting transfers between devices, shards(): others.append(lax.ppermute(shift, AXES, route))  2.22 us
    pallas_call x1, Pallas kernels, shards(): pl.pallas_call(functools.partial(finish_kernel, steps=steps, unit_size=un...  2.19 us
  transfers between devices with their start and end apart: 10, of which 7 were waited for; matrix products, arithmetic and copies ran while one was open for 0% of the time, Pallas kernels for 19%

profile of v6, /device:TPU:0, one launch (start us, length us, event | category | flops | bytes accessed | tf_op | source)
XLA Modules:
  0.0 38.4 jit_solution(14110379292841028261)
XLA Ops:
  0.0 0.9 %prep.1 = f32[16,128]{1,0:T(8,128)S(1)} custom-call(s32[16]{0:T(128)} %count_ref.1, f32[8,128,128]{2,1,0:T(8,128)} %refs_6_.2, f32[8,128]{1,0:T(8,128)} %refs_7_.1), custom_call_target="tpu_custom_call" | custom-call | tf_op jit(solution)/shard_map/prep/pallas_call | solution.py:398
  0.9 3.0 %collective-permute-start = (f32[1,16,128]{2,1,0:T(8,128)S(1)}, f32[1,16,128]{2,1,0:T(8,128)S(1)}, u32[]{:S(2)}, u32[]{:S(2)}) collective-permute-start(f32[1,16,128]{2,1,0:T(8,128)S(1)} %bitcast.5), channel_id=1, source_target_pairs={{0,4},{2,6},{4,0},{6,2},{8,12},{10,14},{12,8},{14,10},{16,20},{18,... | collective-permute-start | bytes 24584 | tf_op jit(solution)/shard_map/ppermute | solution.py:415
  3.9 2.3 %lstm0.1 = (bf16[12,32,1024]{2,1,0:T(8,128)(2,1)S(1)}, bf16[528,256]{1,0:T(8,128)(2,1)S(1)}, bf16[128,1024]{1,0:T(8,128)(2,1)S(1)}, f32[128,1024]{1,0:T(8,128)S(...) custom-call(bf16[512,128]{1,0:T(8,128)(2,1)} %w_recur_hbm.1, bf16[32,512]{1,0:T(8,128)(2,1)} %bitcast.9, ...), custom_call_target="tpu_custom_call" | custom-call | flops 167772160 | bytes 4194304 | tf_op jit(solution)/shard_map/lstm0/pallas_call | solution.py:435
  6.2 0.0 collective-permute-done.refs_5_
  6.2 1.7 %collective-permute-start.1 = (f32[2,16,128]{2,1,0:T(8,128)S(1)}, f32[2,16,128]{2,1,0:T(8,128)S(1)}, u32[]{:S(2)}, u32[]{:S(2)}) collective-permute-start(f32[2,16,128]{2,1,0:T(8,128)S(1)} %pad_maximum_fusion.5), channel_id=1, source_target_pairs={{0,8},{2,10},{4,12},{6,14},{8,0},{10,2},{12,4},{14,6},{16,24},{18,... | collective-permute-start | bytes 49160 | tf_op jit(solution)/shard_map/ppermute | solution.py:415
  7.9 1.8 %lstm1.1 = (bf16[128,1024]{1,0:T(8,128)(2,1)S(1)}, f32[128,1024]{1,0:T(8,128)S(1)}, f32[16,1024]{1,0:T(8,128)S(1)}, f32[8,128,128]{2,1,0:T(8,128)S(1)}, f32[8,128]{1,0:T(8,128)S(1)}) custom-call(bf16[12,32,1024]{2,1,0:T(8,128)(2,1)S(1)} %get-tuple-element.22.refs_0_, bf16[528,256]{1,0:T(8,128)(2,1)S(1)} %get-tuple-element.23.refs_1_, ...), custom_call_target="tpu_custom_call" | custom-call | flops 671088640 | bytes 4194304 | tf_op jit(solution)/shard_map/lstm1/pallas_call | solution.py:474
  9.7 0.3 collective-permute-done.1.refs_5_
  10.1 2.6 %collective-permute-start.2 = (f32[4,16,128]{2,1,0:T(8,128)S(1)}, f32[4,16,128]{2,1,0:T(8,128)S(1)}, u32[]{:S(2)}, u32[]{:S(2)}) collective-permute-start(f32[4,16,128]{2,1,0:T(8,128)S(1)} %pad_maximum_fusion.3), channel_id=1, source_target_pairs={{0,16},{2,18},{4,20},{6,22},{8,24},{10,26},{12,28},{14,30},{16,0},... | collective-permute-start | bytes 98312 | tf_op jit(solution)/shard_map/ppermute | solution.py:415
  12.7 3.1 %lstm2.1 = (bf16[16,1024]{1,0:T(8,128)(2,1)S(1)}, bf16[8,8,128,128]{3,2,1,0:T(8,128)(2,1)S(1)}) custom-call(bf16[12,32,1024]{2,1,0:T(8,128)(2,1)S(1)} %get-tuple-element.22.refs_0_, bf16[528,256]{1,0:T(8,128)(2,1)S(1)} %get-tuple-element.23.refs_1_, bf16[128,1024]{1,0:T(8,128)(2,1)S(1)} %get-tuple-element.27.refs_2_, ...), custom_call_target="tpu_custom_call" | custom-call | flops 1174405120 | bytes 4194304 | tf_op jit(solution)/shard_map/lstm2/pallas_call | solution.py:474
  15.8 0.0 collective-permute-done.2
  15.8 0.1 collective-permute-start.3
  15.9 1.2 %collective-permute-done.3 = f32[8,16,128]{2,1,0:T(8,128)S(1)} collective-permute-done((f32[8,16,128]{2,1,0:T(8,128)S(1)}, f32[8,16,128]{2,1,0:T(8,128)S(1)}, u32[]{:S(2)}, u32[]{:S(2)}) %collective-permute-start.3) | collective-permute-done | bytes 65568 | tf_op jit(solution)/shard_map/ppermute | solution.py:415
  17.1 0.0 copy-done
  17.2 0.0 copy-start.2
  17.2 0.0 copy-start.3
  17.2 0.0 copy-start.4
  17.2 1.5 %remap.1 = (bf16[768,128]{1,0:T(8,128)(2,1)S(1)}, bf16[800,128]{1,0:T(8,128)(2,1)S(1)}, f32[16,128]{1,0:T(8,128)S(1)}) custom-call(s32[8,8]{1,0:T(8,128)S(1)} %copy-done, s32[8,8]{1,0:T(8,128)S(1)} %copy-done.1, bf16[16,1024]{1,0:T(8,128)(2,1)S(1)} %get-tuple-element.30.runoff_ref, bf16[8,8,128,128]{3,2,1,0:T(8,128)(2,1)S(1)} %get-tuple-element.31.weight_ref, ...), custom_call_target="tpu_custom_call" | custom-call | tf_op jit(solution)/shard_map/remap/pallas_call | solution.py:501
  18.6 0.2 collective-permute-start.4
  18.9 1.3 %collective-permute-done.4 = bf16[800,128]{1,0:T(8,128)(2,1)S(1)} collective-permute-done((bf16[800,128]{1,0:T(8,128)(2,1)S(1)}, bf16[800,128]{1,0:T(8,128)(2,1)S(1)}, u32[]{:S(2)}, u32[]{:S(2)}) %collective-permute-start.4) | collective-permute-done | bytes 204832 | tf_op jit(solution)/shard_map/ppermute | solution.py:530
  20.2 0.1 add_convert_fusion
  20.3 1.3 %collective-permute-start.5 = (bf16[416,128]{1,0:T(8,128)(2,1)S(1)}, bf16[416,128]{1,0:T(8,128)(2,1)S(1)}, u32[]{:S(2)}, u32[]{:S(2)}) collective-permute-start(bf16[416,128]{1,0:T(8,128)(2,1)S(1)} %pad_maximum_fusion), channel_id=1, source_target_pairs={{0,4},{2,6},{4,0},{6,2},{8,12},{10,14},{12,8},{14,10},{16,20},{18,... | collective-permute-start | bytes 319496 | tf_op jit(solution)/shard_map/ppermute | solution.py:530
  21.6 1.7 %collective-permute-start.7 = (f32[16,128]{1,0:T(8,128)S(1)}, f32[16,128]{1,0:T(8,128)S(1)}, u32[]{:S(2)}, u32[]{:S(2)}) collective-permute-start(f32[16,128]{1,0:T(8,128)S(1)} %get-tuple-element.42), channel_id=1, source_target_pairs={{0,5},{1,4},{2,7},{3,6},{4,1},{5,0},{6,3},{7,2},{8,13},{9,12},{10,... | collective-permute-start | bytes 24584 | tf_op jit(solution)/shard_map/ppermute | solution.py:540
  23.3 0.6 %collective-permute-start.6 = (f32[16,128]{1,0:T(8,128)S(1)}, f32[16,128]{1,0:T(8,128)S(1)}, u32[]{:S(2)}, u32[]{:S(2)}) collective-permute-start(f32[16,128]{1,0:T(8,128)S(1)} %get-tuple-element.42), channel_id=1, source_target_pairs={{0,1},{1,0},{2,3},{3,2},{4,5},{5,4},{6,7},{7,6},{8,9},{9,8},{10,11... | collective-permute-start | bytes 24584 | tf_op jit(solution)/shard_map/ppermute | solution.py:540
  23.8 2.3 %collective-permute-done.7 = f32[16,128]{1,0:T(8,128)S(1)} collective-permute-done((f32[16,128]{1,0:T(8,128)S(1)}, f32[16,128]{1,0:T(8,128)S(1)}, u32[]{:S(2)}, u32[]{:S(2)}) %collective-permute-start.7) | collective-permute-done | bytes 8224 | tf_op jit(solution)/shard_map/ppermute | solution.py:540
  26.1 0.8 %collective-permute-done.6 = f32[16,128]{1,0:T(8,128)S(1)} collective-permute-done((f32[16,128]{1,0:T(8,128)S(1)}, f32[16,128]{1,0:T(8,128)S(1)}, u32[]{:S(2)}, u32[]{:S(2)}) %collective-permute-start.6) | collective-permute-done | bytes 8224 | tf_op jit(solution)/shard_map/ppermute | solution.py:540
  26.9 0.0 collective-permute-done.5
  27.0 1.7 %collective-permute-start.8 = (bf16[224,128]{1,0:T(8,128)(2,1)S(1)}, bf16[224,128]{1,0:T(8,128)(2,1)S(1)}, u32[]{:S(2)}, u32[]{:S(2)}) collective-permute-start(bf16[224,128]{1,0:T(8,128)(2,1)S(1)} %pad_maximum_fusion.2), channel_id=1, source_target_pairs={{0,8},{2,10},{4,12},{6,14},{8,0},{10,2},{12,4},{14,6},{16,24},{18,... | collective-permute-start | bytes 172040 | tf_op jit(solution)/shard_map/ppermute | solution.py:530
  28.7 2.6 %collective-permute-done.8 = bf16[224,128]{1,0:T(8,128)(2,1)S(1)} collective-permute-done((bf16[224,128]{1,0:T(8,128)(2,1)S(1)}, bf16[224,128]{1,0:T(8,128)(2,1)S(1)}, u32[]{:S(2)}, u32[]{:S(2)}) %collective-permute-start.8) | collective-permute-done | bytes 57376 | tf_op jit(solution)/shard_map/ppermute | solution.py:530
  31.3 1.7 %collective-permute-start.9 = (bf16[128,128]{1,0:T(8,128)(2,1)S(1)}, bf16[128,128]{1,0:T(8,128)(2,1)S(1)}, u32[]{:S(2)}, u32[]{:S(2)}) collective-permute-start(bf16[128,128]{1,0:T(8,128)(2,1)S(1)} %pad_maximum_fusion.4), channel_id=1, source_target_pairs={{0,16},{2,18},{4,20},{6,22},{8,24},{10,26},{12,28},{14,30},{16,0},... | collective-permute-start | bytes 98312 | tf_op jit(solution)/shard_map/ppermute | solution.py:530
  33.0 3.2 %collective-permute-done.9.got_ref = bf16[128,128]{1,0:T(8,128)(2,1)S(1)} collective-permute-done((bf16[128,128]{1,0:T(8,128)(2,1)S(1)}, bf16[128,128]{1,0:T(8,128)(2,1)S(1)}, u32[]{:S(2)}, u32[]{:S(2)}) %collective-permute-start.9) | collective-permute-done | bytes 32800 | tf_op jit(solution)/shard_map/ppermute | solution.py:530
  36.2 0.0 copy-done.3
  36.2 2.2 %finish.1 = f32[12,1024]{1,0:T(8,128)} custom-call(s32[16]{0:T(128)S(1)} %copy-done.2, s32[16]{0:T(128)S(1)} %copy-done.3, s32[16]{0:T(128)S(1)} %copy-done.4, f32[16,128]{1,0:T(8,128)S(1)} %get-tuple-element.21.given_ref, f32[16,128]{1,0:T(8,128)S(1)} %get-tuple-element.38.shift_ref, bf16[96,128]{1,0:T(8,128)(2,1)S(1)} %get-tuple-element.44.mine_ref, ...), custom_call_target="tpu_custom_call" | custom-call | tf_op jit(solution)/shard_map/finish/pallas_call | solution.py:543
  (27 shorter events, 0.2 us)
Async XLA Ops:
  0.9 5.3 %collective-permute-start = (f32[1,16,128]{2,1,0:T(8,128)S(1)}, f32[1,16,128]{2,1,0:T(8,128)S(1)}, u32[]{:S(2)}, u32[]{:S(2)}) collective-permute-start(f32[1,16,128]{2,1,0:T(8,128)S(1)} %bitcast.5), channel_id=1, source_target_pairs={{0,4},{2,6},{4,0},{6,2},{8,12},{10,14},{12,8},{14,10},{16,20},{18,... | collective-permute-start | bytes 24584 | tf_op jit(solution)/shard_map/ppermute | solution.py:415
  6.2 3.8 %collective-permute-start.1 = (f32[2,16,128]{2,1,0:T(8,128)S(1)}, f32[2,16,128]{2,1,0:T(8,128)S(1)}, u32[]{:S(2)}, u32[]{:S(2)}) collective-permute-start(f32[2,16,128]{2,1,0:T(8,128)S(1)} %pad_maximum_fusion.5), channel_id=1, source_target_pairs={{0,8},{2,10},{4,12},{6,14},{8,0},{10,2},{12,4},{14,6},{16,24},{18,... | collective-permute-start | bytes 49160 | tf_op jit(solution)/shard_map/ppermute | solution.py:415
  10.1 5.7 %collective-permute-start.2 = (f32[4,16,128]{2,1,0:T(8,128)S(1)}, f32[4,16,128]{2,1,0:T(8,128)S(1)}, u32[]{:S(2)}, u32[]{:S(2)}) collective-permute-start(f32[4,16,128]{2,1,0:T(8,128)S(1)} %pad_maximum_fusion.3), channel_id=1, source_target_pairs={{0,16},{2,18},{4,20},{6,22},{8,24},{10,26},{12,28},{14,30},{16,0},... | collective-permute-start | bytes 98312 | tf_op jit(solution)/shard_map/ppermute | solution.py:415
  12.7 4.5 %copy-start = (s32[8,8]{1,0:T(8,128)S(1)}, s32[8,8]{1,0:T(8,128)}, u32[]{:S(2)}) copy-start(s32[8,8]{1,0:T(8,128)} %dest_ref.1) | copy-start | bytes 772
  12.7 4.5 %copy-start.1 = (s32[8,8]{1,0:T(8,128)S(1)}, s32[8,8]{1,0:T(8,128)}, u32[]{:S(2)}) copy-start(s32[8,8]{1,0:T(8,128)} %block_ref.1) | copy-start | bytes 772
  15.8 1.3 %collective-permute-start.3 = (f32[8,16,128]{2,1,0:T(8,128)S(1)}, f32[8,16,128]{2,1,0:T(8,128)S(1)}, u32[]{:S(2)}, u32[]{:S(2)}) collective-permute-start(f32[8,16,128]{2,1,0:T(8,128)S(1)} %pad_maximum_fusion.1), channel_id=1, source_target_pairs={{0,2},{2,0},{4,6},{6,4},{8,10},{10,8},{12,14},{14,12},{16,18},{18,... | collective-permute-start | bytes 196616 | tf_op jit(solution)/shard_map/ppermute | solution.py:415
  17.2 19.0 %copy-start.2 = (s32[16]{0:T(128)S(1)}, s32[16]{0:T(128)}, u32[]{:S(2)}) copy-start(s32[16]{0:T(128)} %count_ref.1) | copy-start | bytes 196
  17.2 19.0 %copy-start.3 = (s32[16]{0:T(128)S(1)}, s32[16]{0:T(128)}, u32[]{:S(2)}) copy-start(s32[16]{0:T(128)} %parent_ref.1) | copy-start | bytes 196
  17.2 19.0 %copy-start.4 = (s32[16]{0:T(128)S(1)}, s32[16]{0:T(128)}, u32[]{:S(2)}) copy-start(s32[16]{0:T(128)} %reservoir_ref.1) | copy-start | bytes 196
  18.6 1.5 %collective-permute-start.4 = (bf16[800,128]{1,0:T(8,128)(2,1)S(1)}, bf16[800,128]{1,0:T(8,128)(2,1)S(1)}, u32[]{:S(2)}, u32[]{:S(2)}) collective-permute-start(bf16[800,128]{1,0:T(8,128)(2,1)S(1)} %get-tuple-element.33), channel_id=1, source_target_pairs={{0,2},{2,0},{4,6},{6,4},{8,10},{10,8},{12,14},{14,12},{16,18},{18,... | collective-permute-start | bytes 614408 | tf_op jit(solution)/shard_map/ppermute | solution.py:530
  20.3 6.7 %collective-permute-start.5 = (bf16[416,128]{1,0:T(8,128)(2,1)S(1)}, bf16[416,128]{1,0:T(8,128)(2,1)S(1)}, u32[]{:S(2)}, u32[]{:S(2)}) collective-permute-start(bf16[416,128]{1,0:T(8,128)(2,1)S(1)} %pad_maximum_fusion), channel_id=1, source_target_pairs={{0,4},{2,6},{4,0},{6,2},{8,12},{10,14},{12,8},{14,10},{16,20},{18,... | collective-permute-start | bytes 319496 | tf_op jit(solution)/shard_map/ppermute | solution.py:530
  21.6 4.5 %collective-permute-start.7 = (f32[16,128]{1,0:T(8,128)S(1)}, f32[16,128]{1,0:T(8,128)S(1)}, u32[]{:S(2)}, u32[]{:S(2)}) collective-permute-start(f32[16,128]{1,0:T(8,128)S(1)} %get-tuple-element.42), channel_id=1, source_target_pairs={{0,5},{1,4},{2,7},{3,6},{4,1},{5,0},{6,3},{7,2},{8,13},{9,12},{10,... | collective-permute-start | bytes 24584 | tf_op jit(solution)/shard_map/ppermute | solution.py:540
  23.3 3.7 %collective-permute-start.6 = (f32[16,128]{1,0:T(8,128)S(1)}, f32[16,128]{1,0:T(8,128)S(1)}, u32[]{:S(2)}, u32[]{:S(2)}) collective-permute-start(f32[16,128]{1,0:T(8,128)S(1)} %get-tuple-element.42), channel_id=1, source_target_pairs={{0,1},{1,0},{2,3},{3,2},{4,5},{5,4},{6,7},{7,6},{8,9},{9,8},{10,11... | collective-permute-start | bytes 24584 | tf_op jit(solution)/shard_map/ppermute | solution.py:540
  27.0 4.2 %collective-permute-start.8 = (bf16[224,128]{1,0:T(8,128)(2,1)S(1)}, bf16[224,128]{1,0:T(8,128)(2,1)S(1)}, u32[]{:S(2)}, u32[]{:S(2)}) collective-permute-start(bf16[224,128]{1,0:T(8,128)(2,1)S(1)} %pad_maximum_fusion.2), channel_id=1, source_target_pairs={{0,8},{2,10},{4,12},{6,14},{8,0},{10,2},{12,4},{14,6},{16,24},{18,... | collective-permute-start | bytes 172040 | tf_op jit(solution)/shard_map/ppermute | solution.py:530
  31.3 4.9 %collective-permute-start.9 = (bf16[128,128]{1,0:T(8,128)(2,1)S(1)}, bf16[128,128]{1,0:T(8,128)(2,1)S(1)}, u32[]{:S(2)}, u32[]{:S(2)}) collective-permute-start(bf16[128,128]{1,0:T(8,128)(2,1)S(1)} %pad_maximum_fusion.4), channel_id=1, source_target_pairs={{0,16},{2,18},{4,20},{6,22},{8,24},{10,26},{12,28},{14,30},{16,0},... | collective-permute-start | bytes 98312 | tf_op jit(solution)/shard_map/ppermute | solution.py:530
